TPU v7x, 32 devices: a whole 2x2x4 slice. The times are simulated.
32 devices in a mesh: dp: 8 (over z, x), seq: 4 (over y, core).
Axes of the slice: x: 2, y: 2, z: 4, core: 2. Of those that a mesh axis runs over, the one named last changes fastest.
Arguments:
- inputs: bfloat16 [16, 512, 1536], P('dp', 'seq'), may hold values from -6 to 6
- conditioning: bfloat16 [16, 128, 1536], P('dp', 'seq'), may hold values from -6 to 6
- seq_lengths: int32 [16], P('dp'), may hold values from 128 to 512, as said below
- cond_lengths: int32 [16], P('dp'), may hold values from 32 to 128, as said below
- gain_self: bfloat16 [1536], P(('dp', 'seq')), may hold values from 0.5 to 1.5
- gain_cross: bfloat16 [1536], P(('dp', 'seq')), may hold values from 0.5 to 1.5
- gain_mlp: bfloat16 [1536], P(('dp', 'seq')), may hold values from 0.5 to 1.5
- w_query: bfloat16 [1536, 1536], P(('dp', 'seq')), may hold values from -0.15625 to 0.15625
- w_key: bfloat16 [1536, 1536], P(('dp', 'seq')), may hold values from -0.15625 to 0.15625
- w_value: bfloat16 [1536, 1536], P(('dp', 'seq')), may hold values from -0.15625 to 0.15625
- w_output: bfloat16 [1536, 1536], P(('dp', 'seq')), may hold values from -2 to 2
- c_query: bfloat16 [1536, 1536], P(('dp', 'seq')), may hold values from -0.15625 to 0.15625
- c_key: bfloat16 [1536, 1536], P(('dp', 'seq')), may hold values from -0.15625 to 0.15625
- c_value: bfloat16 [1536, 1536], P(('dp', 'seq')), may hold values from -0.15625 to 0.15625
- c_output: bfloat16 [1536, 1536], P(('dp', 'seq')), may hold values from -1 to 1
- w_gate: bfloat16 [1536, 6144], P(('dp', 'seq')), may hold values from -0.15625 to 0.15625
- w_up: bfloat16 [1536, 6144], P(('dp', 'seq')), may hold values from -0.15625 to 0.15625
- w_down: bfloat16 [1536, 6144], P(('dp', 'seq')), may hold values from -0.078125 to 0.078125
- cotangent: bfloat16 [16, 512, 1536], P('dp', 'seq'), may hold values from -6 to 6
Outputs:
- block_out: bfloat16 [16, 512, 1536], P('dp', 'seq')
- grad_inputs: float32 [16, 512, 1536], P('dp', 'seq')
- grad_conditioning: float32 [16, 128, 1536], P('dp', 'seq')
- grad_gain_self: float32 [1536], P(('dp', 'seq'))
- grad_gain_cross: float32 [1536], P(('dp', 'seq'))
- grad_gain_mlp: float32 [1536], P(('dp', 'seq'))
- grad_w_query: float32 [1536, 1536], P(('dp', 'seq'))
- grad_w_key: float32 [1536, 1536], P(('dp', 'seq'))
- grad_w_value: float32 [1536, 1536], P(('dp', 'seq'))
- grad_w_output: float32 [1536, 1536], P(('dp', 'seq'))
- grad_c_query: float32 [1536, 1536], P(('dp', 'seq'))
- grad_c_key: float32 [1536, 1536], P(('dp', 'seq'))
- grad_c_value: float32 [1536, 1536], P(('dp', 'seq'))
- grad_c_output: float32 [1536, 1536], P(('dp', 'seq'))
- grad_w_gate: float32 [1536, 6144], P(('dp', 'seq'))
- grad_w_up: float32 [1536, 6144], P(('dp', 'seq'))
- grad_w_down: float32 [1536, 6144], P(('dp', 'seq'))
Inputs may be any that keep to these rules, and one draw needn't show every extreme that they name: The valid tokens of a sequence are its first seq_lengths slots; some sequence has all 512. The valid conditioning tokens are the first cond_lengths slots; some sequence has all 128.
All inputs are finite; a program needn't handle non-finite values.
Results may differ from a plain program's by a relative error of at most 0.025.
Values may be sent and summed in bfloat16 or wider, within the bound.
A program may use at most 320 MiB of HBM per device.

v0:
```python
import math

import jax
import jax.numpy as jnp
from jax import lax
from jax.sharding import PartitionSpec as P

D = 1536
HEADS = 24
HEAD = 64
ROT = 32


EPSILON = 1e-05
PAIRINGS = ((0, 0), (0, 1), (0, 2), (1, 3), (2, 4), (3, 5), (3, 6), (4, 7), (5, 8), (5, 9), (6, 10))


def as_sent(x):
    return jax.tree.map(lambda a: a.astype(jnp.bfloat16) if a.dtype == jnp.float32 else a, x)


def contract_rows(left, right):
    return lax.dot_general(
        left, right, (((0,), (0,)), ((), ())), preferred_element_type=jnp.float32
    )


def times_transpose(left, right):
    return lax.dot_general(
        left, right, (((1,), (1,)), ((), ())), preferred_element_type=jnp.float32
    )


def product(left, right):
    return jnp.dot(left, right, preferred_element_type=jnp.float32)


def norm_forward(values, gain_vec):
    average = jnp.mean(values, axis=-1, keepdims=True)
    centred = values - average
    variance = jnp.mean(centred * centred, axis=-1, keepdims=True)
    inv_std = lax.rsqrt(variance + EPSILON)
    normal = centred * inv_std
    return (normal, inv_std, (normal * gain_vec).astype(jnp.bfloat16))


def norm_backward(grad_normed, normal, inv_std, gain_vec):
    grad_gain = jnp.sum(grad_normed * normal, axis=0)
    grad_hat = grad_normed * gain_vec
    mean_hat = jnp.mean(grad_hat, axis=-1, keepdims=True)
    mean_mix = jnp.mean(grad_hat * normal, axis=-1, keepdims=True)
    return (inv_std * (grad_hat - mean_hat - normal * mean_mix), grad_gain)


def rotate(matrix_rows, cosine, sine_table):
    shaped = matrix_rows.reshape(matrix_rows.shape[0], HEADS, HEAD)
    half_rot = ROT // 2
    lower_half = shaped[..., :half_rot]
    upper_half = shaped[..., half_rot:ROT]
    return jnp.concatenate(
        [
            lower_half * cosine - upper_half * sine_table,
            upper_half * cosine + lower_half * sine_table,
            shaped[..., ROT:],
        ],
        axis=-1,
    )


def masked_scores(queries, key_rows, key_ok, score_scale):
    scores = (
        jnp.einsum("thd,shd->hts", queries, key_rows, preferred_element_type=jnp.float32)
        * score_scale
    )
    return jnp.where(key_ok[None, None, :], scores, -1e30)


def attend(queries, key_rows, values, key_ok, score_scale):
    scores = masked_scores(queries, key_rows, key_ok, score_scale)
    row_max = jnp.max(scores, axis=-1, keepdims=True)
    row_sum = jnp.sum(jnp.exp(scores - row_max), axis=-1, keepdims=True)
    log_total = row_max + jnp.log(row_sum)
    attn_weights = jnp.exp(scores - log_total).astype(jnp.bfloat16)
    mixed = jnp.einsum("hts,shd->thd", attn_weights, values, preferred_element_type=jnp.float32)
    return (mixed.reshape(mixed.shape[0], D).astype(jnp.bfloat16), log_total)


def attend_back(queries, key_rows, values, key_ok, log_total, grad_mixed, score_scale):
    scores = masked_scores(queries, key_rows, key_ok, score_scale)
    attn_weights = jnp.exp(scores - log_total)
    grad_weights = jnp.einsum(
        "thd,shd->hts", grad_mixed, values, preferred_element_type=jnp.float32
    )
    inner_sum = jnp.sum(attn_weights * grad_weights, axis=-1, keepdims=True)
    grad_scores = (attn_weights * (grad_weights - inner_sum)).astype(jnp.bfloat16)
    grad_queries = (
        jnp.einsum("hts,shd->thd", grad_scores, key_rows, preferred_element_type=jnp.float32)
        * score_scale
    )
    grad_keys = (
        jnp.einsum("hts,thd->shd", grad_scores, queries, preferred_element_type=jnp.float32)
        * score_scale
    )
    grad_values = jnp.einsum(
        "hts,thd->shd",
        attn_weights.astype(jnp.bfloat16),
        grad_mixed,
        preferred_element_type=jnp.float32,
    )
    return (grad_queries, grad_keys, grad_values)


def add_tuples(first, second):
    if first is None:
        return second
    return tuple((left + right for left, right in zip(first, second)))


def per_device(
    inputs,
    conditioning,
    seq_lengths,
    cond_lengths,
    gain_self,
    gain_cross,
    gain_mlp,
    w_query,
    w_key,
    w_value,
    w_output,
    c_query,
    c_key,
    c_value,
    c_output,
    w_gate,
    w_up,
    w_down,
    cotangent,
):
    shards = (
        gain_self,
        gain_cross,
        gain_mlp,
        w_query,
        w_key,
        w_value,
        w_output,
        c_query,
        c_key,
        c_value,
        c_output,
        w_gate,
        w_up,
        w_down,
    )
    tokens_dev = inputs.shape[1]
    cond_dev = conditioning.shape[1]
    group_size = lax.axis_size("seq")
    seq_index = lax.axis_index("seq")
    seq_total = tokens_dev * group_size
    cond_total = cond_dev * group_size
    score_scale = 1.0 / math.sqrt(HEAD)
    half_rot = ROT // 2
    positions = (seq_index * tokens_dev + jnp.arange(tokens_dev)).astype(jnp.float32)
    inverse = 10000.0 ** (-jnp.arange(half_rot).astype(jnp.float32) / half_rot)
    angles = positions[:, None] * inverse[None, :]
    cosine = jnp.cos(angles)[:, None, :]
    sine_table = jnp.sin(angles)[:, None, :]
    key_index = jnp.arange(seq_total)
    cond_index = jnp.arange(cond_total)
    block_rows = []
    grad_rows = []
    cond_grads = []
    grad_mats = None
    grad_gains = None
    for batch in range(inputs.shape[0]):
        whole = (
            lax.all_gather(shards[0], ("dp", "seq"), axis=0, tiled=True),
            lax.all_gather(shards[1], ("dp", "seq"), axis=0, tiled=True),
            lax.all_gather(shards[2], ("dp", "seq"), axis=0, tiled=True),
            lax.all_gather(shards[3], ("dp", "seq"), axis=0, tiled=True),
            lax.all_gather(shards[4], ("dp", "seq"), axis=0, tiled=True),
            lax.all_gather(shards[5], ("dp", "seq"), axis=0, tiled=True),
            lax.all_gather(shards[6], ("dp", "seq"), axis=0, tiled=True),
            lax.all_gather(shards[7], ("dp", "seq"), axis=0, tiled=True),
            lax.all_gather(shards[8], ("dp", "seq"), axis=0, tiled=True),
            lax.all_gather(shards[9], ("dp", "seq"), axis=0, tiled=True),
            lax.all_gather(shards[10], ("dp", "seq"), axis=0, tiled=True),
            lax.all_gather(shards[11], ("dp", "seq"), axis=0, tiled=True),
            lax.all_gather(shards[12], ("dp", "seq"), axis=0, tiled=True),
            lax.all_gather(shards[13], ("dp", "seq"), axis=0, tiled=True),
        )
        gain_one = whole[0].astype(jnp.float32)
        gain_two = whole[1].astype(jnp.float32)
        gain_three = whole[2].astype(jnp.float32)
        (
            full_query,
            full_key,
            full_value,
            full_output,
            cross_query,
            cross_key,
            cross_value,
            cross_output,
            full_gate,
            full_up,
            full_down,
        ) = whole[3:]
        tokens = inputs[batch]
        cond_rows = conditioning[batch]
        key_ok = key_index < seq_lengths[batch]
        cond_ok = cond_index < cond_lengths[batch]
        normal_one, inv_one, normed_one = norm_forward(tokens.astype(jnp.float32), gain_one)
        query_rot = rotate(product(normed_one, full_query), cosine, sine_table).astype(jnp.bfloat16)
        key_rot = rotate(product(normed_one, full_key), cosine, sine_table).astype(jnp.bfloat16)
        value_loc = (
            product(normed_one, full_value).astype(jnp.bfloat16).reshape(tokens_dev, HEADS, HEAD)
        )
        key_all, value_all = (
            lax.all_gather(key_rot, "seq", axis=0, tiled=True),
            lax.all_gather(value_loc, "seq", axis=0, tiled=True),
        )
        attended, log_one = attend(query_rot, key_all, value_all, key_ok, score_scale)
        after_self = tokens.astype(jnp.float32) + product(attended, full_output)
        normal_two, inv_two, normed_two = norm_forward(after_self, gain_two)
        cq_loc = (
            product(normed_two, cross_query).astype(jnp.bfloat16).reshape(tokens_dev, HEADS, HEAD)
        )
        ck_loc = product(cond_rows, cross_key).astype(jnp.bfloat16).reshape(cond_dev, HEADS, HEAD)
        cv_loc = product(cond_rows, cross_value).astype(jnp.bfloat16).reshape(cond_dev, HEADS, HEAD)
        ck_all, cv_all = (
            lax.all_gather(ck_loc, "seq", axis=0, tiled=True),
            lax.all_gather(cv_loc, "seq", axis=0, tiled=True),
        )
        cross_att, log_two = attend(cq_loc, ck_all, cv_all, cond_ok, score_scale)
        after_cross = after_self + product(cross_att, cross_output)
        normal_three, inv_three, normed_three = norm_forward(after_cross, gain_three)
        gate = product(normed_three, full_gate)
        up_vals = product(normed_three, full_up)
        hidden = (jax.nn.silu(gate) * up_vals).astype(jnp.bfloat16)
        block_rows.append((after_cross + times_transpose(hidden, full_down)).astype(jnp.bfloat16))
        incoming = cotangent[batch]
        grad_hidden = product(incoming, full_down)
        sigmoid_gate = jax.nn.sigmoid(gate)
        grad_gate = (
            grad_hidden * up_vals * sigmoid_gate * (1.0 + gate * (1.0 - sigmoid_gate))
        ).astype(jnp.bfloat16)
        grad_upv = (grad_hidden * gate * sigmoid_gate).astype(jnp.bfloat16)
        grad_norm3 = times_transpose(grad_gate, full_gate) + times_transpose(grad_upv, full_up)
        back_three, gain_grad_three = norm_backward(grad_norm3, normal_three, inv_three, gain_three)
        grad_after_cross = incoming.astype(jnp.float32) + back_three
        cross_low = grad_after_cross.astype(jnp.bfloat16)
        grad_catt = (
            times_transpose(cross_low, cross_output)
            .astype(jnp.bfloat16)
            .reshape(tokens_dev, HEADS, HEAD)
        )
        gq_cross, gk_cross, gv_cross = attend_back(
            cq_loc, ck_all, cv_all, cond_ok, log_two, grad_catt, score_scale
        )
        gk_cond, gv_cond = (
            lax.psum_scatter(
                gk_cross.reshape(cond_total, D).astype(jnp.bfloat16),
                "seq",
                scatter_dimension=0,
                tiled=True,
            ).astype(jnp.float32),
            lax.psum_scatter(
                gv_cross.reshape(cond_total, D).astype(jnp.bfloat16),
                "seq",
                scatter_dimension=0,
                tiled=True,
            ).astype(jnp.float32),
        )
        ck_grad_low = gk_cond.astype(jnp.bfloat16)
        cv_grad_low = gv_cond.astype(jnp.bfloat16)
        cond_grads.append(
            times_transpose(ck_grad_low, cross_key) + times_transpose(cv_grad_low, cross_value)
        )
        cq_grad_low = gq_cross.reshape(tokens_dev, D).astype(jnp.bfloat16)
        grad_norm2 = times_transpose(cq_grad_low, cross_query)
        back_two, gain_grad_two = norm_backward(grad_norm2, normal_two, inv_two, gain_two)
        grad_after_self = grad_after_cross + back_two
        self_low = grad_after_self.astype(jnp.bfloat16)
        grad_att = (
            times_transpose(self_low, full_output)
            .astype(jnp.bfloat16)
            .reshape(tokens_dev, HEADS, HEAD)
        )
        gq_self, gk_self, gv_self = attend_back(
            query_rot, key_all, value_all, key_ok, log_one, grad_att, score_scale
        )
        gk_own, gv_own = (
            lax.psum_scatter(
                gk_self.reshape(seq_total, D).astype(jnp.bfloat16),
                "seq",
                scatter_dimension=0,
                tiled=True,
            ).astype(jnp.float32),
            lax.psum_scatter(
                gv_self.reshape(seq_total, D).astype(jnp.bfloat16),
                "seq",
                scatter_dimension=0,
                tiled=True,
            ).astype(jnp.float32),
        )
        q_grad_low = (
            rotate(gq_self.reshape(tokens_dev, D), cosine, -sine_table)
            .reshape(tokens_dev, D)
            .astype(jnp.bfloat16)
        )
        k_grad_low = rotate(gk_own, cosine, -sine_table).reshape(tokens_dev, D).astype(jnp.bfloat16)
        v_grad_low = gv_own.astype(jnp.bfloat16)
        grad_norm1 = (
            times_transpose(q_grad_low, full_query)
            + times_transpose(k_grad_low, full_key)
            + times_transpose(v_grad_low, full_value)
        )
        back_one, gain_grad_one = norm_backward(grad_norm1, normal_one, inv_one, gain_one)
        grad_rows.append(grad_after_self + back_one)
        group_left = (
            lax.all_gather(normed_one, "seq", axis=0, tiled=True),
            lax.all_gather(attended, "seq", axis=0, tiled=True),
            lax.all_gather(normed_two, "seq", axis=0, tiled=True),
            lax.all_gather(cond_rows, "seq", axis=0, tiled=True),
            lax.all_gather(cross_att, "seq", axis=0, tiled=True),
            lax.all_gather(normed_three, "seq", axis=0, tiled=True),
            lax.all_gather(incoming, "seq", axis=0, tiled=True),
        )
        group_right = (
            lax.all_to_all(q_grad_low, "seq", split_axis=1, concat_axis=0, tiled=True),
            lax.all_to_all(k_grad_low, "seq", split_axis=1, concat_axis=0, tiled=True),
            lax.all_to_all(v_grad_low, "seq", split_axis=1, concat_axis=0, tiled=True),
            lax.all_to_all(self_low, "seq", split_axis=1, concat_axis=0, tiled=True),
            lax.all_to_all(cq_grad_low, "seq", split_axis=1, concat_axis=0, tiled=True),
            lax.all_to_all(ck_grad_low, "seq", split_axis=1, concat_axis=0, tiled=True),
            lax.all_to_all(cv_grad_low, "seq", split_axis=1, concat_axis=0, tiled=True),
            lax.all_to_all(cross_low, "seq", split_axis=1, concat_axis=0, tiled=True),
            lax.all_to_all(grad_gate, "seq", split_axis=1, concat_axis=0, tiled=True),
            lax.all_to_all(grad_upv, "seq", split_axis=1, concat_axis=0, tiled=True),
            lax.all_to_all(hidden, "seq", split_axis=1, concat_axis=0, tiled=True),
        )
        partial_value = tuple(
            (contract_rows(group_left[left], group_right[right]) for left, right in PAIRINGS)
        )
        summed_now = jax.tree.map(
            lambda part: part.astype(jnp.float32),
            lax.psum_scatter(as_sent(partial_value), "dp", scatter_dimension=0, tiled=True),
        )
        grad_mats = add_tuples(grad_mats, summed_now)
        gains_now = lax.psum_scatter(
            jnp.stack([gain_grad_one, gain_grad_two, gain_grad_three]),
            ("dp", "seq"),
            scatter_dimension=1,
            tiled=True,
        )
        if grad_gains is None:
            grad_gains = gains_now
        else:
            grad_gains = grad_gains + gains_now
    owned = jax.tree.map(
        lambda part, own: part.astype(own.dtype),
        lax.all_to_all(as_sent(grad_mats), "seq", split_axis=0, concat_axis=1, tiled=True),
        grad_mats,
    )
    return (
        jnp.stack(block_rows),
        jnp.stack(grad_rows),
        jnp.stack(cond_grads),
        grad_gains[0],
        grad_gains[1],
        grad_gains[2],
        owned[0],
        owned[1],
        owned[2],
        owned[3],
        owned[4],
        owned[5],
        owned[6],
        owned[7],
        owned[8],
        owned[9],
        owned[10],
    )


def solution(mesh):
    placed = (
        P("dp", "seq", None),
        P("dp", "seq", None),
        P("dp"),
        P("dp"),
        P(("dp", "seq")),
        P(("dp", "seq")),
        P(("dp", "seq")),
        P(("dp", "seq"), None),
        P(("dp", "seq"), None),
        P(("dp", "seq"), None),
        P(("dp", "seq"), None),
        P(("dp", "seq"), None),
        P(("dp", "seq"), None),
        P(("dp", "seq"), None),
        P(("dp", "seq"), None),
        P(("dp", "seq"), None),
        P(("dp", "seq"), None),
        P(("dp", "seq"), None),
        P("dp", "seq", None),
    )
    return jax.shard_map(
        per_device,
        mesh=mesh,
        in_specs=placed,
        out_specs=(
            P("dp", "seq", None),
            P("dp", "seq", None),
            P("dp", "seq", None),
            P(("dp", "seq")),
            P(("dp", "seq")),
            P(("dp", "seq")),
            P(("dp", "seq"), None),
            P(("dp", "seq"), None),
            P(("dp", "seq"), None),
            P(("dp", "seq"), None),
            P(("dp", "seq"), None),
            P(("dp", "seq"), None),
            P(("dp", "seq"), None),
            P(("dp", "seq"), None),
            P(("dp", "seq"), None),
            P(("dp", "seq"), None),
            P(("dp", "seq"), None),
        ),
        check_vma=False,
    )
```

profile of v0, /device:TPU:0, one launch (start us, length us, event | category | flops | bytes accessed | tf_op | source)
XLA Modules:
  0.0 3291.6 jit_solution(3212743950297339765)
XLA Ops:
  12.0 42.3 %all-reduce.3 = (bf16[1536]{0:T(1024)(128)(2,1)S(1)}, bf16[1536]{0:T(1024)(128)(2,1)S(1)}, bf16[1536]{0:T(1024)(128)(2,1)S(1)}) all-reduce(bf16[1536]{0:T(1024)(128)(2,1)S(1)} %dynamic-update-slice, bf16[1536]{0:T(1024)(128)(2,1)S(1)} %dynamic-update-slice.1, ...), channel_id=1, replica_groups=mesh['dp'=8,'seq'=4] {'dp','seq'}, use_global_device_ids=true, to_apply=%add | all-reduce | flops 4608 | bytes 18432
  57.9 19.4 all-gather.38.cloned.1.call-done
  88.8 53.3 %all-gather.36.cloned.1.call-done = bf16[1536,1536]{1,0:T(8,128)(2,1)} async-done(((bf16[48,1536]{1,0:T(8,128)(2,1)}), bf16[1536,1536]{1,0:T(8,128)(2,1)}) %all-gather.36.cloned.1.call-update) | async-done | bytes 4718608 | tf_op jit(solution)/shard_map/all_gather | solution.py:181
  158.0 48.9 %all-gather.32.cloned.1.call-done = bf16[1536,1536]{1,0:T(8,128)(2,1)} async-done(((bf16[48,1536]{1,0:T(8,128)(2,1)}), bf16[1536,1536]{1,0:T(8,128)(2,1)}) %all-gather.32.cloned.1.call-update) | async-done | bytes 4718608 | tf_op jit(solution)/shard_map/all_gather | solution.py:183
  232.4 16.6 all-gather.58.cloned.1.call-done
  255.4 15.3 all-gather.40.cloned.1.call-done
  276.0 16.8 all-gather.34.cloned.1.call-done
  298.5 60.7 %all-gather.42.cloned.1.call-done = bf16[1536,1536]{1,0:T(8,128)(2,1)} async-done(((bf16[48,1536]{1,0:T(8,128)(2,1)}), bf16[1536,1536]{1,0:T(8,128)(2,1)}) %all-gather.42.cloned.1.call-update) | async-done | bytes 4718608 | tf_op jit(solution)/shard_map/all_gather | solution.py:184
  368.2 55.9 %all-gather.44.cloned.1.call-done = bf16[1536,1536]{1,0:T(8,128)(2,1)} async-done(((bf16[48,1536]{1,0:T(8,128)(2,1)}), bf16[1536,1536]{1,0:T(8,128)(2,1)}) %all-gather.44.cloned.1.call-update) | async-done | bytes 4718608 | tf_op jit(solution)/shard_map/all_gather | solution.py:187
  427.5 61.2 %all-gather.48.cloned.1.call-done = bf16[1536,1536]{1,0:T(8,128)(2,1)} async-done(((bf16[48,1536]{1,0:T(8,128)(2,1)}), bf16[1536,1536]{1,0:T(8,128)(2,1)}) %all-gather.48.cloned.1.call-update) | async-done | bytes 4718608 | tf_op jit(solution)/shard_map/all_gather | solution.py:186
  537.0 16.6 all-gather.46.cloned.1.call-done
  565.5 52.7 %all-gather.50.cloned.1.call-done = bf16[1536,1536]{1,0:T(8,128)(2,1)} async-done(((bf16[48,1536]{1,0:T(8,128)(2,1)}), bf16[1536,1536]{1,0:T(8,128)(2,1)}) %all-gather.50.cloned.1.call-update) | async-done | bytes 4718608 | tf_op jit(solution)/shard_map/all_gather | solution.py:188
  625.1 118.4 %all-gather.52.cloned.1.call-done = bf16[1536,6144]{1,0:T(8,128)(2,1)} async-done(((bf16[48,6144]{1,0:T(8,128)(2,1)}), bf16[1536,6144]{1,0:T(8,128)(2,1)}) %all-gather.52.cloned.1.call-update) | async-done | bytes 18874384 | tf_op jit(solution)/shard_map/all_gather | solution.py:189
  754.0 114.4 %all-gather.54.cloned.1.call-done = bf16[1536,6144]{1,0:T(8,128)(2,1)} async-done(((bf16[48,6144]{1,0:T(8,128)(2,1)}), bf16[1536,6144]{1,0:T(8,128)(2,1)}) %all-gather.54.cloned.1.call-update) | async-done | bytes 18874384 | tf_op jit(solution)/shard_map/all_gather | solution.py:190
  879.1 114.4 %all-gather.56.cloned.1.call-done = bf16[1536,6144]{1,0:T(8,128)(2,1)} async-done(((bf16[48,6144]{1,0:T(8,128)(2,1)}), bf16[1536,6144]{1,0:T(8,128)(2,1)}) %all-gather.56.cloned.1.call-update) | async-done | bytes 18874384 | tf_op jit(solution)/shard_map/all_gather | solution.py:191
  993.4 15.3 multiply_convert_fusion.6
  1008.7 14.4 fusion.132
  1023.1 15.1 multiply_reduce_fusion.6
  1055.1 13.5 multiply_convert_fusion.3
  1068.6 14.2 fusion.134
  1082.8 14.9 multiply_reduce_fusion.4
  1463.4 13.9 all_to_all.547
  1498.6 19.9 all-to-all-done.31
  1537.2 19.9 all-to-all-done.30
  1575.8 19.9 all-to-all-done.24
  1603.0 22.5 all_to_all.549
  1632.8 22.6 all_to_all.550
  1695.4 13.5 fusion.13
  1728.0 41.2 %reduce-scatter.78.cloned.1.call-done = bf16[192,384]{1,0:T(8,128)(2,1)} async-done(((bf16[1536,384]{1,0:T(8,128)(2,1)}), bf16[192,384]{1,0:T(8,128)(2,1)}) %reduce-scatter.78.cloned.1.call-update) | async-done | bytes 147472 | tf_op jit(solution)/shard_map/reduce_scatter | solution.py:348
  1770.9 65.4 %reduce-scatter.84.cloned.1.call-done = bf16[192,384]{1,0:T(8,128)(2,1)} async-done(((bf16[1536,384]{1,0:T(8,128)(2,1)}), bf16[192,384]{1,0:T(8,128)(2,1)}) %reduce-scatter.84.cloned.1.call-update) | async-done | bytes 147472 | tf_op jit(solution)/shard_map/reduce_scatter | solution.py:348
  1836.4 67.1 %reduce-scatter.82.cloned.1.call-done = bf16[192,384]{1,0:T(8,128)(2,1)} async-done(((bf16[1536,384]{1,0:T(8,128)(2,1)}), bf16[192,384]{1,0:T(8,128)(2,1)}) %reduce-scatter.82.cloned.1.call-update) | async-done | bytes 147472 | tf_op jit(solution)/shard_map/reduce_scatter | solution.py:348
  1928.2 75.7 %reduce-scatter.114.cloned.1.call-done = f32[48,3]{1,0:T(8,128)} async-done(((f32[1536,3]{1,0:T(8,128)}), f32[48,3]{1,0:T(8,128)}) %reduce-scatter.114.cloned.1.call-update) | async-done | bytes 592
  2006.6 64.6 %reduce-scatter.104.cloned.1.call-done = bf16[192,384]{1,0:T(8,128)(2,1)} async-done(((bf16[1536,384]{1,0:T(8,128)(2,1)}), bf16[192,384]{1,0:T(8,128)(2,1)}) %reduce-scatter.104.cloned.1.call-update) | async-done | bytes 147472 | tf_op jit(solution)/shard_map/reduce_scatter | solution.py:348
  2071.2 67.0 %reduce-scatter.102.cloned.1.call-done = bf16[192,384]{1,0:T(8,128)(2,1)} async-done(((bf16[1536,384]{1,0:T(8,128)(2,1)}), bf16[192,384]{1,0:T(8,128)(2,1)}) %reduce-scatter.102.cloned.1.call-update) | async-done | bytes 147472 | tf_op jit(solution)/shard_map/reduce_scatter | solution.py:348
  2143.2 61.9 %reduce-scatter.108.cloned.1.call-done = bf16[192,384]{1,0:T(8,128)(2,1)} async-done(((bf16[1536,384]{1,0:T(8,128)(2,1)}), bf16[192,384]{1,0:T(8,128)(2,1)}) %reduce-scatter.108.cloned.1.call-update) | async-done | bytes 147472 | tf_op jit(solution)/shard_map/reduce_scatter | solution.py:348
  2205.1 66.8 %reduce-scatter.106.cloned.1.call-done = bf16[192,384]{1,0:T(8,128)(2,1)} async-done(((bf16[1536,384]{1,0:T(8,128)(2,1)}), bf16[192,384]{1,0:T(8,128)(2,1)}) %reduce-scatter.106.cloned.1.call-update) | async-done | bytes 147472 | tf_op jit(solution)/shard_map/reduce_scatter | solution.py:348
  2282.5 57.0 %reduce-scatter.64.cloned.1.call-done = bf16[192,384]{1,0:T(8,128)(2,1)} async-done(((bf16[1536,384]{1,0:T(8,128)(2,1)}), bf16[192,384]{1,0:T(8,128)(2,1)}) %reduce-scatter.64.cloned.1.call-update) | async-done | bytes 147472 | tf_op jit(solution)/shard_map/reduce_scatter | solution.py:348
  2339.4 67.5 %reduce-scatter.62.cloned.1.call-done = bf16[192,384]{1,0:T(8,128)(2,1)} async-done(((bf16[1536,384]{1,0:T(8,128)(2,1)}), bf16[192,384]{1,0:T(8,128)(2,1)}) %reduce-scatter.62.cloned.1.call-update) | async-done | bytes 147472 | tf_op jit(solution)/shard_map/reduce_scatter | solution.py:348
  2412.0 62.5 %reduce-scatter.68.cloned.1.call-done = bf16[192,384]{1,0:T(8,128)(2,1)} async-done(((bf16[1536,384]{1,0:T(8,128)(2,1)}), bf16[192,384]{1,0:T(8,128)(2,1)}) %reduce-scatter.68.cloned.1.call-update) | async-done | bytes 147472 | tf_op jit(solution)/shard_map/reduce_scatter | solution.py:348
  2474.5 67.0 %reduce-scatter.66.cloned.1.call-done = bf16[192,384]{1,0:T(8,128)(2,1)} async-done(((bf16[1536,384]{1,0:T(8,128)(2,1)}), bf16[192,384]{1,0:T(8,128)(2,1)}) %reduce-scatter.66.cloned.1.call-update) | async-done | bytes 147472 | tf_op jit(solution)/shard_map/reduce_scatter | solution.py:348
  2543.1 65.2 %reduce-scatter.72.cloned.1.call-done = bf16[192,384]{1,0:T(8,128)(2,1)} async-done(((bf16[1536,384]{1,0:T(8,128)(2,1)}), bf16[192,384]{1,0:T(8,128)(2,1)}) %reduce-scatter.72.cloned.1.call-update) | async-done | bytes 147472 | tf_op jit(solution)/shard_map/reduce_scatter | solution.py:348
  2608.3 67.1 %reduce-scatter.70.cloned.1.call-done = bf16[192,384]{1,0:T(8,128)(2,1)} async-done(((bf16[1536,384]{1,0:T(8,128)(2,1)}), bf16[192,384]{1,0:T(8,128)(2,1)}) %reduce-scatter.70.cloned.1.call-update) | async-done | bytes 147472 | tf_op jit(solution)/shard_map/reduce_scatter | solution.py:348
  2688.5 85.1 %reduce-scatter.112.cloned.1.call-done = bf16[192,1536]{1,0:T(8,128)(2,1)} async-done(((bf16[1536,1536]{1,0:T(8,128)(2,1)}), bf16[192,1536]{1,0:T(8,128)(2,1)}) %reduce-scatter.112.cloned.1.call-update) | async-done | bytes 589840 | tf_op jit(solution)/shard_map/reduce_scatter | solution.py:348
  2773.6 99.0 %reduce-scatter.110.cloned.1.call-done = bf16[192,1536]{1,0:T(8,128)(2,1)} async-done(((bf16[1536,1536]{1,0:T(8,128)(2,1)}), bf16[192,1536]{1,0:T(8,128)(2,1)}) %reduce-scatter.110.cloned.1.call-update) | async-done | bytes 589840 | tf_op jit(solution)/shard_map/reduce_scatter | solution.py:348
  2889.0 82.6 %reduce-scatter.86.cloned.1.call-done = bf16[192,1536]{1,0:T(8,128)(2,1)} async-done(((bf16[1536,1536]{1,0:T(8,128)(2,1)}), bf16[192,1536]{1,0:T(8,128)(2,1)}) %reduce-scatter.86.cloned.1.call-update) | async-done | bytes 589840 | tf_op jit(solution)/shard_map/reduce_scatter | solution.py:348
  2971.6 99.0 %reduce-scatter.88.cloned.1.call-done = bf16[192,1536]{1,0:T(8,128)(2,1)} async-done(((bf16[1536,1536]{1,0:T(8,128)(2,1)}), bf16[192,1536]{1,0:T(8,128)(2,1)}) %reduce-scatter.88.cloned.1.call-update) | async-done | bytes 589840 | tf_op jit(solution)/shard_map/reduce_scatter | solution.py:348
  3076.3 93.3 %reduce-scatter.90.cloned.1.call-done = bf16[192,1536]{1,0:T(8,128)(2,1)} async-done(((bf16[1536,1536]{1,0:T(8,128)(2,1)}), bf16[192,1536]{1,0:T(8,128)(2,1)}) %reduce-scatter.90.cloned.1.call-update) | async-done | bytes 589840 | tf_op jit(solution)/shard_map/reduce_scatter | solution.py:348
  3169.6 98.8 %reduce-scatter.92.cloned.1.call-done = bf16[192,1536]{1,0:T(8,128)(2,1)} async-done(((bf16[1536,1536]{1,0:T(8,128)(2,1)}), bf16[192,1536]{1,0:T(8,128)(2,1)}) %reduce-scatter.92.cloned.1.call-update) | async-done | bytes 589840 | tf_op jit(solution)/shard_map/reduce_scatter | solution.py:348
  (813 shorter events, 793.3 us)
Async XLA Ops:
  8.7 198.3 %all-gather.32.cloned.1.call-start = ((), (), s32[]{:S(2)}) async-start(), calls=%async_computation.64 | async-start | bytes 4866048 | tf_op jit(solution)/shard_map/all_gather | solution.py:183
  9.4 217.7 %all-gather.60.cloned.1.call-start = ((), (), s32[]{:S(2)}) async-start(), calls=%async_computation.78 | async-start | bytes 1966080 | tf_op jit(solution)/shard_map/all_gather | solution.py:220
  219.0 205.0 %all-gather.44.cloned.1.call-start = ((), (), s32[]{:S(2)}) async-start(), calls=%async_computation.70 | async-start | bytes 4866048 | tf_op jit(solution)/shard_map/all_gather | solution.py:187
  219.8 268.9 %all-gather.48.cloned.1.call-start = ((), (), s32[]{:S(2)}) async-start(), calls=%async_computation.72 | async-start | bytes 4866048 | tf_op jit(solution)/shard_map/all_gather | solution.py:186
  220.3 333.2 %all-gather.46.cloned.1.call-start = ((), (), s32[]{:S(2)}) async-start(), calls=%async_computation.71 | async-start | bytes 4866048 | tf_op jit(solution)/shard_map/all_gather | solution.py:185
  221.1 397.1 %all-gather.50.cloned.1.call-start = ((), (), s32[]{:S(2)}) async-start(), calls=%async_computation.73 | async-start | bytes 4866048 | tf_op jit(solution)/shard_map/all_gather | solution.py:188
  221.7 521.8 %all-gather.52.cloned.1.call-start = ((), (), s32[]{:S(2)}) async-start(), calls=%async_computation.74 | async-start | bytes 19464192 | tf_op jit(solution)/shard_map/all_gather | solution.py:189
  222.4 646.0 %all-gather.54.cloned.1.call-start = ((), (), s32[]{:S(2)}) async-start(), calls=%async_computation.75 | async-start | bytes 19464192 | tf_op jit(solution)/shard_map/all_gather | solution.py:190
  223.0 770.5 %all-gather.56.cloned.1.call-start = ((), (), s32[]{:S(2)}) async-start(), calls=%async_computation.76 | async-start | bytes 19464192 | tf_op jit(solution)/shard_map/all_gather | solution.py:191
  223.6 983.7 %all-gather.68.cloned.1.call-start = ((), (), s32[]{:S(2)}) async-start(), calls=%async_computation.93 | async-start | bytes 1966080 | tf_op jit(solution)/shard_map/all_gather | solution.py:323
  254.7 971.9 %all-gather.66.cloned.1.call-start = ((), (), s32[]{:S(2)}) async-start(), calls=%async_computation.91 | async-start | bytes 1966080 | tf_op jit(solution)/shard_map/all_gather | solution.py:323
  298.5 943.4 %all-gather.72.cloned.1.call-start = ((), (), s32[]{:S(2)}) async-start(), calls=%async_computation.97 | async-start | bytes 1966080 | tf_op jit(solution)/shard_map/all_gather | solution.py:324
  365.6 895.9 %all-gather.70.cloned.1.call-start = ((), (), s32[]{:S(2)}) async-start(), calls=%async_computation.95 | async-start | bytes 1966080 | tf_op jit(solution)/shard_map/all_gather | solution.py:324
  518.4 759.3 %all-gather.76.cloned.1.call-start = ((), (), s32[]{:S(2)}) async-start(), calls=%async_computation.101 | async-start | bytes 1966080 | tf_op jit(solution)/shard_map/all_gather | solution.py:326
  563.8 749.3 %all-gather.74.cloned.1.call-start = ((), (), s32[]{:S(2)}) async-start(), calls=%async_computation.99 | async-start | bytes 1966080 | tf_op jit(solution)/shard_map/all_gather | solution.py:326
  623.5 696.4 %reduce-scatter.58.cloned.1.call-start = ((), (), s32[]{:S(2)}) async-start(), calls=%async_computation.81 | async-start | bytes 491520 | tf_op jit(solution)/shard_map/reduce_scatter | solution.py:262
  1194.0 194.6 %reduce-scatter.56.cloned.1.call-start = ((), (), s32[]{:S(2)}) async-start(), calls=%async_computation.80 | async-start | bytes 491520 | tf_op jit(solution)/shard_map/reduce_scatter | solution.py:268
  1198.5 206.6 %all-gather.64.cloned.1.call-start = ((), (), s32[]{:S(2)}) async-start(), calls=%async_computation.85 | async-start | bytes 1966080 | tf_op jit(solution)/shard_map/all_gather | solution.py:322
  1199.1 220.9 %all-gather.62.cloned.1.call-start = ((), (), s32[]{:S(2)}) async-start(), calls=%async_computation.83 | async-start | bytes 1966080 | tf_op jit(solution)/shard_map/all_gather | solution.py:322
  1199.8 298.7 %all-gather.84.cloned.1.call-start = ((), (), s32[]{:S(2)}) async-start(), calls=%async_computation.110 | async-start | bytes 1966080 | tf_op jit(solution)/shard_map/all_gather | solution.py:328
  1200.9 336.3 %all-gather.82.cloned.1.call-start = ((), (), s32[]{:S(2)}) async-start(), calls=%async_computation.109 | async-start | bytes 1966080 | tf_op jit(solution)/shard_map/all_gather | solution.py:328
  1201.4 374.4 %all-gather.78.cloned.1.call-start = ((), (), s32[]{:S(2)}) async-start(), calls=%async_computation.103 | async-start | bytes 1966080 | tf_op jit(solution)/shard_map/all_gather | solution.py:327
  1202.2 423.3 %all-gather.80.cloned.1.call-start = ((), (), s32[]{:S(2)}) async-start(), calls=%async_computation.105 | async-start | bytes 1966080 | tf_op jit(solution)/shard_map/all_gather | solution.py:327
  1207.2 515.7 %reduce-scatter.76.cloned.1.call-start = ((), (), s32[]{:S(2)}) async-start(), calls=%async_computation.94 | async-start | bytes 1327104 | tf_op jit(solution)/shard_map/reduce_scatter | solution.py:348
  1226.5 496.4 %reduce-scatter.74.cloned.1.call-start = ((), (), s32[]{:S(2)}) async-start(), calls=%async_computation.92 | async-start | bytes 1327104 | tf_op jit(solution)/shard_map/reduce_scatter | solution.py:348
  1241.8 486.3 %reduce-scatter.80.cloned.1.call-start = ((), (), s32[]{:S(2)}) async-start(), calls=%async_computation.98 | async-start | bytes 1327104 | tf_op jit(solution)/shard_map/reduce_scatter | solution.py:348
  1261.4 507.8 %reduce-scatter.78.cloned.1.call-start = ((), (), s32[]{:S(2)}) async-start(), calls=%async_computation.96 | async-start | bytes 1327104 | tf_op jit(solution)/shard_map/reduce_scatter | solution.py:348
  1277.6 558.8 %reduce-scatter.84.cloned.1.call-start = ((), (), s32[]{:S(2)}) async-start(), calls=%async_computation.102 | async-start | bytes 1327104 | tf_op jit(solution)/shard_map/reduce_scatter | solution.py:348
  1306.9 596.5 %reduce-scatter.82.cloned.1.call-start = ((), (), s32[]{:S(2)}) async-start(), calls=%async_computation.100 | async-start | bytes 1327104 | tf_op jit(solution)/shard_map/reduce_scatter | solution.py:348
  1325.4 678.5 %reduce-scatter.114.cloned.1.call-start = ((), (), s32[]{:S(2)}) async-start(), calls=%async_computation.121 | async-start | bytes 811008
  1357.7 713.5 %reduce-scatter.104.cloned.1.call-start = ((), (), s32[]{:S(2)}) async-start(), calls=%async_computation.116 | async-start | bytes 1327104 | tf_op jit(solution)/shard_map/reduce_scatter | solution.py:348
  1365.6 772.6 %reduce-scatter.102.cloned.1.call-start = ((), (), s32[]{:S(2)}) async-start(), calls=%async_computation.115 | async-start | bytes 1327104 | tf_op jit(solution)/shard_map/reduce_scatter | solution.py:348
  1378.0 827.1 %reduce-scatter.108.cloned.1.call-start = ((), (), s32[]{:S(2)}) async-start(), calls=%async_computation.118 | async-start | bytes 1327104 | tf_op jit(solution)/shard_map/reduce_scatter | solution.py:348
  1388.6 883.3 %reduce-scatter.106.cloned.1.call-start = ((), (), s32[]{:S(2)}) async-start(), calls=%async_computation.117 | async-start | bytes 1327104 | tf_op jit(solution)/shard_map/reduce_scatter | solution.py:348
  1404.7 934.8 %reduce-scatter.64.cloned.1.call-start = ((), (), s32[]{:S(2)}) async-start(), calls=%async_computation.86 | async-start | bytes 1327104 | tf_op jit(solution)/shard_map/reduce_scatter | solution.py:348
  1419.9 987.0 %reduce-scatter.62.cloned.1.call-start = ((), (), s32[]{:S(2)}) async-start(), calls=%async_computation.84 | async-start | bytes 1327104 | tf_op jit(solution)/shard_map/reduce_scatter | solution.py:348
  1433.4 1041.0 %reduce-scatter.68.cloned.1.call-start = ((), (), s32[]{:S(2)}) async-start(), calls=%async_computation.88 | async-start | bytes 1327104 | tf_op jit(solution)/shard_map/reduce_scatter | solution.py:348
  1449.5 1091.9 %reduce-scatter.66.cloned.1.call-start = ((), (), s32[]{:S(2)}) async-start(), calls=%async_computation.87 | async-start | bytes 1327104 | tf_op jit(solution)/shard_map/reduce_scatter | solution.py:348
  1463.1 1145.2 %reduce-scatter.72.cloned.1.call-start = ((), (), s32[]{:S(2)}) async-start(), calls=%async_computation.90 | async-start | bytes 1327104 | tf_op jit(solution)/shard_map/reduce_scatter | solution.py:348
  1479.7 1195.7 %reduce-scatter.70.cloned.1.call-start = ((), (), s32[]{:S(2)}) async-start(), calls=%async_computation.89 | async-start | bytes 1327104 | tf_op jit(solution)/shard_map/reduce_scatter | solution.py:348
  1498.5 1275.1 %reduce-scatter.112.cloned.1.call-start = ((), (), s32[]{:S(2)}) async-start(), calls=%async_computation.120 | async-start | bytes 5308416 | tf_op jit(solution)/shard_map/reduce_scatter | solution.py:348
  1537.1 1335.5 %reduce-scatter.110.cloned.1.call-start = ((), (), s32[]{:S(2)}) async-start(), calls=%async_computation.119 | async-start | bytes 5308416 | tf_op jit(solution)/shard_map/reduce_scatter | solution.py:348
  1575.7 1395.9 %reduce-scatter.86.cloned.1.call-start = ((), (), s32[]{:S(2)}) async-start(), calls=%async_computation.104 | async-start | bytes 5308416 | tf_op jit(solution)/shard_map/reduce_scatter | solution.py:348
  1601.5 1469.1 %reduce-scatter.88.cloned.1.call-start = ((), (), s32[]{:S(2)}) async-start(), calls=%async_computation.106 | async-start | bytes 5308416 | tf_op jit(solution)/shard_map/reduce_scatter | solution.py:348
  1631.3 1538.3 %reduce-scatter.90.cloned.1.call-start = ((), (), s32[]{:S(2)}) async-start(), calls=%async_computation.107 | async-start | bytes 5308416 | tf_op jit(solution)/shard_map/reduce_scatter | solution.py:348
  1667.0 1601.4 %reduce-scatter.92.cloned.1.call-start = ((), (), s32[]{:S(2)}) async-start(), calls=%async_computation.108 | async-start | bytes 5308416 | tf_op jit(solution)/shard_map/reduce_scatter | solution.py:348
  2408.6 268.5 %all-to-all-start.2 = ((bf16[4,48,384]{2,1,0:T(8,128)(2,1)}), bf16[4,48,384]{2,1,0:T(8,128)(2,1)S(1)}, u32[]{:S(2)}, u32[]{:S(2)}) async-start(bf16[4,48,384]{2,1,0:T(8,128)(2,1)} %bitcast.79), calls=%async_computation.8 | async-start | bytes 294912 | tf_op jit(solution)/shard_map/all_to_all | solution.py:363
  3072.8 197.9 %all-to-all-start.26 = ((bf16[4,48,1536]{2,1,0:T(8,128)(2,1)}), bf16[4,48,1536]{2,1,0:T(8,128)(2,1)S(1)}, u32[]{:S(2)}, u32[]{:S(2)}) async-start(bf16[4,48,1536]{2,1,0:T(8,128)(2,1)} %bitcast.143), calls=%async_computation.44 | async-start | bytes 1179648 | tf_op jit(solution)/shard_map/all_to_all | solution.py:363
  (201 other events, 7690.0 us)
Sparse Core Ops, SparseCore 0:
  10.9 66.3 all-gather.37
  80.2 61.8 all-gather.35
  145.0 61.8 all-gather.31
  229.1 19.8 all-gather.57
  295.7 63.5 all-gather.41
  362.2 61.8 all-gather.43
  426.8 61.8 all-gather.47
  491.6 61.9 all-gather.45
  556.3 61.8 all-gather.49
  621.1 122.2 all-gather.51
  746.2 122.1 all-gather.53
  871.2 122.1 all-gather.55
  1014.9 19.8 all-gather.65
  1157.3 27.9 reduce-scatter.97
  1187.7 32.2 reduce-scatter.93
  1222.5 32.2 reduce-scatter.99
  1257.2 31.2 reduce-scatter.95
  1291.4 23.9 reduce-scatter.53
  1318.4 20.8 reduce-scatter.59
  1341.8 20.8 reduce-scatter.55
  1385.3 20.7 all-gather.61
  1407.6 22.3 all-gather.83
  1431.4 22.0 all-gather.81
  1455.0 23.6 all-gather.77
  1480.3 19.8 all-gather.79
  1503.4 64.6 reduce-scatter.75
  1571.4 63.6 reduce-scatter.73
  1638.5 63.6 reduce-scatter.79
  1705.4 63.7 reduce-scatter.77
  1772.6 63.6 reduce-scatter.83
  1839.7 63.6 reduce-scatter.81
  1908.6 95.2 reduce-scatter.113
  2007.1 63.9 reduce-scatter.103
  2074.6 63.5 reduce-scatter.101
  2141.5 63.5 reduce-scatter.107
  2208.3 63.5 reduce-scatter.105
  2275.7 63.6 reduce-scatter.63
  2343.2 63.6 reduce-scatter.61
  2410.8 63.6 reduce-scatter.67
  2477.8 63.5 reduce-scatter.65
  2544.7 63.5 reduce-scatter.71
  2611.7 63.6 reduce-scatter.69
  2678.9 94.6 reduce-scatter.111
  2777.3 95.2 reduce-scatter.109
  2876.3 95.2 reduce-scatter.85
  2975.2 95.3 reduce-scatter.87
  3074.2 95.3 reduce-scatter.89
  3173.1 95.2 reduce-scatter.91
  (10 shorter events, 192.9 us)
where the time goes:
time: 3310 us; the launch traced here: 3290 us
  waiting for transfers between devices  2400 us (73%)
  matrix products  396 us (12%)
  blocking collectives  201 us (6%)
  local copies, waits for them, and re-layouts  126 us (4%)
  starting transfers between devices  93.5 us (3%)
  other arithmetic  60 us (2%)
    reduce_scatter x22, waiting for transfers between devices, per_device(): lax.psum_scatter(as_sent(partial_value), 'dp', scatter_dimension=0, tiled...  1380 us
    dot_general x22, matrix products, times_transpose(): lax.dot_general(left, right, (((1,), (1,)), ((), ())), preferred_element_...  138 us
    all_gather x1, waiting for transfers between devices, per_device(): lax.all_gather(shards[11], ('dp', 'seq'), axis=0, tiled=True)  118 us
    all_gather x1, waiting for transfers between devices, per_device(): lax.all_gather(shards[12], ('dp', 'seq'), axis=0, tiled=True)  114 us
    all_gather x1, waiting for transfers between devices, per_device(): lax.all_gather(shards[13], ('dp', 'seq'), axis=0, tiled=True)  114 us
    dot_general x22, matrix products, product(): return jnp.dot(left, right, preferred_element_type=jnp.float32)  112 us
    unnamed x63, waiting for transfers between devices  86.5 us
    dot_general x22, matrix products, contract_rows(): lax.dot_general(left, right, (((0,), (0,)), ((), ())), preferred_element_...  80.2 us
  transfers between devices with their start and end apart: 83, of which 53 were waited for; matrix products, arithmetic and copies ran while one was open for 17% of the time, Pallas kernels for 0%

commit v1 on v0

v1 whole, which is shorter than its diff:
```python
import functools
import math

import jax
import jax.numpy as jnp
from jax import lax
from jax.experimental import pallas as pl
from jax.experimental.pallas import tpu as pltpu
from jax.sharding import PartitionSpec as P

HEADS = 24
HEAD = 64
ROT = 32
EPSILON = 1e-05
BF = jnp.bfloat16
F32 = jnp.float32
PAIR = 2 * HEAD


def mm(left, right):
    return jnp.dot(left, right, preferred_element_type=F32)


def mm_t(left, right):
    return lax.dot_general(left, right, (((1,), (1,)), ((), ())), preferred_element_type=F32)


def t_mm(left, right):
    return lax.dot_general(left, right, (((0,), (0,)), ((), ())), preferred_element_type=F32)


def seq_swap(x, mask):
    n = lax.axis_size("seq")
    return lax.ppermute(x, "seq", [(i, i ^ mask) for i in range(n)])


def dp_swap(x, mask):
    n = lax.axis_size("dp")
    return lax.ppermute(x, "dp", [(i, i ^ mask) for i in range(n)])


def all_sum(v):
    for mask in (1, 2):
        v = v + seq_swap(v, mask)
    mask = 1
    while mask < lax.axis_size("dp"):
        v = v + dp_swap(v, mask)
        mask *= 2
    return v


def gather_seq(x):
    core = seq_swap(x, 1)
    far = seq_swap(x, 2)
    diag = seq_swap(far, 1)
    return jnp.stack([x, core, far, diag])


def scatter_seq(partial):
    far = partial[2].astype(F32) + seq_swap(partial[3], 1).astype(F32)
    arrived = seq_swap(far.astype(BF), 2)
    near = partial[0].astype(F32) + seq_swap(partial[1], 1).astype(F32)
    return near + arrived.astype(F32)


RING_Z, RING_X = 4, 2


def ringed():
    return lax.axis_size("dp") == RING_Z * RING_X


def z_next(x):
    n = lax.axis_size("dp")
    return lax.ppermute(x, "dp", [(i, (i + RING_X) % n) for i in range(n)])


def ring_pieces(x):
    d = lax.axis_index("dp")
    z, xx = d // RING_X, d % RING_X
    held = x
    for k in range(RING_Z):
        zk = (z + RING_Z - k) % RING_Z
        yield zk * RING_X + xx, held
        yield zk * RING_X + 1 - xx, dp_swap(held, 1)
        if k < RING_Z - 1:
            held = z_next(held)


def gather_dp(chunk):
    if not ringed():
        return lax.all_gather(chunk, "dp", axis=0, tiled=True)
    rows, cols = chunk.shape
    out = jnp.zeros((rows * lax.axis_size("dp"), cols), chunk.dtype)
    for index, piece in ring_pieces(chunk):
        out = lax.dynamic_update_slice(out, piece, (index * rows, 0))
    return out


def reduce_dp(slots):
    if not ringed():
        n, rows, cols = slots.shape
        return lax.psum_scatter(
            slots.reshape(n * rows, cols), "dp", scatter_dimension=0, tiled=True
        ).astype(F32)
    d = lax.axis_index("dp")
    z, xx = d // RING_X, d % RING_X
    n, rows, cols = slots.shape
    split = slots.reshape(RING_Z, RING_X, rows, cols)
    away = lax.dynamic_index_in_dim(split, 1 - xx, axis=1, keepdims=False)
    kept = lax.dynamic_index_in_dim(split, xx, axis=1, keepdims=False)
    arrived = dp_swap(away, 1)
    both = (kept.astype(F32) + arrived.astype(F32)).astype(BF)

    def at(k):
        return lax.dynamic_index_in_dim(both, (z + RING_Z - k) % RING_Z, axis=0, keepdims=False)

    total = at(1)
    for k in range(2, RING_Z + 1):
        total = z_next(total.astype(BF)).astype(F32) + at(k).astype(F32)
    return total


def columns_out(x):
    rows = x.shape[0]
    n = lax.axis_size("seq")
    return x.reshape(rows, HEADS // n, n, HEAD).transpose(2, 0, 1, 3).reshape(n, rows, -1)


def columns_back(x):
    n, rows, _ = x.shape
    return x.reshape(n, rows, HEADS // n, HEAD).transpose(1, 2, 0, 3).reshape(rows, HEADS * HEAD)


def blocks_out(x):
    rows = x.shape[0]
    n = lax.axis_size("seq")
    return x.reshape(rows, n, -1).transpose(1, 0, 2)


def blocks_back(x):
    return x.transpose(1, 0, 2).reshape(x.shape[1], -1)


def deal(x):
    got = lax.all_to_all(x, "seq", split_axis=0, concat_axis=0, tiled=True)
    return got.reshape(-1, x.shape[-1])


def collect(x):
    n = lax.axis_size("seq")
    return lax.all_to_all(
        x.reshape(n, -1, x.shape[-1]), "seq", split_axis=0, concat_axis=0, tiled=True
    )


def head_slot():
    s, d = lax.axis_index("seq"), lax.axis_index("dp")
    n = lax.axis_size("seq")
    per = HEADS // lax.axis_size("dp")
    return (s + (n - per % n) * d) % n, per, n


def slot_place(d):
    s = lax.axis_index("seq")
    n = lax.axis_size("seq")
    per = HEADS // lax.axis_size("dp")
    j = (s + (n - per % n) * d) % n
    return jnp.where(j < per, (per * d + j - s) // n, HEADS // n)


def gather_head_rows(x):
    n = lax.axis_size("seq")
    s = lax.axis_index("seq")
    cols = x.shape[1]
    mine = HEADS // n
    if not ringed():
        full = lax.all_gather(x, ("dp", "seq"), axis=0, tiled=True)
        picked = lax.dynamic_index_in_dim(full.reshape(mine, n, HEAD, cols), s, 1, keepdims=False)
        return picked.reshape(mine * HEAD, cols)
    rows = lax.all_gather(x, "seq", axis=0, tiled=True)
    j, per, _ = head_slot()
    rows = jnp.concatenate([rows, jnp.zeros((HEAD, cols), x.dtype)])
    piece = lax.dynamic_slice(rows, (j * HEAD, 0), (HEAD, cols))
    out = jnp.zeros(((mine + 1) * HEAD, cols), x.dtype)
    for index, held in ring_pieces(piece):
        out = lax.dynamic_update_slice(out, held, (slot_place(index) * HEAD, 0))
    return out[: mine * HEAD]


def reduce_head_rows(x):
    n = lax.axis_size("seq")
    s = lax.axis_index("seq")
    size = lax.axis_size("dp")
    cols = x.shape[1]
    mine = HEADS // n
    if not ringed():
        full = jnp.zeros((mine, n, HEAD, cols), BF)
        full = lax.dynamic_update_index_in_dim(full, x.reshape(mine, 1, HEAD, cols), s, 1)
        return lax.psum_scatter(
            full.reshape(-1, cols), ("dp", "seq"), scatter_dimension=0, tiled=True
        ).astype(F32)
    padded = jnp.concatenate([x, jnp.zeros((HEAD, cols), x.dtype)])
    slots = jnp.stack(
        [lax.dynamic_slice(padded, (slot_place(d) * HEAD, 0), (HEAD, cols)) for d in range(size)]
    )
    own = reduce_dp(slots).astype(BF)
    pieces = lax.all_gather(own, "seq", axis=0, tiled=False)
    per = HEADS // size
    d = lax.axis_index("dp")
    rows = jnp.concatenate(
        [
            lax.dynamic_index_in_dim(pieces, (per * d + j) % n, 0, keepdims=False)
            for j in range(per)
        ]
    )
    share = per * HEAD // n
    return lax.dynamic_slice(rows, (s * share, 0), (share, cols)).astype(F32)


def norm_forward(values, gain_vec):
    average = jnp.mean(values, axis=-1, keepdims=True)
    centred = values - average
    variance = jnp.mean(centred * centred, axis=-1, keepdims=True)
    inv_std = lax.rsqrt(variance + EPSILON)
    normal = centred * inv_std
    return normal, inv_std, (normal * gain_vec).astype(BF)


def norm_backward(grad_normed, normal, inv_std, gain_vec):
    grad_gain = jnp.sum(grad_normed * normal, axis=0)
    grad_hat = grad_normed * gain_vec
    mean_hat = jnp.mean(grad_hat, axis=-1, keepdims=True)
    mean_mix = jnp.mean(grad_hat * normal, axis=-1, keepdims=True)
    return inv_std * (grad_hat - mean_hat - normal * mean_mix), grad_gain


def flat(ref):
    value = ref[...]
    return value.reshape(value.shape[0] * value.shape[1] * value.shape[2], value.shape[3])


def turn(m, cos, up, down):
    return m * cos + pltpu.roll(m, PAIR - ROT // 2, 1) * up + pltpu.roll(m, ROT // 2, 1) * down


SCALE = 1.0 / math.sqrt(HEAD)


def soft(q, k, ok):
    scores = mm_t(q, k) * SCALE
    scores = jnp.where(ok > 0.0, scores, -1e30)
    top = jnp.max(scores, axis=-1, keepdims=True)
    e = jnp.exp(scores - top)
    return e * (1.0 / jnp.sum(e, axis=-1, keepdims=True))


def self_forward_kernel(ok_ref, cos_ref, up_ref, down_ref, q_ref, k_ref, v_ref, o_ref, qr_ref, kr_ref, vr_ref):
    cos, up, down = (r[...].reshape(-1, PAIR) for r in (cos_ref, up_ref, down_ref))
    q = turn(flat(q_ref), cos, up, down).astype(BF)
    k = turn(flat(k_ref), cos, up, down).astype(BF)
    v = flat(v_ref).astype(BF)
    ok = ok_ref[0]
    outs = []
    for h in (0, 1):
        sl = slice(h * HEAD, (h + 1) * HEAD)
        p = soft(q[:, sl], k[:, sl], ok).astype(BF)
        outs.append(mm(p, v[:, sl]))
    o_ref[...] = jnp.concatenate(outs, axis=1).astype(BF).reshape(o_ref.shape)
    qr_ref[...] = q.reshape(qr_ref.shape)
    kr_ref[...] = k.reshape(kr_ref.shape)
    vr_ref[...] = v.reshape(vr_ref.shape)


def pair_back(q, k, v, g, ok):
    dqs, dks, dvs = [], [], []
    for h in (0, 1):
        sl = slice(h * HEAD, (h + 1) * HEAD)
        p = soft(q[:, sl], k[:, sl], ok)
        dp = mm_t(g[:, sl], v[:, sl])
        inner = jnp.sum(p * dp, axis=-1, keepdims=True)
        ds = (p * (dp - inner)).astype(BF)
        dqs.append(mm(ds, k[:, sl]) * SCALE)
        dks.append(t_mm(ds, q[:, sl]) * SCALE)
        dvs.append(t_mm(p.astype(BF), g[:, sl]))
    return [jnp.concatenate(t, axis=1) for t in (dqs, dks, dvs)]


def self_backward_kernel(ok_ref, cos_ref, up_ref, down_ref, q_ref, k_ref, v_ref, g_ref, o_ref):
    cos, up, down = (r[...].reshape(-1, PAIR) for r in (cos_ref, up_ref, down_ref))
    dq, dk, dv = pair_back(flat(q_ref), flat(k_ref), flat(v_ref), flat(g_ref), ok_ref[0])
    dq = turn(dq, cos, -up, -down)
    dk = turn(dk, cos, -up, -down)
    pairs = o_ref.shape[3] // (3 * PAIR)
    hp = pl.program_id(1)
    shape = o_ref.shape[:3] + (PAIR,)
    for which, value in enumerate((dq, dk, dv)):
        at = pl.ds(pl.multiple_of((which * pairs + hp) * PAIR, PAIR), PAIR)
        o_ref[:, :, :, at] = value.astype(BF).reshape(shape)


def cross_forward_kernel(ok_ref, q_ref, k_ref, v_ref, o_ref):
    q, k, v = flat(q_ref), flat(k_ref), flat(v_ref)
    ok = ok_ref[0]
    outs = []
    for h in (0, 1):
        sl = slice(h * HEAD, (h + 1) * HEAD)
        p = soft(q[:, sl], k[:, sl], ok).astype(BF)
        outs.append(mm(p, v[:, sl]))
    o_ref[...] = jnp.concatenate(outs, axis=1).astype(BF).reshape(o_ref.shape)


def cross_backward_kernel(ok_ref, q_ref, k_ref, v_ref, g_ref, dq_ref, dkv_ref):
    dq, dk, dv = pair_back(flat(q_ref), flat(k_ref), flat(v_ref), flat(g_ref), ok_ref[0])
    dq_ref[...] = dq.astype(BF).reshape(dq_ref.shape)
    pairs = dkv_ref.shape[3] // (2 * PAIR)
    hp = pl.program_id(1)
    shape = dkv_ref.shape[:3] + (PAIR,)
    for which, value in enumerate((dk, dv)):
        at = pl.ds(pl.multiple_of((which * pairs + hp) * PAIR, PAIR), PAIR)
        dkv_ref[:, :, :, at] = value.astype(BF).reshape(shape)


def pair_spec(x, offset=0):
    r, _, t, _ = x.shape
    return pl.BlockSpec((r, 1, t, PAIR), lambda b, hp: (0, b, 0, offset + hp))


def wide_spec(r, t, width):
    return pl.BlockSpec((r, 1, t, width), lambda b, hp: (0, b, 0, 0))


def ok_spec(ok):
    return pl.BlockSpec((1, 1, ok.shape[2]), lambda b, hp: (b, 0, 0))


def table_spec(table):
    return pl.BlockSpec(table.shape, lambda b, hp: (0, 0, 0))


def cost(x, keys, products):
    r, b, t, width = x.shape
    return pl.CostEstimate(
        flops=2 * r * b * t * width * keys * products * 2,
        bytes_accessed=8 * x.size,
        transcendentals=r * b * t * keys * (width // HEAD),
    )


def self_forward(ok, tables, qkv):
    r, b, t, width = qkv.shape
    pairs = width // (3 * PAIR)
    shape = jax.ShapeDtypeStruct((r, b, t, pairs * PAIR), BF)
    return pl.pallas_call(
        self_forward_kernel,
        grid=(b, pairs),
        in_specs=[ok_spec(ok)]
        + [table_spec(x) for x in tables]
        + [pair_spec(qkv, i * pairs) for i in range(3)],
        out_specs=[pair_spec(shape)] * 4,
        out_shape=[shape] * 4,
        cost_estimate=cost(shape, r * t, 2),
        name="self_forward",
    )(ok, *tables, qkv, qkv, qkv)


def self_backward(ok, tables, q, k, v, g):
    r, b, t, width = q.shape
    pairs = width // PAIR
    return pl.pallas_call(
        self_backward_kernel,
        grid=(b, pairs),
        in_specs=[ok_spec(ok)] + [table_spec(x) for x in tables] + [pair_spec(q)] * 4,
        out_specs=wide_spec(r, t, 3 * width),
        out_shape=jax.ShapeDtypeStruct((r, b, t, 3 * width), BF),
        cost_estimate=cost(q, r * t, 5),
        name="self_backward",
    )(ok, *tables, q, k, v, g)


def cross_forward(ok, q, kv):
    r, b, t, width = q.shape
    pairs = width // PAIR
    return pl.pallas_call(
        cross_forward_kernel,
        grid=(b, pairs),
        in_specs=[ok_spec(ok), pair_spec(q), pair_spec(kv), pair_spec(kv, pairs)],
        out_specs=pair_spec(q),
        out_shape=jax.ShapeDtypeStruct(q.shape, BF),
        cost_estimate=cost(q, r * kv.shape[2], 2),
        name="cross_forward",
    )(ok, q, kv, kv)


def cross_backward(ok, q, kv, g):
    r, b, t, width = q.shape
    pairs = width // PAIR
    return pl.pallas_call(
        cross_backward_kernel,
        grid=(b, pairs),
        in_specs=[ok_spec(ok), pair_spec(q), pair_spec(kv), pair_spec(kv, pairs), pair_spec(q)],
        out_specs=[pair_spec(q), wide_spec(r, kv.shape[2], kv.shape[3])],
        out_shape=[jax.ShapeDtypeStruct(q.shape, BF), jax.ShapeDtypeStruct(kv.shape, BF)],
        cost_estimate=cost(q, r * kv.shape[2], 5),
        name="cross_backward",
    )(ok, q, kv, kv, g)


def per_device(
    inputs,
    conditioning,
    seq_lengths,
    cond_lengths,
    gain_self,
    gain_cross,
    gain_mlp,
    w_query,
    w_key,
    w_value,
    w_output,
    c_query,
    c_key,
    c_value,
    c_output,
    w_gate,
    w_up,
    w_down,
    cotangent,
):
    batch, tokens_dev, width = inputs.shape
    cond_dev = conditioning.shape[1]
    n = lax.axis_size("seq")
    dp = lax.axis_size("dp")
    s = lax.axis_index("seq")
    d = lax.axis_index("dp")
    rel = jnp.arange(n) ^ s
    mine = width // n

    positions = rel[:, None] * tokens_dev + jnp.arange(tokens_dev)[None, :]
    key_ok = (positions.reshape(1, 1, -1) < seq_lengths[:, None, None]).astype(F32)
    cond_pos = rel[:, None] * cond_dev + jnp.arange(cond_dev)[None, :]
    cond_ok = (cond_pos.reshape(1, 1, -1) < cond_lengths[:, None, None]).astype(F32)
    half = ROT // 2
    inverse = 10000.0 ** (-jnp.arange(half).astype(F32) / half)
    angles = positions.astype(F32)[:, :, None] * inverse
    cosine, sine = jnp.cos(angles), jnp.sin(angles)
    one, nil = jnp.ones(cosine.shape[:2] + (HEAD - ROT,), F32), jnp.zeros_like(cosine)
    nil_rest = jnp.zeros_like(one)
    tables = [
        jnp.concatenate(parts + parts, axis=-1)
        for parts in (
            [cosine, cosine, one],
            [-sine, nil, nil_rest],
            [nil, sine, nil_rest],
        )
    ]

    gain_rows = jnp.stack([gain_self, gain_cross, gain_mlp]).astype(F32)
    share = gain_rows.shape[1]
    gains = all_sum(
        lax.dynamic_update_slice(jnp.zeros((3, width), F32), gain_rows, (0, (d * n + s) * share))
    )
    gain_one, gain_two, gain_three = gains[0], gains[1], gains[2]

    rows = batch * tokens_dev
    total = n * rows
    qkv_w = gather_dp(
        deal(jnp.concatenate([columns_out(w) for w in (w_query, w_key, w_value)], axis=2))
    )
    out_w = gather_head_rows(jnp.concatenate([w_output, c_output], axis=1))
    w_out, c_out = out_w[:, :width], out_w[:, width:]
    cross_w = gather_dp(
        deal(jnp.concatenate([columns_out(w) for w in (c_query, c_key, c_value)], axis=2))
    )
    cq_w, ckv_w = cross_w[:, :mine], cross_w[:, mine:]
    gu_w = gather_dp(deal(jnp.concatenate([blocks_out(w_gate), blocks_out(w_up)], axis=2)))
    down_w = gather_dp(deal(blocks_out(w_down)))
    hid = down_w.shape[1]

    tokens = inputs.reshape(rows, width)
    incoming = cotangent.reshape(rows, width)
    tokens_all = gather_seq(tokens)
    cond_all = gather_seq(conditioning.reshape(batch * cond_dev, width)).reshape(-1, width)
    incoming_all = gather_seq(incoming).reshape(total, width)

    normed_one = norm_forward(tokens_all.reshape(total, width).astype(F32), gain_one)[2]
    qkv = mm(normed_one, qkv_w).reshape(n, batch, tokens_dev, 3 * mine)
    attended, q_rot, k_rot, v_low = self_forward(key_ok, tables, qkv)
    attended = attended.reshape(total, mine)
    partial = mm(attended, w_out).astype(BF).reshape(n, rows, width)
    after_self = tokens.astype(F32) + scatter_seq(partial)
    normal_two, inv_two, own_two = norm_forward(after_self, gain_two)
    normed_two = gather_seq(own_two).reshape(total, width)
    cq = mm(normed_two, cq_w).astype(BF).reshape(n, batch, tokens_dev, mine)
    ckv = mm(cond_all, ckv_w).astype(BF).reshape(n, batch, cond_dev, 2 * mine)
    cross_att = cross_forward(cond_ok, cq, ckv).reshape(total, mine)
    partial = mm(cross_att, c_out).astype(BF).reshape(n, rows, width)
    after_cross = after_self + scatter_seq(partial)
    normal_three, inv_three, own_three = norm_forward(after_cross, gain_three)
    normed_three = gather_seq(own_three).reshape(total, width)
    gate = mm(normed_three, gu_w[:, :hid])
    up = mm(normed_three, gu_w[:, hid:])
    sig = jax.nn.sigmoid(gate)
    hidden = (gate * sig * up).astype(BF)
    partial = mm_t(hidden, down_w).astype(BF).reshape(n, rows, width)
    block = (after_cross + scatter_seq(partial)).astype(BF)
    d_down = t_mm(incoming_all, hidden).astype(BF)
    d_hidden = mm(incoming_all, down_w)
    d_gate = (d_hidden * up * sig * (1.0 + gate * (1.0 - sig))).astype(BF)
    d_up = (d_hidden * gate * sig).astype(BF)
    d_gu = jnp.concatenate([d_gate, d_up], axis=1)
    partial = mm_t(d_gu, gu_w).astype(BF).reshape(n, rows, width)
    d_norm3 = scatter_seq(partial)
    grad_gu = t_mm(normed_three, d_gu).astype(BF)
    back, gain_grad_three = norm_backward(d_norm3, normal_three, inv_three, gain_three)
    d_after_cross = incoming.astype(F32) + back
    dc_low = gather_seq(d_after_cross.astype(BF)).reshape(total, width)
    d_catt = mm_t(dc_low, c_out).astype(BF).reshape(n, batch, tokens_dev, mine)
    grad_c_out = t_mm(cross_att, dc_low).astype(BF)
    d_cq, d_ckv = cross_backward(cond_ok, cq, ckv, d_catt)
    d_cq = d_cq.reshape(total, mine)
    d_ckv = d_ckv.reshape(n * batch * cond_dev, 2 * mine)
    partial = mm_t(d_cq, cq_w).astype(BF).reshape(n, rows, width)
    d_norm2 = scatter_seq(partial)
    partial = mm_t(d_ckv, ckv_w).astype(BF).reshape(n, batch * cond_dev, width)
    grad_cond = scatter_seq(partial)
    grad_cross = jnp.concatenate([t_mm(normed_two, d_cq), t_mm(cond_all, d_ckv)], axis=1).astype(BF)
    back, gain_grad_two = norm_backward(d_norm2, normal_two, inv_two, gain_two)
    d_after_self = d_after_cross + back
    ds_low = gather_seq(d_after_self.astype(BF)).reshape(total, width)
    d_att = mm_t(ds_low, w_out).astype(BF).reshape(n, batch, tokens_dev, mine)
    grad_out = t_mm(attended, ds_low).astype(BF)
    d_qkv = self_backward(key_ok, tables, q_rot, k_rot, v_low, d_att).reshape(total, 3 * mine)
    partial = mm_t(d_qkv, qkv_w).astype(BF).reshape(n, rows, width)
    d_norm1 = scatter_seq(partial)
    grad_qkv = t_mm(normed_one, d_qkv).astype(BF)
    normal_one, inv_one, _ = norm_forward(tokens.astype(F32), gain_one)
    back, gain_grad_one = norm_backward(d_norm1, normal_one, inv_one, gain_one)
    grad_in = d_after_self + back

    def owned(grad):
        return collect(reduce_dp(grad.reshape(dp, width // dp, grad.shape[1])).astype(BF))

    own_down = blocks_back(owned(d_down))
    own_gu = owned(grad_gu)
    own_gate, own_up = blocks_back(own_gu[:, :, :hid]), blocks_back(own_gu[:, :, hid:])
    own_cross = owned(grad_cross)
    own_out = reduce_head_rows(jnp.concatenate([grad_out, grad_c_out], axis=1))
    own_qkv = owned(grad_qkv)
    g_q, g_k, g_v = (columns_back(own_qkv[:, :, i * mine : (i + 1) * mine]) for i in range(3))
    g_cq, g_ck, g_cv = (columns_back(own_cross[:, :, i * mine : (i + 1) * mine]) for i in range(3))
    gain_grads = all_sum(jnp.stack([gain_grad_one, gain_grad_two, gain_grad_three]))
    gain_grads = lax.dynamic_slice(gain_grads, (0, (d * n + s) * share), (3, share))

    def f32(x):
        return x.astype(F32)

    return (
        block.reshape(inputs.shape),
        grad_in.reshape(inputs.shape),
        grad_cond.reshape(conditioning.shape),
        gain_grads[0],
        gain_grads[1],
        gain_grads[2],
        f32(g_q),
        f32(g_k),
        f32(g_v),
        f32(own_out[:, :width]),
        f32(g_cq),
        f32(g_ck),
        f32(g_cv),
        f32(own_out[:, width:]),
        f32(own_gate),
        f32(own_up),
        f32(own_down),
    )


def solution(mesh):
    rows = P("dp", "seq", None)
    split = P(("dp", "seq"))
    matrix = P(("dp", "seq"), None)
    return jax.shard_map(
        per_device,
        mesh=mesh,
        in_specs=(rows, rows, P("dp"), P("dp"), split, split, split) + (matrix,) * 11 + (rows,),
        out_specs=(rows, rows, rows, split, split, split) + (matrix,) * 11,
        check_vma=False,
    )
```

time: 3310 us -> 997 us (0.30)
  waiting for transfers between devices: 2400 us -> 435 us
  matrix products: 396 us -> 128 us
  blocking collectives: 201 us -> 0 us
  Pallas kernels: 0 us -> 53.5 us
    reduce_scatter x26 -> x0, waiting for transfers between devices: 1380 us -> none  [the longest x22 1380 us: per_device(): lax.psum_scatter(as_sent(partial_value), 'dp', scatter_dimension=0, tiled...]
    all_gather x27 -> x2, waiting for transfers between devices: 767 us -> 0.01 us  [the longest x1 0.01 us: gather_head_rows(): rows = lax.all_gather(x, 'seq', axis=0, tiled=True)]
    ppermute x0 -> x107, waiting for transfers between devices: none -> 419 us  [the longest x31 225 us: dp_swap(): return lax.ppermute(x, 'dp', [(i, i ^ mask) for i in range(n)])]
    dot_general x90 -> x22, matrix products: 396 us -> 128 us  [the longest x8 52 us: mm(): return jnp.dot(left, right, preferred_element_type=F32)]
    all_to_all x25 -> x8, waiting for transfers between devices: 166 us -> 15.9 us  [the longest x4 11.8 us: deal(): got = lax.all_to_all(x, 'seq', split_axis=0, concat_axis=0, tiled=True)]
    all_to_all x8 -> x0, blocking collectives: 105 us -> none  [the longest x2 23.8 us: per_device(): lax.all_to_all(v_grad_low, 'seq', split_axis=1, concat_axis=0, tiled=True)]
    ppermute x0 -> x107, starting transfers between devices: none -> 86.8 us  [the longest x31 30.2 us: dp_swap(): return lax.ppermute(x, 'dp', [(i, i ^ mask) for i in range(n)])]
    unnamed x63 -> x2, waiting for transfers between devices: 86.5 us -> 0.03 us
  transfers between devices with their start and end apart: 83 -> 117, of which waited for: 53 -> 49; matrix products, arithmetic and copies ran while one was open for 17% -> 31% of each run, Pallas kernels for 0% -> 5%
where the time goes in v1:
time: 997 us; the launch traced here: 986 us
  waiting for transfers between devices  435 us (44%)
  local copies, waits for them, and re-layouts  143 us (14%)
  matrix products  128 us (13%)
  starting transfers between devices  119 us (12%)
  other arithmetic  91.7 us (9%)
  Pallas kernels  53.5 us (5%)
  between operations  16.2 us (2%)
    ppermute x31, waiting for transfers between devices, dp_swap(): return lax.ppermute(x, 'dp', [(i, i ^ mask) for i in range(n)])  225 us
    ppermute x30, waiting for transfers between devices, z_next(): return lax.ppermute(x, 'dp', [(i, (i + RING_X) % n) for i in range(n)])  144 us
    dot_general x8, matrix products, mm(): return jnp.dot(left, right, preferred_element_type=F32)  52 us
    ppermute x46, waiting for transfers between devices, seq_swap(): return lax.ppermute(x, 'seq', [(i, i ^ mask) for i in range(n)])  49.4 us
    dynamic_update_slice x32, local copies, waits for them, and re-layouts, gather_dp(): out = lax.dynamic_update_slice(out, piece, (index * rows, 0))  46.6 us
    dot_general x7, matrix products, mm_t(): lax.dot_general(left, right, (((1,), (1,)), ((), ())), preferred_element_...  45.3 us
    dot_general x7, matrix products, t_mm(): lax.dot_general(left, right, (((0,), (0,)), ((), ())), preferred_element_...  30.8 us
    ppermute x31, starting transfers between devices, dp_swap(): return lax.ppermute(x, 'dp', [(i, i ^ mask) for i in range(n)])  30.2 us
  transfers between devices with their start and end apart: 117, of which 49 were waited for; matrix products, arithmetic and copies ran while one was open for 31% of the time, Pallas kernels for 5%

profile of v1, /device:TPU:0, one launch (start us, length us, event | category | flops | bytes accessed | tf_op | source)
XLA Modules:
  0.0 986.0 jit_solution(5277267275906308991)
XLA Ops:
  83.3 10.7 %all-to-all-done.1 = bf16[4,48,1152]{2,1,0:T(8,128)(2,1)S(1)} async-done(((bf16[4,48,1152]{2,1,0:T(8,128)(2,1)}), bf16[4,48,1152]{2,1,0:T(8,128)(2,1)S(1)}, u32[]{:S(2)}, u32[]{:S(2)}) %all-to-all-start.1) | async-done | bytes 442400 | tf_op jit(solution)/shard_map/all_to_all | solution.py:146
  120.5 5.6 collective-permute-done.28
  132.2 4.8 broadcast_in_dim.19
  151.5 9.0 collective-permute-done.13
  160.9 9.8 collective-permute-done.12
  181.9 8.1 fusion.17.q_ref.k_ref.v_ref
  190.0 15.6 %self_forward.1 = (bf16[4,2,128,384]{3,2,1,0:T(8,128)(2,1)}, bf16[4,2,128,384]{3,2,1,0:T(8,128)(2,1)}, bf16[4,2,128,384]{3,2,1,0:T(8,128)(2,1)}, bf16[4,2,128,384]{3,2,1,0:T(8,128)(2,1)}) custom-call(f32[2,1,512]{2,1,0:T(1,128)} %compare_convert_fusion.ok_ref, f32[4,128,128]{2,1,0:T(8,128)} %concatenate.42.cos_ref, f32[4,128,128]{2,1,0:T(8,128)} %concatenate.43.up_ref, ...), custom_call_target="tpu_custom_call" | custom-call | flops 1610612736 | bytes 3145728 | tf_op jit(solution)/shard_map/self_forward/pallas_call | solution.py:354
  209.6 6.2 collective-permute-done.18
  220.3 6.1 collective-permute-done.19
  226.4 6.1 collective-permute-done.20
  234.1 6.6 collective-permute-done.21
  251.5 11.2 %collective-permute-done.31 = bf16[192,1152]{1,0:T(8,128)(2,1)S(1)} collective-permute-done((bf16[192,1152]{1,0:T(8,128)(2,1)S(1)}, bf16[192,1152]{1,0:T(8,128)(2,1)S(1)}, u32[]{:S(2)}, u32[]{:S(2)}) %collective-permute-start.31) | collective-permute-done | bytes 442400 | tf_op jit(solution)/shard_map/ppermute | solution.py:75
  268.9 21.6 %collective-permute-done.53 = bf16[192,1536]{1,0:T(8,128)(2,1)S(1)} collective-permute-done((bf16[192,1536]{1,0:T(8,128)(2,1)S(1)}, bf16[192,1536]{1,0:T(8,128)(2,1)S(1)}, u32[]{:S(2)}, u32[]{:S(2)}) %collective-permute-start.53) | collective-permute-done | bytes 589856 | tf_op jit(solution)/shard_map/ppermute | solution.py:39
  294.9 6.9 collective-permute-done.32
  301.8 12.7 %collective-permute-start.45 = (bf16[192,3072]{1,0:T(8,128)(2,1)}, bf16[192,3072]{1,0:T(8,128)(2,1)S(1)}, u32[]{:S(2)}, u32[]{:S(2)}) collective-permute-start(bf16[192,3072]{1,0:T(8,128)(2,1)} %bitcast.45), channel_id=1, source_target_pairs={{0,8},{4,12},{8,16},{12,20},{16,24},{20,28},{24,0},{28,4},{1,9},{5... | collective-permute-start | bytes 3538952 | tf_op jit(solution)/shard_map/ppermute | solution.py:75
  323.7 20.3 %collective-permute-done.45 = bf16[192,3072]{1,0:T(8,128)(2,1)S(1)} collective-permute-done((bf16[192,3072]{1,0:T(8,128)(2,1)}, bf16[192,3072]{1,0:T(8,128)(2,1)S(1)}, u32[]{:S(2)}, u32[]{:S(2)}) %collective-permute-start.45) | collective-permute-done | bytes 1179680 | tf_op jit(solution)/shard_map/ppermute | solution.py:75
  361.0 7.8 cross_forward.1
  384.4 9.2 fusion.100
  396.6 13.4 %collective-permute-done.49 = bf16[192,3072]{1,0:T(8,128)(2,1)S(1)} collective-permute-done((bf16[192,3072]{1,0:T(8,128)(2,1)}, bf16[192,3072]{1,0:T(8,128)(2,1)S(1)}, u32[]{:S(2)}, u32[]{:S(2)}) %collective-permute-start.49) | collective-permute-done | bytes 1179680 | tf_op jit(solution)/shard_map/ppermute | solution.py:75
  416.9 5.7 collective-permute-done.48
  424.9 5.3 collective-permute-done.42
  430.2 16.9 %collective-permute-done.50 = bf16[192,3072]{1,0:T(8,128)(2,1)S(1)} collective-permute-done((bf16[192,3072]{1,0:T(8,128)(2,1)S(1)}, bf16[192,3072]{1,0:T(8,128)(2,1)S(1)}, u32[]{:S(2)}, u32[]{:S(2)}) %collective-permute-start.50) | collective-permute-done | bytes 1179680 | tf_op jit(solution)/shard_map/ppermute | solution.py:39
  449.0 8.1 fusion.8
  457.1 13.2 %multiply_convert_fusion.1 = (bf16[1024,1536]{1,0:T(8,128)(2,1)}, bf16[1024,1536]{1,0:T(8,128)(2,1)}, bf16[1024,1536]{1,0:T(8,128)(2,1)}) fusion(f32[1024,1536]{1,0:T(8,128)} %fusion.100, f32[1024,1536]{1,0:T(8,128)S(1)} %fusion.8, bf16[1024,1536]{1,0:T(8,128)(2,1)S(1)} %bitcast.322, bf16[1536,3072]{1,0:T(8,128)(2,1)} %constant_dynamic-update-slice_fusion.8), kind=kOutput, calls=%fused_computation.14 | convolution fusion | flops 4857004032 | bytes 29884416 | tf_op jit(solution)/shard_map/dot_general | solution.py:21
  470.3 7.3 convolution_convert_fusion.4
  477.7 5.8 convolution_convert_fusion.1
  483.5 15.8 %fusion.14 = bf16[1024,1536]{1,0:T(8,128)(2,1)S(1)} fusion(bf16[1536,3072]{1,0:T(8,128)(2,1)} %constant_dynamic-update-slice_fusion.8, bf16[1024,1536]{1,0:T(8,128)(2,1)} %get-tuple-element.53, bf16[1024,1536]{1,0:T(8,128)(2,1)} %get-tuple-element.51), kind=kOutput, calls=%fused_computation.36 | convolution fusion | flops 9677832192 | bytes 18874368 | tf_op jit(solution)/shard_map/dot_general | solution.py:25
  516.1 10.1 %collective-permute-done.66 = bf16[256,1536]{1,0:T(8,128)(2,1)} collective-permute-done((bf16[256,1536]{1,0:T(8,128)(2,1)}, bf16[256,1536]{1,0:T(8,128)(2,1)}, u32[]{:S(2)}, u32[]{:S(2)}) %collective-permute-start.66) | collective-permute-done | bytes 786464 | tf_op jit(solution)/shard_map/ppermute | solution.py:34
  528.7 13.5 %collective-permute-done.60 = bf16[256,1536]{1,0:T(8,128)(2,1)S(1)} collective-permute-done((bf16[256,1536]{1,0:T(8,128)(2,1)S(1)}, bf16[256,1536]{1,0:T(8,128)(2,1)S(1)}, u32[]{:S(2)}, u32[]{:S(2)}) %collective-permute-start.60) | collective-permute-done | bytes 786464 | tf_op jit(solution)/shard_map/ppermute | solution.py:34
  547.3 10.5 %collective-permute-done.103 = bf16[4,192,1536]{2,1,0:T(8,128)(2,1)} collective-permute-done((bf16[4,192,1536]{2,1,0:T(8,128)(2,1)}, bf16[4,192,1536]{2,1,0:T(8,128)(2,1)}, u32[]{:S(2)}, u32[]{:S(2)}) %collective-permute-start.103) | collective-permute-done | bytes 2359328 | tf_op jit(solution)/shard_map/ppermute | solution.py:39
  562.0 13.6 %convolution_convert_fusion = bf16[1536,3072]{1,0:T(8,128)(2,1)S(1)} fusion(bf16[1024,1536]{1,0:T(8,128)(2,1)} %bitcast.323, bf16[1024,1536]{1,0:T(8,128)(2,1)} %get-tuple-element.53, bf16[1024,1536]{1,0:T(8,128)(2,1)} %get-tuple-element.51), kind=kOutput, calls=%fused_computation | convolution fusion | flops 9680977920 | bytes 18874368 | tf_op jit(solution)/shard_map/dot_general | solution.py:29
  586.7 10.3 %cross_backward.1 = (bf16[4,2,128,384]{3,2,1,0:T(8,128)(2,1)}, bf16[4,2,32,768]{3,2,1,0:T(8,128)(2,1)}) custom-call(f32[2,1,128]{2,1,0:T(1,128)} %compare_convert_fusion.1.ok_ref, bf16[4,2,128,384]{3,2,1,0:T(8,128)(2,1)} %bitcast.373, bf16[4,2,32,768]{3,2,1,0:T(8,128)(2,1)} %bitcast.353, bf16[4,2,32,768]{3,2,1,0:T(8,128)(2,1)} %bitcast.354, ...), custom_call_target="tpu_custom_call" | custom-call | flops 1006632960 | bytes 3145728 | tf_op jit(solution)/shard_map/cross_backward/pallas_call | solution.py:398
  624.8 12.7 %collective-permute-done.106 = bf16[192,1536]{1,0:T(8,128)(2,1)S(1)} collective-permute-done((bf16[192,1536]{1,0:T(8,128)(2,1)S(1)}, bf16[192,1536]{1,0:T(8,128)(2,1)S(1)}, u32[]{:S(2)}, u32[]{:S(2)}) %collective-permute-start.106) | collective-permute-done | bytes 589856 | tf_op jit(solution)/shard_map/ppermute | solution.py:75
  642.8 41.4 %collective-permute-done.99 = bf16[4,192,3072]{2,1,0:T(8,128)(2,1)} collective-permute-done((bf16[4,192,3072]{2,1,0:T(8,128)(2,1)}, bf16[4,192,3072]{2,1,0:T(8,128)(2,1)}, u32[]{:S(2)}, u32[]{:S(2)}) %collective-permute-start.99) | collective-permute-done | bytes 4718624 | tf_op jit(solution)/shard_map/ppermute | solution.py:39
  684.1 5.7 fusion
  693.3 28.1 %collective-permute-done.95 = bf16[4,192,1152]{2,1,0:T(8,128)(2,1)} collective-permute-done((bf16[4,192,1152]{2,1,0:T(8,128)(2,1)}, bf16[4,192,1152]{2,1,0:T(8,128)(2,1)}, u32[]{:S(2)}, u32[]{:S(2)}) %collective-permute-start.95) | collective-permute-done | bytes 1769504 | tf_op jit(solution)/shard_map/ppermute | solution.py:39
  727.2 9.7 collective-permute-done.96
  739.4 6.1 collective-permute-done.74
  753.9 11.8 %collective-permute-done.98 = bf16[192,1152]{1,0:T(8,128)(2,1)S(1)} collective-permute-done((bf16[192,1152]{1,0:T(8,128)(2,1)S(1)}, bf16[192,1152]{1,0:T(8,128)(2,1)S(1)}, u32[]{:S(2)}, u32[]{:S(2)}) %collective-permute-start.98) | collective-permute-done | bytes 442400 | tf_op jit(solution)/shard_map/ppermute | solution.py:75
  777.4 19.8 %self_backward.1 = bf16[4,2,128,1152]{3,2,1,0:T(8,128)(2,1)} custom-call(f32[2,1,512]{2,1,0:T(1,128)} %compare_convert_fusion.ok_ref, f32[4,128,128]{2,1,0:T(8,128)} %concatenate.42.cos_ref, f32[4,128,128]{2,1,0:T(8,128)} %concatenate.43.up_ref, f32[4,128,128]{2,1,0:T(8,128)} %concatenate.44.down_ref, bf16[4,2,128,384]{3,2,1,0:T(8,128)(2,1)} %get-tuple-element.25.q_ref, ...), custom_call_target="tpu_custom_call" | custom-call | flops 4026531840 | bytes 3145728 | tf_op jit(solution)/shard_map/self_backward/pallas_call | solution.py:370
  797.2 7.1 convolution_convert_fusion.7
  807.6 5.0 convolution_convert_fusion.2
  834.1 5.7 collective-permute-done.78
  842.2 47.9 %collective-permute-done.91 = bf16[4,64,3072]{2,1,0:T(8,128)(2,1)} collective-permute-done((bf16[4,64,3072]{2,1,0:T(8,128)(2,1)}, bf16[4,64,3072]{2,1,0:T(8,128)(2,1)}, u32[]{:S(2)}, u32[]{:S(2)}) %collective-permute-start.91) | collective-permute-done | bytes 1572896 | tf_op jit(solution)/shard_map/ppermute | solution.py:39
  902.1 5.1 collective-permute-done.85
  921.9 7.0 collective-permute-done.93
  932.6 10.5 %collective-permute-done.94 = bf16[64,3072]{1,0:T(8,128)(2,1)S(1)} collective-permute-done((bf16[64,3072]{1,0:T(8,128)(2,1)S(1)}, bf16[64,3072]{1,0:T(8,128)(2,1)S(1)}, u32[]{:S(2)}, u32[]{:S(2)}) %collective-permute-start.94) | collective-permute-done | bytes 393248 | tf_op jit(solution)/shard_map/ppermute | solution.py:75
  953.8 5.4 collective-permute-done.90
  (623 shorter events, 413.0 us)
Async XLA Ops:
  7.2 124.9 %collective-permute-start.1 = (bf16[256,1536]{1,0:T(8,128)(2,1)}, bf16[256,1536]{1,0:T(8,128)(2,1)S(1)}, u32[]{:S(2)}, u32[]{:S(2)}) collective-permute-start(bf16[256,1536]{1,0:T(8,128)(2,1)} %bitcast.283), channel_id=1, source_target_pairs={{0,2},{1,3},{2,0},{3,1},{4,6},{5,7},{6,4},{7,5},{8,10},{9,11},{10,... | collective-permute-start | bytes 2359304 | tf_op jit(solution)/shard_map/ppermute | solution.py:34
  10.3 136.5 %collective-permute-start = (bf16[256,1536]{1,0:T(8,128)(2,1)}, bf16[256,1536]{1,0:T(8,128)(2,1)S(1)}, u32[]{:S(2)}, u32[]{:S(2)}) collective-permute-start(bf16[256,1536]{1,0:T(8,128)(2,1)} %bitcast.284), channel_id=1, source_target_pairs={{0,1},{1,0},{2,3},{3,2},{4,5},{5,4},{6,7},{7,6},{8,9},{9,8},{10,11... | collective-permute-start | bytes 2359304 | tf_op jit(solution)/shard_map/ppermute | solution.py:34
  10.3 68.6 %collective-permute-start.36 = (bf16[64,1536]{1,0:T(8,128)(2,1)}, bf16[64,1536]{1,0:T(8,128)(2,1)}, u32[]{:S(2)}, u32[]{:S(2)}) collective-permute-start(bf16[64,1536]{1,0:T(8,128)(2,1)} %bitcast.378), channel_id=1, source_target_pairs={{0,2},{1,3},{2,0},{3,1},{4,6},{5,7},{6,4},{7,5},{8,10},{9,11},{10,... | collective-permute-start | bytes 589832 | tf_op jit(solution)/shard_map/ppermute | solution.py:34
  10.4 90.6 %collective-permute-start.35 = (bf16[64,1536]{1,0:T(8,128)(2,1)}, bf16[64,1536]{1,0:T(8,128)(2,1)}, u32[]{:S(2)}, u32[]{:S(2)}) collective-permute-start(bf16[64,1536]{1,0:T(8,128)(2,1)} %bitcast.379), channel_id=1, source_target_pairs={{0,1},{1,0},{2,3},{3,2},{4,5},{5,4},{6,7},{7,6},{8,9},{9,8},{10,11... | collective-permute-start | bytes 589832 | tf_op jit(solution)/shard_map/ppermute | solution.py:34
  15.2 59.5 %all-to-all-start = ((bf16[4,48,1152]{2,1,0:T(8,128)(2,1)}), bf16[4,48,1152]{2,1,0:T(8,128)(2,1)}, u32[]{:S(2)}, u32[]{:S(2)}) async-start(bf16[4,48,1152]{2,1,0:T(8,128)(2,1)} %pad_maximum_fusion.13), calls=%async_computation | async-start | bytes 884736 | tf_op jit(solution)/shard_map/all_to_all | solution.py:146
  19.5 154.8 %all-gather.4.cloned.1.call-start = ((), (), s32[]{:S(2)}) async-start(), calls=%async_computation.8 | async-start | bytes 1474560 | tf_op jit(solution)/shard_map/all_gather | solution.py:181
  73.0 175.4 %collective-permute-start.62 = (bf16[256,1536]{1,0:T(8,128)(2,1)}, bf16[256,1536]{1,0:T(8,128)(2,1)}, u32[]{:S(2)}, u32[]{:S(2)}) collective-permute-start(bf16[256,1536]{1,0:T(8,128)(2,1)} %bitcast.49), channel_id=1, source_target_pairs={{0,2},{1,3},{2,0},{3,1},{4,6},{5,7},{6,4},{7,5},{8,10},{9,11},{10,... | collective-permute-start | bytes 2359304 | tf_op jit(solution)/shard_map/ppermute | solution.py:34
  139.4 124.6 %collective-permute-start.61 = (bf16[256,1536]{1,0:T(8,128)(2,1)}, bf16[256,1536]{1,0:T(8,128)(2,1)}, u32[]{:S(2)}, u32[]{:S(2)}) collective-permute-start(bf16[256,1536]{1,0:T(8,128)(2,1)} %bitcast.49), channel_id=1, source_target_pairs={{0,1},{1,0},{2,3},{3,2},{4,5},{5,4},{6,7},{7,6},{8,9},{9,8},{10,11... | collective-permute-start | bytes 2359304 | tf_op jit(solution)/shard_map/ppermute | solution.py:34
  144.6 101.7 %collective-permute-start.51 = (bf16[192,1536]{1,0:T(8,128)(2,1)}, bf16[192,1536]{1,0:T(8,128)(2,1)}, u32[]{:S(2)}, u32[]{:S(2)}) collective-permute-start(bf16[192,1536]{1,0:T(8,128)(2,1)} %bitcast.47), channel_id=1, source_target_pairs={{0,4},{4,0},{8,12},{12,8},{16,20},{20,16},{24,28},{28,24},{1,5},{5... | collective-permute-start | bytes 1769480 | tf_op jit(solution)/shard_map/ppermute | solution.py:39
  177.0 29.1 %collective-permute-start.15 = (bf16[64,3072]{1,0:T(8,128)(2,1)S(1)}, bf16[64,3072]{1,0:T(8,128)(2,1)}, u32[]{:S(2)}, u32[]{:S(2)}) collective-permute-start(bf16[64,3072]{1,0:T(8,128)(2,1)S(1)} %get-tuple-element.50), channel_id=1, source_target_pairs={{0,4},{4,0},{8,12},{12,8},{16,20},{20,16},{24,28},{28,24},{1,5},{5... | collective-permute-start | bytes 1179656 | tf_op jit(solution)/shard_map/ppermute | solution.py:39
  249.8 71.2 %collective-permute-start.44 = (bf16[192,3072]{1,0:T(8,128)(2,1)}, bf16[192,3072]{1,0:T(8,128)(2,1)S(1)}, u32[]{:S(2)}, u32[]{:S(2)}) collective-permute-start(bf16[192,3072]{1,0:T(8,128)(2,1)} %bitcast.45), channel_id=1, source_target_pairs={{0,4},{4,0},{8,12},{12,8},{16,20},{20,16},{24,28},{28,24},{1,5},{5... | collective-permute-start | bytes 3538952 | tf_op jit(solution)/shard_map/ppermute | solution.py:39
  262.7 27.8 %collective-permute-start.53 = (bf16[192,1536]{1,0:T(8,128)(2,1)S(1)}, bf16[192,1536]{1,0:T(8,128)(2,1)S(1)}, u32[]{:S(2)}, u32[]{:S(2)}) collective-permute-start(bf16[192,1536]{1,0:T(8,128)(2,1)S(1)} %collective-permute-done.52), channel_id=1, source_target_pairs={{0,4},{4,0},{8,12},{12,8},{16,20},{20,16},{24,28},{28,24},{1,5},{5... | collective-permute-start | bytes 1769480 | tf_op jit(solution)/shard_map/ppermute | solution.py:39
  263.8 27.9 %collective-permute-start.54 = (bf16[192,1536]{1,0:T(8,128)(2,1)S(1)}, bf16[192,1536]{1,0:T(8,128)(2,1)}, u32[]{:S(2)}, u32[]{:S(2)}) collective-permute-start(bf16[192,1536]{1,0:T(8,128)(2,1)S(1)} %collective-permute-done.52), channel_id=1, source_target_pairs={{0,8},{4,12},{8,16},{12,20},{16,24},{20,28},{24,0},{28,4},{1,9},{5... | collective-permute-start | bytes 1769480 | tf_op jit(solution)/shard_map/ppermute | solution.py:75
  264.1 51.5 %collective-permute-start.22 = (bf16[256,1536]{1,0:T(8,128)(2,1)S(1)}, bf16[256,1536]{1,0:T(8,128)(2,1)S(1)}, u32[]{:S(2)}, u32[]{:S(2)}) collective-permute-start(bf16[256,1536]{1,0:T(8,128)(2,1)S(1)} %get-tuple-element.64), channel_id=1, source_target_pairs={{0,1},{1,0},{2,3},{3,2},{4,5},{5,4},{6,7},{7,6},{8,9},{9,8},{10,11... | collective-permute-start | bytes 2359304 | tf_op jit(solution)/shard_map/ppermute | solution.py:34
  264.2 53.2 %collective-permute-start.24 = (bf16[256,1536]{1,0:T(8,128)(2,1)S(1)}, bf16[256,1536]{1,0:T(8,128)(2,1)S(1)}, u32[]{:S(2)}, u32[]{:S(2)}) collective-permute-start(bf16[256,1536]{1,0:T(8,128)(2,1)S(1)} %add_convert_fusion.6), channel_id=1, source_target_pairs={{0,2},{1,3},{2,0},{3,1},{4,6},{5,7},{6,4},{7,5},{8,10},{9,11},{10,... | collective-permute-start | bytes 2359304 | tf_op jit(solution)/shard_map/ppermute | solution.py:34
  301.8 42.3 %collective-permute-start.45 = (bf16[192,3072]{1,0:T(8,128)(2,1)}, bf16[192,3072]{1,0:T(8,128)(2,1)S(1)}, u32[]{:S(2)}, u32[]{:S(2)}) collective-permute-start(bf16[192,3072]{1,0:T(8,128)(2,1)} %bitcast.45), channel_id=1, source_target_pairs={{0,8},{4,12},{8,16},{12,20},{16,24},{20,28},{24,0},{28,4},{1,9},{5... | collective-permute-start | bytes 3538952 | tf_op jit(solution)/shard_map/ppermute | solution.py:75
  315.3 58.2 %collective-permute-start.55 = (bf16[192,1536]{1,0:T(8,128)(2,1)}, bf16[192,1536]{1,0:T(8,128)(2,1)}, u32[]{:S(2)}, u32[]{:S(2)}) collective-permute-start(bf16[192,1536]{1,0:T(8,128)(2,1)} %collective-permute-done.54), channel_id=1, source_target_pairs={{0,4},{4,0},{8,12},{12,8},{16,20},{20,16},{24,28},{28,24},{1,5},{5... | collective-permute-start | bytes 1769480 | tf_op jit(solution)/shard_map/ppermute | solution.py:39
  315.6 29.8 %collective-permute-start.34 = (bf16[192,1152]{1,0:T(8,128)(2,1)S(1)}, bf16[192,1152]{1,0:T(8,128)(2,1)S(1)}, u32[]{:S(2)}, u32[]{:S(2)}) collective-permute-start(bf16[192,1152]{1,0:T(8,128)(2,1)S(1)} %collective-permute-done.33), channel_id=1, source_target_pairs={{0,4},{4,0},{8,12},{12,8},{16,20},{20,16},{24,28},{28,24},{1,5},{5... | collective-permute-start | bytes 1327112 | tf_op jit(solution)/shard_map/ppermute | solution.py:39
  318.5 27.8 %collective-permute-start.26 = (bf16[256,1536]{1,0:T(8,128)(2,1)S(1)}, bf16[256,1536]{1,0:T(8,128)(2,1)S(1)}, u32[]{:S(2)}, u32[]{:S(2)}) collective-permute-start(bf16[256,1536]{1,0:T(8,128)(2,1)S(1)} %multiply_convert_fusion.6), channel_id=1, source_target_pairs={{0,2},{1,3},{2,0},{3,1},{4,6},{5,7},{6,4},{7,5},{8,10},{9,11},{10,... | collective-permute-start | bytes 2359304 | tf_op jit(solution)/shard_map/ppermute | solution.py:34
  321.0 33.6 %collective-permute-start.56 = (bf16[192,1536]{1,0:T(8,128)(2,1)}, bf16[192,1536]{1,0:T(8,128)(2,1)}, u32[]{:S(2)}, u32[]{:S(2)}) collective-permute-start(bf16[192,1536]{1,0:T(8,128)(2,1)} %collective-permute-done.54), channel_id=1, source_target_pairs={{0,8},{4,12},{8,16},{12,20},{16,24},{20,28},{24,0},{28,4},{1,9},{5... | collective-permute-start | bytes 1769480 | tf_op jit(solution)/shard_map/ppermute | solution.py:75
  344.0 50.2 %collective-permute-start.46 = (bf16[192,3072]{1,0:T(8,128)(2,1)S(1)}, bf16[192,3072]{1,0:T(8,128)(2,1)}, u32[]{:S(2)}, u32[]{:S(2)}) collective-permute-start(bf16[192,3072]{1,0:T(8,128)(2,1)S(1)} %collective-permute-done.45), channel_id=1, source_target_pairs={{0,4},{4,0},{8,12},{12,8},{16,20},{20,16},{24,28},{28,24},{1,5},{5... | collective-permute-start | bytes 3538952 | tf_op jit(solution)/shard_map/ppermute | solution.py:39
  354.7 27.8 %collective-permute-start.47 = (bf16[192,3072]{1,0:T(8,128)(2,1)S(1)}, bf16[192,3072]{1,0:T(8,128)(2,1)}, u32[]{:S(2)}, u32[]{:S(2)}) collective-permute-start(bf16[192,3072]{1,0:T(8,128)(2,1)S(1)} %collective-permute-done.45), channel_id=1, source_target_pairs={{0,8},{4,12},{8,16},{12,20},{16,24},{20,28},{24,0},{28,4},{1,9},{5... | collective-permute-start | bytes 3538952 | tf_op jit(solution)/shard_map/ppermute | solution.py:75
  382.5 27.5 %collective-permute-start.49 = (bf16[192,3072]{1,0:T(8,128)(2,1)}, bf16[192,3072]{1,0:T(8,128)(2,1)S(1)}, u32[]{:S(2)}, u32[]{:S(2)}) collective-permute-start(bf16[192,3072]{1,0:T(8,128)(2,1)} %collective-permute-done.47), channel_id=1, source_target_pairs={{0,8},{4,12},{8,16},{12,20},{16,24},{20,28},{24,0},{28,4},{1,9},{5... | collective-permute-start | bytes 3538952 | tf_op jit(solution)/shard_map/ppermute | solution.py:75
  382.5 29.3 %collective-permute-start.38 = (bf16[256,1536]{1,0:T(8,128)(2,1)S(1)}, bf16[256,1536]{1,0:T(8,128)(2,1)S(1)}, u32[]{:S(2)}, u32[]{:S(2)}) collective-permute-start(bf16[256,1536]{1,0:T(8,128)(2,1)S(1)} %get-tuple-element.62), channel_id=1, source_target_pairs={{0,1},{1,0},{2,3},{3,2},{4,5},{5,4},{6,7},{7,6},{8,9},{9,8},{10,11... | collective-permute-start | bytes 2359304 | tf_op jit(solution)/shard_map/ppermute | solution.py:34
  382.7 29.0 %collective-permute-start.40 = (bf16[256,1536]{1,0:T(8,128)(2,1)S(1)}, bf16[256,1536]{1,0:T(8,128)(2,1)S(1)}, u32[]{:S(2)}, u32[]{:S(2)}) collective-permute-start(bf16[256,1536]{1,0:T(8,128)(2,1)S(1)} %add_convert_fusion.5), channel_id=1, source_target_pairs={{0,2},{1,3},{2,0},{3,1},{4,6},{5,7},{6,4},{7,5},{8,10},{9,11},{10,... | collective-permute-start | bytes 2359304 | tf_op jit(solution)/shard_map/ppermute | solution.py:34
  393.6 29.0 %collective-permute-start.48 = (bf16[192,3072]{1,0:T(8,128)(2,1)}, bf16[192,3072]{1,0:T(8,128)(2,1)S(1)}, u32[]{:S(2)}, u32[]{:S(2)}) collective-permute-start(bf16[192,3072]{1,0:T(8,128)(2,1)} %collective-permute-done.47), channel_id=1, source_target_pairs={{0,4},{4,0},{8,12},{12,8},{16,20},{20,16},{24,28},{28,24},{1,5},{5... | collective-permute-start | bytes 3538952 | tf_op jit(solution)/shard_map/ppermute | solution.py:39
  410.0 37.1 %collective-permute-start.50 = (bf16[192,3072]{1,0:T(8,128)(2,1)S(1)}, bf16[192,3072]{1,0:T(8,128)(2,1)S(1)}, u32[]{:S(2)}, u32[]{:S(2)}) collective-permute-start(bf16[192,3072]{1,0:T(8,128)(2,1)S(1)} %collective-permute-done.49), channel_id=1, source_target_pairs={{0,4},{4,0},{8,12},{12,8},{16,20},{20,16},{24,28},{28,24},{1,5},{5... | collective-permute-start | bytes 3538952 | tf_op jit(solution)/shard_map/ppermute | solution.py:39
  503.9 54.0 %collective-permute-start.103 = (bf16[4,192,1536]{2,1,0:T(8,128)(2,1)}, bf16[4,192,1536]{2,1,0:T(8,128)(2,1)}, u32[]{:S(2)}, u32[]{:S(2)}) collective-permute-start(bf16[4,192,1536]{2,1,0:T(8,128)(2,1)} %dynamic-slice_bitcast_fusion.1), channel_id=1, source_target_pairs={{0,4},{4,0},{8,12},{12,8},{16,20},{20,16},{24,28},{28,24},{1,5},{5... | collective-permute-start | bytes 7077896 | tf_op jit(solution)/shard_map/ppermute | solution.py:39
  514.4 27.8 %collective-permute-start.60 = (bf16[256,1536]{1,0:T(8,128)(2,1)S(1)}, bf16[256,1536]{1,0:T(8,128)(2,1)S(1)}, u32[]{:S(2)}, u32[]{:S(2)}) collective-permute-start(bf16[256,1536]{1,0:T(8,128)(2,1)S(1)} %add_convert_fusion.4), channel_id=1, source_target_pairs={{0,2},{1,3},{2,0},{3,1},{4,6},{5,7},{6,4},{7,5},{8,10},{9,11},{10,... | collective-permute-start | bytes 2359304 | tf_op jit(solution)/shard_map/ppermute | solution.py:34
  546.9 28.7 %collective-permute-start.68 = (bf16[256,1536]{1,0:T(8,128)(2,1)S(1)}, bf16[256,1536]{1,0:T(8,128)(2,1)S(1)}, u32[]{:S(2)}, u32[]{:S(2)}) collective-permute-start(bf16[256,1536]{1,0:T(8,128)(2,1)S(1)} %get-tuple-element.43), channel_id=1, source_target_pairs={{0,2},{1,3},{2,0},{3,1},{4,6},{5,7},{6,4},{7,5},{8,10},{9,11},{10,... | collective-permute-start | bytes 2359304 | tf_op jit(solution)/shard_map/ppermute | solution.py:34
  579.1 105.0 %collective-permute-start.99 = (bf16[4,192,3072]{2,1,0:T(8,128)(2,1)}, bf16[4,192,3072]{2,1,0:T(8,128)(2,1)}, u32[]{:S(2)}, u32[]{:S(2)}) collective-permute-start(bf16[4,192,3072]{2,1,0:T(8,128)(2,1)} %dynamic-slice_bitcast_fusion), channel_id=1, source_target_pairs={{0,4},{4,0},{8,12},{12,8},{16,20},{20,16},{24,28},{28,24},{1,5},{5... | collective-permute-start | bytes 14155784 | tf_op jit(solution)/shard_map/ppermute | solution.py:39
  579.8 33.6 %collective-permute-start.105 = (bf16[192,1536]{1,0:T(8,128)(2,1)S(1)}, bf16[192,1536]{1,0:T(8,128)(2,1)S(1)}, u32[]{:S(2)}, u32[]{:S(2)}) collective-permute-start(bf16[192,1536]{1,0:T(8,128)(2,1)S(1)} %fusion.57), channel_id=1, source_target_pairs={{0,8},{4,12},{8,16},{12,20},{16,24},{20,28},{24,0},{28,4},{1,9},{5... | collective-permute-start | bytes 1769480 | tf_op jit(solution)/shard_map/ppermute | solution.py:75
  601.4 90.7 %collective-permute-start.70 = (bf16[256,1536]{1,0:T(8,128)(2,1)}, bf16[256,1536]{1,0:T(8,128)(2,1)S(1)}, u32[]{:S(2)}, u32[]{:S(2)}) collective-permute-start(bf16[256,1536]{1,0:T(8,128)(2,1)} %get-tuple-element.56), channel_id=1, source_target_pairs={{0,1},{1,0},{2,3},{3,2},{4,5},{5,4},{6,7},{7,6},{8,9},{9,8},{10,11... | collective-permute-start | bytes 2359304 | tf_op jit(solution)/shard_map/ppermute | solution.py:34
  614.8 106.6 %collective-permute-start.95 = (bf16[4,192,1152]{2,1,0:T(8,128)(2,1)}, bf16[4,192,1152]{2,1,0:T(8,128)(2,1)}, u32[]{:S(2)}, u32[]{:S(2)}) collective-permute-start(bf16[4,192,1152]{2,1,0:T(8,128)(2,1)} %fusion.38), channel_id=1, source_target_pairs={{0,4},{4,0},{8,12},{12,8},{16,20},{20,16},{24,28},{28,24},{1,5},{5... | collective-permute-start | bytes 5308424 | tf_op jit(solution)/shard_map/ppermute | solution.py:39
  624.4 67.7 %collective-permute-start.72 = (bf16[256,1536]{1,0:T(8,128)(2,1)}, bf16[256,1536]{1,0:T(8,128)(2,1)S(1)}, u32[]{:S(2)}, u32[]{:S(2)}) collective-permute-start(bf16[256,1536]{1,0:T(8,128)(2,1)} %add_convert_fusion.1), channel_id=1, source_target_pairs={{0,2},{1,3},{2,0},{3,1},{4,6},{5,7},{6,4},{7,5},{8,10},{9,11},{10,... | collective-permute-start | bytes 2359304 | tf_op jit(solution)/shard_map/ppermute | solution.py:34
  638.6 98.5 %all-to-all-start.7 = ((bf16[4,48,1536]{2,1,0:T(8,128)(2,1)}), bf16[4,48,1536]{2,1,0:T(8,128)(2,1)}, u32[]{:S(2)}, u32[]{:S(2)}) async-start(bf16[4,48,1536]{2,1,0:T(8,128)(2,1)} %bitcast.338), calls=%async_computation.7 | async-start | bytes 1179648 | tf_op jit(solution)/shard_map/all_to_all | solution.py:152
  691.0 59.8 %collective-permute-start.100 = (bf16[192,3072]{1,0:T(8,128)(2,1)}, bf16[192,3072]{1,0:T(8,128)(2,1)}, u32[]{:S(2)}, u32[]{:S(2)}) collective-permute-start(bf16[192,3072]{1,0:T(8,128)(2,1)} %dynamic-slice_bitcast_fusion.4), channel_id=1, source_target_pairs={{0,8},{4,12},{8,16},{12,20},{16,24},{20,28},{24,0},{28,4},{1,9},{5... | collective-permute-start | bytes 3538952 | tf_op jit(solution)/shard_map/ppermute | solution.py:75
  739.4 30.6 %collective-permute-start.73 = (bf16[256,1536]{1,0:T(8,128)(2,1)}, bf16[256,1536]{1,0:T(8,128)(2,1)}, u32[]{:S(2)}, u32[]{:S(2)}) collective-permute-start(bf16[256,1536]{1,0:T(8,128)(2,1)} %get-tuple-element.41), channel_id=1, source_target_pairs={{0,1},{1,0},{2,3},{3,2},{4,5},{5,4},{6,7},{7,6},{8,9},{9,8},{10,11... | collective-permute-start | bytes 2359304 | tf_op jit(solution)/shard_map/ppermute | solution.py:34
  753.9 78.0 %collective-permute-start.101 = (bf16[192,3072]{1,0:T(8,128)(2,1)}, bf16[192,3072]{1,0:T(8,128)(2,1)}, u32[]{:S(2)}, u32[]{:S(2)}) collective-permute-start(bf16[192,3072]{1,0:T(8,128)(2,1)} %fusion.33), channel_id=1, source_target_pairs={{0,8},{4,12},{8,16},{12,20},{16,24},{20,28},{24,0},{28,4},{1,9},{5... | collective-permute-start | bytes 3538952 | tf_op jit(solution)/shard_map/ppermute | solution.py:75
  766.6 55.7 %all-to-all-start.5 = ((bf16[4,48,1152]{2,1,0:T(8,128)(2,1)}), bf16[4,48,1152]{2,1,0:T(8,128)(2,1)S(1)}, u32[]{:S(2)}, u32[]{:S(2)}) async-start(bf16[4,48,1152]{2,1,0:T(8,128)(2,1)} %bitcast.122), calls=%async_computation.5 | async-start | bytes 884736 | tf_op jit(solution)/shard_map/all_to_all | solution.py:152
  805.8 28.3 %collective-permute-start.76 = (bf16[256,1536]{1,0:T(8,128)(2,1)}, bf16[256,1536]{1,0:T(8,128)(2,1)S(1)}, u32[]{:S(2)}, u32[]{:S(2)}) collective-permute-start(bf16[256,1536]{1,0:T(8,128)(2,1)} %get-tuple-element.54), channel_id=1, source_target_pairs={{0,1},{1,0},{2,3},{3,2},{4,5},{5,4},{6,7},{7,6},{8,9},{9,8},{10,11... | collective-permute-start | bytes 2359304 | tf_op jit(solution)/shard_map/ppermute | solution.py:34
  815.1 92.1 %collective-permute-start.87 = (bf16[4,192,1152]{2,1,0:T(8,128)(2,1)}, bf16[4,192,1152]{2,1,0:T(8,128)(2,1)}, u32[]{:S(2)}, u32[]{:S(2)}) collective-permute-start(bf16[4,192,1152]{2,1,0:T(8,128)(2,1)} %dynamic-slice_bitcast_fusion.2), channel_id=1, source_target_pairs={{0,4},{4,0},{8,12},{12,8},{16,20},{20,16},{24,28},{28,24},{1,5},{5... | collective-permute-start | bytes 5308424 | tf_op jit(solution)/shard_map/ppermute | solution.py:39
  817.6 72.5 %collective-permute-start.91 = (bf16[4,64,3072]{2,1,0:T(8,128)(2,1)}, bf16[4,64,3072]{2,1,0:T(8,128)(2,1)}, u32[]{:S(2)}, u32[]{:S(2)}) collective-permute-start(bf16[4,64,3072]{2,1,0:T(8,128)(2,1)} %dynamic-slice_bitcast_fusion.3), channel_id=1, source_target_pairs={{0,4},{4,0},{8,12},{12,8},{16,20},{20,16},{24,28},{28,24},{1,5},{5... | collective-permute-start | bytes 4718600 | tf_op jit(solution)/shard_map/ppermute | solution.py:39
  834.0 80.9 %collective-permute-start.102 = (bf16[192,3072]{1,0:T(8,128)(2,1)S(1)}, bf16[192,3072]{1,0:T(8,128)(2,1)S(1)}, u32[]{:S(2)}, u32[]{:S(2)}) collective-permute-start(bf16[192,3072]{1,0:T(8,128)(2,1)S(1)} %fusion.32), channel_id=1, source_target_pairs={{0,8},{4,12},{8,16},{12,20},{16,24},{20,28},{24,0},{28,4},{1,9},{5... | collective-permute-start | bytes 3538952 | tf_op jit(solution)/shard_map/ppermute | solution.py:75
  842.1 50.0 %collective-permute-start.82 = (f32[3,1536]{1,0:T(4,128)S(1)}, f32[3,1536]{1,0:T(4,128)S(1)}, u32[]{:S(2)}, u32[]{:S(2)}) collective-permute-start(f32[3,1536]{1,0:T(4,128)S(1)} %pad_maximum_fusion.16), channel_id=1, source_target_pairs={{0,1},{1,0},{2,3},{3,2},{4,5},{5,4},{6,7},{7,6},{8,9},{9,8},{10,11... | collective-permute-start | bytes 55304 | tf_op jit(solution)/shard_map/ppermute | solution.py:34
  907.1 46.0 %collective-permute-start.86 = (f32[3,1536]{1,0:T(4,128)S(1)}, f32[3,1536]{1,0:T(4,128)S(1)}, u32[]{:S(2)}, u32[]{:S(2)}) collective-permute-start(f32[3,1536]{1,0:T(4,128)S(1)} %add.878), channel_id=1, source_target_pairs={{0,16},{4,20},{8,24},{12,28},{16,0},{20,4},{24,8},{28,12},{1,17},{... | collective-permute-start | bytes 55304 | tf_op jit(solution)/shard_map/ppermute | solution.py:39
  917.6 42.5 %all-to-all-start.6 = ((bf16[4,48,3072]{2,1,0:T(8,128)(2,1)}), bf16[4,48,3072]{2,1,0:T(8,128)(2,1)}, u32[]{:S(2)}, u32[]{:S(2)}) async-start(bf16[4,48,3072]{2,1,0:T(8,128)(2,1)} %bitcast.312), calls=%async_computation.6 | async-start | bytes 2359296 | tf_op jit(solution)/shard_map/all_to_all | solution.py:152
  921.9 54.7 %all-gather.6.cloned.1.call-start = ((), (), s32[]{:S(2)}) async-start(), calls=%async_computation.9 | async-start | bytes 1966080 | tf_op jit(solution)/shard_map/all_gather | solution.py:208
  (157 other events, 2670.9 us)
Sparse Core Ops, SparseCore 0:
  23.9 20.8 all-gather.3
  945.1 17.0 all-gather.5

commit v2 on v1

--- a/solution.py
+++ b/solution.py
@@ -63,6 +63,41 @@
     return near + arrived.astype(F32)
 
 
+def x_swap(x):
+    return dp_swap(x, 1)
+
+
+def gather_eight(x):
+    half = x.shape[0] // 2
+    far = seq_swap(x, 2)
+    side = x_swap(x)
+    corner = jnp.concatenate([x_swap(far[:half]), seq_swap(side[half:], 2)])
+    blocks = []
+    for near in (x, far, side, corner):
+        blocks += [near, seq_swap(near, 1)]
+    return jnp.stack(blocks)
+
+
+def scatter_eight(partial):
+    half = partial.shape[1] // 2
+
+    def with_core(k):
+        return partial[k].astype(F32) + seq_swap(partial[k + 1], 1).astype(F32)
+
+    corner = with_core(6).astype(BF)
+    from_x, from_y = x_swap(corner[:half]), seq_swap(corner[half:], 2)
+    far = with_core(2)
+    far = jnp.concatenate([far[:half] + from_x.astype(F32), far[half:]]).astype(BF)
+    side = with_core(4)
+    side = jnp.concatenate([side[:half], side[half:] + from_y.astype(F32)]).astype(BF)
+    from_y, from_x = seq_swap(far, 2), x_swap(side)
+    return with_core(0) + from_y.astype(F32) + from_x.astype(F32)
+
+
+def together(*values):
+    return lax.optimization_barrier(values)
+
+
 RING_Z, RING_X = 4, 2
 
 
@@ -70,55 +105,101 @@
     return lax.axis_size("dp") == RING_Z * RING_X
 
 
-def z_next(x):
-    n = lax.axis_size("dp")
-    return lax.ppermute(x, "dp", [(i, (i + RING_X) % n) for i in range(n)])
-
-
-def ring_pieces(x):
-    d = lax.axis_index("dp")
-    z, xx = d // RING_X, d % RING_X
-    held = x
-    for k in range(RING_Z):
-        zk = (z + RING_Z - k) % RING_Z
-        yield zk * RING_X + xx, held
-        yield zk * RING_X + 1 - xx, dp_swap(held, 1)
-        if k < RING_Z - 1:
-            held = z_next(held)
+def z_groups():
+    return [[z * RING_X + x for z in range(RING_Z)] for x in range(RING_X)]
+
+
+def gather_z(chunk):
+    return lax.all_gather(chunk, "dp", axis=0, axis_index_groups=z_groups())
 
 
 def gather_dp(chunk):
     if not ringed():
         return lax.all_gather(chunk, "dp", axis=0, tiled=True)
     rows, cols = chunk.shape
-    out = jnp.zeros((rows * lax.axis_size("dp"), cols), chunk.dtype)
-    for index, piece in ring_pieces(chunk):
-        out = lax.dynamic_update_slice(out, piece, (index * rows, 0))
-    return out
+    first = lax.axis_index("dp") % RING_X == 0
+    own = gather_z(chunk)
+    other = dp_swap(own, 1)
+    both = jnp.stack([jnp.where(first, own, other), jnp.where(first, other, own)], axis=1)
+    return both.reshape(-1, cols)
 
 
 def reduce_dp(slots):
+    n, rows, cols = slots.shape
     if not ringed():
-        n, rows, cols = slots.shape
         return lax.psum_scatter(
             slots.reshape(n * rows, cols), "dp", scatter_dimension=0, tiled=True
-        ).astype(F32)
-    d = lax.axis_index("dp")
-    z, xx = d // RING_X, d % RING_X
-    n, rows, cols = slots.shape
+        )
+    xx = lax.axis_index("dp") % RING_X
     split = slots.reshape(RING_Z, RING_X, rows, cols)
     away = lax.dynamic_index_in_dim(split, 1 - xx, axis=1, keepdims=False)
     kept = lax.dynamic_index_in_dim(split, xx, axis=1, keepdims=False)
     arrived = dp_swap(away, 1)
     both = (kept.astype(F32) + arrived.astype(F32)).astype(BF)
-
-    def at(k):
-        return lax.dynamic_index_in_dim(both, (z + RING_Z - k) % RING_Z, axis=0, keepdims=False)
-
-    total = at(1)
-    for k in range(2, RING_Z + 1):
-        total = z_next(total.astype(BF)).astype(F32) + at(k).astype(F32)
-    return total
+    return lax.psum_scatter(
+        both.reshape(RING_Z * rows, cols),
+        "dp",
+        scatter_dimension=0,
+        tiled=True,
+        axis_index_groups=z_groups(),
+    )
+
+
+def wide():
+    return lax.axis_size("seq") * (RING_X if ringed() else 1)
+
+
+def hidden_out(mats):
+    n = lax.axis_size("seq")
+    parts = wide() // n
+    rows = mats[0].shape[0]
+    cut = [m.reshape(rows, n, parts, -1) for m in mats]
+    return jnp.concatenate(cut, axis=3).transpose(1, 0, 2, 3).reshape(n, rows, -1)
+
+
+def deal_hidden(x):
+    got = deal(x)
+    if not ringed():
+        return got
+    rows = got.shape[0]
+    xx = lax.axis_index("dp") % RING_X
+    cut = got.reshape(rows, RING_X, -1)
+    kept = lax.dynamic_index_in_dim(cut, xx, 1, keepdims=False)
+    arrived = x_swap(lax.dynamic_index_in_dim(cut, 1 - xx, 1, keepdims=False))
+    first = xx == 0
+    return jnp.concatenate([jnp.where(first, kept, arrived), jnp.where(first, arrived, kept)])
+
+
+def gather_hidden(x):
+    if not ringed():
+        return lax.all_gather(x, "dp", axis=0, tiled=True)
+    return lax.all_gather(x, "dp", axis=0, tiled=True, axis_index_groups=z_groups())
+
+
+def reduce_hidden(grad):
+    if not ringed():
+        return lax.psum_scatter(grad, "dp", scatter_dimension=0, tiled=True)
+    return lax.psum_scatter(
+        grad, "dp", scatter_dimension=0, tiled=True, axis_index_groups=z_groups()
+    )
+
+
+def collect_hidden(x, count):
+    n = lax.axis_size("seq")
+    parts = wide() // n
+    if ringed():
+        xx = lax.axis_index("dp") % RING_X
+        cut = x.reshape(RING_X, -1, x.shape[1])
+        kept = lax.dynamic_index_in_dim(cut, xx, 0, keepdims=False)
+        arrived = x_swap(lax.dynamic_index_in_dim(cut, 1 - xx, 0, keepdims=False))
+        first = xx == 0
+        x = jnp.concatenate(
+            [jnp.where(first, kept, arrived), jnp.where(first, arrived, kept)], axis=1
+        )
+    got = collect(x)
+    rows = got.shape[1]
+    got = got.reshape(n, rows, parts, count, -1)
+    return [got[:, :, :, i].transpose(1, 0, 2, 3).reshape(rows, -1) for i in range(count)]
 
 
 def columns_out(x):
@@ -130,16 +211,6 @@
 def columns_back(x):
     n, rows, _ = x.shape
     return x.reshape(n, rows, HEADS // n, HEAD).transpose(1, 2, 0, 3).reshape(rows, HEADS * HEAD)
-
-
-def blocks_out(x):
-    rows = x.shape[0]
-    n = lax.axis_size("seq")
-    return x.reshape(rows, n, -1).transpose(1, 0, 2)
-
-
-def blocks_back(x):
-    return x.transpose(1, 0, 2).reshape(x.shape[1], -1)
 
 
 def deal(x):
@@ -183,8 +254,13 @@
     rows = jnp.concatenate([rows, jnp.zeros((HEAD, cols), x.dtype)])
     piece = lax.dynamic_slice(rows, (j * HEAD, 0), (HEAD, cols))
     out = jnp.zeros(((mine + 1) * HEAD, cols), x.dtype)
-    for index, held in ring_pieces(piece):
-        out = lax.dynamic_update_slice(out, held, (slot_place(index) * HEAD, 0))
+    own = gather_z(piece)
+    other = dp_swap(own, 1)
+    xx = lax.axis_index("dp") % RING_X
+    for z in range(RING_Z):
+        for held, x_of in ((own, xx), (other, 1 - xx)):
+            place = slot_place(z * RING_X + x_of) * HEAD
+            out = lax.dynamic_update_slice(out, held[z], (place, 0))
     return out[: mine * HEAD]
 
 
@@ -204,7 +280,7 @@
     slots = jnp.stack(
         [lax.dynamic_slice(padded, (slot_place(d) * HEAD, 0), (HEAD, cols)) for d in range(size)]
     )
-    own = reduce_dp(slots).astype(BF)
+    own = reduce_dp(slots)
     pieces = lax.all_gather(own, "seq", axis=0, tiled=False)
     per = HEADS // size
     d = lax.axis_index("dp")
@@ -473,15 +549,20 @@
         deal(jnp.concatenate([columns_out(w) for w in (c_query, c_key, c_value)], axis=2))
     )
     cq_w, ckv_w = cross_w[:, :mine], cross_w[:, mine:]
-    gu_w = gather_dp(deal(jnp.concatenate([blocks_out(w_gate), blocks_out(w_up)], axis=2)))
-    down_w = gather_dp(deal(blocks_out(w_down)))
-    hid = down_w.shape[1]
+    ffn_w = deal_hidden(hidden_out([w_gate, w_up, w_down]))
+    hid = w_gate.shape[1] // wide()
+    gu_w = gather_hidden(ffn_w[:, : 2 * hid])
+    down_w = gather_hidden(ffn_w[:, 2 * hid :])
+    gather_ffn, scatter_ffn = (
+        (gather_eight, scatter_eight) if ringed() else (gather_seq, scatter_seq)
+    )
+    shared = wide()
 
     tokens = inputs.reshape(rows, width)
     incoming = cotangent.reshape(rows, width)
     tokens_all = gather_seq(tokens)
     cond_all = gather_seq(conditioning.reshape(batch * cond_dev, width)).reshape(-1, width)
-    incoming_all = gather_seq(incoming).reshape(total, width)
+    incoming_all = gather_ffn(incoming).reshape(shared * rows, width)
 
     normed_one = norm_forward(tokens_all.reshape(total, width).astype(F32), gain_one)[2]
     qkv = mm(normed_one, qkv_w).reshape(n, batch, tokens_dev, 3 * mine)
@@ -497,21 +578,23 @@
     partial = mm(cross_att, c_out).astype(BF).reshape(n, rows, width)
     after_cross = after_self + scatter_seq(partial)
     normal_three, inv_three, own_three = norm_forward(after_cross, gain_three)
-    normed_three = gather_seq(own_three).reshape(total, width)
+    normed_three = gather_ffn(own_three).reshape(shared * rows, width)
     gate = mm(normed_three, gu_w[:, :hid])
     up = mm(normed_three, gu_w[:, hid:])
     sig = jax.nn.sigmoid(gate)
     hidden = (gate * sig * up).astype(BF)
-    partial = mm_t(hidden, down_w).astype(BF).reshape(n, rows, width)
-    block = (after_cross + scatter_seq(partial)).astype(BF)
-    d_down = t_mm(incoming_all, hidden).astype(BF)
+    grad_down = t_mm(incoming_all, hidden).astype(BF)
+    incoming_all, grad_down = together(incoming_all, grad_down)
     d_hidden = mm(incoming_all, down_w)
     d_gate = (d_hidden * up * sig * (1.0 + gate * (1.0 - sig))).astype(BF)
     d_up = (d_hidden * gate * sig).astype(BF)
     d_gu = jnp.concatenate([d_gate, d_up], axis=1)
-    partial = mm_t(d_gu, gu_w).astype(BF).reshape(n, rows, width)
-    d_norm3 = scatter_seq(partial)
+    partial = mm_t(d_gu, gu_w).astype(BF).reshape(shared, rows, width)
+    d_norm3 = scatter_ffn(partial)
     grad_gu = t_mm(normed_three, d_gu).astype(BF)
+    d_norm3, grad_gu = together(d_norm3, grad_gu)
+    partial = mm_t(hidden, down_w).astype(BF).reshape(shared, rows, width)
+    block = (after_cross + scatter_ffn(partial)).astype(BF)
     back, gain_grad_three = norm_backward(d_norm3, normal_three, inv_three, gain_three)
     d_after_cross = incoming.astype(F32) + back
     dc_low = gather_seq(d_after_cross.astype(BF)).reshape(total, width)
@@ -522,28 +605,31 @@
     d_ckv = d_ckv.reshape(n * batch * cond_dev, 2 * mine)
     partial = mm_t(d_cq, cq_w).astype(BF).reshape(n, rows, width)
     d_norm2 = scatter_seq(partial)
+    grad_cross = jnp.concatenate([t_mm(normed_two, d_cq), t_mm(cond_all, d_ckv)], axis=1).astype(BF)
+    d_norm2, grad_cross = together(d_norm2, grad_cross)
     partial = mm_t(d_ckv, ckv_w).astype(BF).reshape(n, batch * cond_dev, width)
     grad_cond = scatter_seq(partial)
-    grad_cross = jnp.concatenate([t_mm(normed_two, d_cq), t_mm(cond_all, d_ckv)], axis=1).astype(BF)
     back, gain_grad_two = norm_backward(d_norm2, normal_two, inv_two, gain_two)
     d_after_self = d_after_cross + back
     ds_low = gather_seq(d_after_self.astype(BF)).reshape(total, width)
+    ds_low, grad_c_out = together(ds_low, grad_c_out)
     d_att = mm_t(ds_low, w_out).astype(BF).reshape(n, batch, tokens_dev, mine)
     grad_out = t_mm(attended, ds_low).astype(BF)
     d_qkv = self_backward(key_ok, tables, q_rot, k_rot, v_low, d_att).reshape(total, 3 * mine)
+    grad_qkv = t_mm(normed_one, d_qkv).astype(BF)
+    d_qkv, grad_qkv = together(d_qkv, grad_qkv)
     partial = mm_t(d_qkv, qkv_w).astype(BF).reshape(n, rows, width)
     d_norm1 = scatter_seq(partial)
-    grad_qkv = t_mm(normed_one, d_qkv).astype(BF)
     normal_one, inv_one, _ = norm_forward(tokens.astype(F32), gain_one)
     back, gain_grad_one = norm_backward(d_norm1, normal_one, inv_one, gain_one)
     grad_in = d_after_self + back
 
     def owned(grad):
-        return collect(reduce_dp(grad.reshape(dp, width // dp, grad.shape[1])).astype(BF))
-
-    own_down = blocks_back(owned(d_down))
-    own_gu = owned(grad_gu)
-    own_gate, own_up = blocks_back(own_gu[:, :, :hid]), blocks_back(own_gu[:, :, hid:])
+        return collect(reduce_dp(grad.reshape(dp, width // dp, grad.shape[1])))
+
+    own_down = reduce_hidden(grad_down)
+    own_gu = reduce_hidden(grad_gu)
+    own_gate, own_up, own_down = collect_hidden(jnp.concatenate([own_gu, own_down], axis=1), 3)
     own_cross = owned(grad_cross)
     own_out = reduce_head_rows(jnp.concatenate([grad_out, grad_c_out], axis=1))
     own_qkv = owned(grad_qkv)

time: 997 us -> 866 us (0.87)
  waiting for transfers between devices: 435 us -> 351 us
  starting transfers between devices: 119 us -> 68.7 us
  blocking collectives: 0 us -> 14.9 us
    ppermute x30 -> x0, waiting for transfers between devices: 144 us -> none  [z_next(): return lax.ppermute(x, 'dp', [(i, (i + RING_X) % n) for i in range(n)])]
    ppermute x46 -> x58, waiting for transfers between devices: 49.4 us -> 155 us  [seq_swap(): return lax.ppermute(x, 'seq', [(i, i ^ mask) for i in range(n)])]
    ppermute x31 -> x22, waiting for transfers between devices: 225 us -> 173 us  [dp_swap(): return lax.ppermute(x, 'dp', [(i, i ^ mask) for i in range(n)])]
    dynamic_update_slice x40 -> x8, local copies, waits for them, and re-layouts: 54.9 us -> 8.23 us  [gather_head_rows(): out = lax.dynamic_update_slice(out, held[z], (place, 0))]
    unnamed x183, local copies, waits for them, and re-layouts: 8.3 us -> 43.5 us
    ppermute x30 -> x0, starting transfers between devices: 30.1 us -> none  [z_next(): return lax.ppermute(x, 'dp', [(i, (i + RING_X) % n) for i in range(n)])]
    convert_element_type x15 -> x0, other arithmetic: 19.3 us -> none  [the longest x10 11.9 us: reduce_dp(): total = z_next(total.astype(BF)).astype(F32) + at(k).astype(F32)]
    all_to_all x4 -> x3, waiting for transfers between devices: 4.15 us -> 21.9 us  [collect(): lax.all_to_all(x.reshape(n, -1, x.shape[-1]), 'seq', split_axis=0, concat...]
  transfers between devices with their start and end apart: 117 -> 97, of which waited for: 49 -> 33; matrix products, arithmetic and copies ran while one was open for 31% -> 34% of each run, Pallas kernels for 5% -> 6%
where the time goes in v2:
time: 866 us; the launch traced here: 856 us
  waiting for transfers between devices  351 us (41%)
  local copies, waits for them, and re-layouts  135 us (16%)
  matrix products  129 us (15%)
  other arithmetic  86.8 us (10%)
  starting transfers between devices  68.7 us (8%)
  Pallas kernels  54.2 us (6%)
  between operations  16.5 us (2%)
  blocking collectives  14.9 us (2%)
    ppermute x22, waiting for transfers between devices, dp_swap(): return lax.ppermute(x, 'dp', [(i, i ^ mask) for i in range(n)])  173 us
    ppermute x58, waiting for transfers between devices, seq_swap(): return lax.ppermute(x, 'seq', [(i, i ^ mask) for i in range(n)])  155 us
    dot_general x8, matrix products, mm(): return jnp.dot(left, right, preferred_element_type=F32)  47.7 us
    unnamed x183, local copies, waits for them, and re-layouts  43.5 us
    dot_general x7, matrix products, mm_t(): lax.dot_general(left, right, (((1,), (1,)), ((), ())), preferred_element_...  43.4 us
    dot_general x7, matrix products, t_mm(): lax.dot_general(left, right, (((0,), (0,)), ((), ())), preferred_element_...  38 us
    ppermute x22, starting transfers between devices, dp_swap(): return lax.ppermute(x, 'dp', [(i, i ^ mask) for i in range(n)])  25.7 us
    all_to_all x3, waiting for transfers between devices, collect(): lax.all_to_all(x.reshape(n, -1, x.shape[-1]), 'seq', split_axis=0, concat...  21.9 us
  transfers between devices with their start and end apart: 97, of which 33 were waited for; matrix products, arithmetic and copies ran while one was open for 34% of the time, Pallas kernels for 6%

profile of v2, /device:TPU:0, one launch (start us, length us, event | category | flops | bytes accessed | tf_op | source)
XLA Modules:
  0.0 856.0 jit_solution(2581307863192024228)
XLA Ops:
  12.8 14.9 %all_to_all.30 = bf16[4,48,1152]{2,1,0:T(8,128)(2,1)} all-to-all(bf16[4,48,1152]{2,1,0:T(8,128)(2,1)S(1)} %pad_maximum_fusion.18), channel_id=1, replica_groups=mesh['dp'=8,'seq'=4] {'seq'}, dimensions={0} | all-to-all | bytes 884736 | tf_op jit(solution)/shard_map/all_to_all | solution.py:217
  37.2 4.1 all-to-all-start.1
  54.9 19.4 %collective-permute-done.4 = f32[3,1536]{1,0:T(4,128)S(1)} collective-permute-done((f32[3,1536]{1,0:T(4,128)S(1)}, f32[3,1536]{1,0:T(4,128)S(1)}, u32[]{:S(2)}, u32[]{:S(2)}) %collective-permute-start.4) | collective-permute-done | bytes 18464 | tf_op jit(solution)/shard_map/ppermute | solution.py:34
  90.7 3.6 all-to-all-start.2
  114.6 11.0 %collective-permute-done.43 = bf16[256,1536]{1,0:T(8,128)(2,1)} collective-permute-done((bf16[256,1536]{1,0:T(8,128)(2,1)}, bf16[256,1536]{1,0:T(8,128)(2,1)}, u32[]{:S(2)}, u32[]{:S(2)}) %collective-permute-start.43) | collective-permute-done | bytes 786464 | tf_op jit(solution)/shard_map/ppermute | solution.py:39
  142.2 32.6 %collective-permute-done.8 = bf16[4,192,1152]{2,1,0:T(8,128)(2,1)} collective-permute-done((bf16[4,192,1152]{2,1,0:T(8,128)(2,1)}, bf16[4,192,1152]{2,1,0:T(8,128)(2,1)}, u32[]{:S(2)}, u32[]{:S(2)}) %collective-permute-start.8) | collective-permute-done | bytes 1769504 | tf_op jit(solution)/shard_map/ppermute | solution.py:39
  179.1 8.0 fusion.9.q_ref.k_ref.v_ref
  187.1 16.0 %self_forward.1 = (bf16[4,2,128,384]{3,2,1,0:T(8,128)(2,1)}, bf16[4,2,128,384]{3,2,1,0:T(8,128)(2,1)}, bf16[4,2,128,384]{3,2,1,0:T(8,128)(2,1)}, bf16[4,2,128,384]{3,2,1,0:T(8,128)(2,1)}) custom-call(f32[2,1,512]{2,1,0:T(1,128)} %compare_convert_fusion.ok_ref, f32[4,128,128]{2,1,0:T(8,128)} %concatenate.76.cos_ref, f32[4,128,128]{2,1,0:T(8,128)} %concatenate.77.up_ref, ...), custom_call_target="tpu_custom_call" | custom-call | flops 1610612736 | bytes 3145728 | tf_op jit(solution)/shard_map/self_forward/pallas_call | solution.py:430
  218.1 3.6 constant_dynamic-slice_fusion.3
  229.3 16.2 %collective-permute-done.31 = bf16[192,2304]{1,0:T(8,128)(2,1)S(1)} collective-permute-done((bf16[192,2304]{1,0:T(8,128)(2,1)}, bf16[192,2304]{1,0:T(8,128)(2,1)S(1)}, u32[]{:S(2)}, u32[]{:S(2)}) %collective-permute-start.31) | collective-permute-done | bytes 884768 | tf_op jit(solution)/shard_map/ppermute | solution.py:39
  248.6 14.7 %collective-permute-done.12 = bf16[256,1536]{1,0:T(8,128)(2,1)} collective-permute-done((bf16[256,1536]{1,0:T(8,128)(2,1)}, bf16[256,1536]{1,0:T(8,128)(2,1)}, u32[]{:S(2)}, u32[]{:S(2)}) %collective-permute-start.12) | collective-permute-done | bytes 786464 | tf_op jit(solution)/shard_map/ppermute | solution.py:34
  266.6 15.9 %collective-permute-done.16 = bf16[4,192,1152]{2,1,0:T(8,128)(2,1)} collective-permute-done((bf16[4,192,1152]{2,1,0:T(8,128)(2,1)}, bf16[4,192,1152]{2,1,0:T(8,128)(2,1)}, u32[]{:S(2)}, u32[]{:S(2)}) %collective-permute-start.16) | collective-permute-done | bytes 1769504 | tf_op jit(solution)/shard_map/ppermute | solution.py:39
  291.6 7.8 cross_forward.1
  310.4 16.3 %collective-permute-done.22 = bf16[256,1536]{1,0:T(8,128)(2,1)S(1)} collective-permute-done((bf16[256,1536]{1,0:T(8,128)(2,1)S(1)}, bf16[256,1536]{1,0:T(8,128)(2,1)S(1)}, u32[]{:S(2)}, u32[]{:S(2)}) %collective-permute-start.22) | collective-permute-done | bytes 786464 | tf_op jit(solution)/shard_map/ppermute | solution.py:34
  333.9 14.5 %collective-permute-done.24 = bf16[256,1536]{1,0:T(8,128)(2,1)S(1)} collective-permute-done((bf16[256,1536]{1,0:T(8,128)(2,1)}, bf16[256,1536]{1,0:T(8,128)(2,1)S(1)}, u32[]{:S(2)}, u32[]{:S(2)}) %collective-permute-start.24) | collective-permute-done | bytes 786464 | tf_op jit(solution)/shard_map/ppermute | solution.py:34
  354.0 4.3 collective-permute-done.28
  364.5 8.7 %fusion.24 = f32[2048,768]{0,1:T(8,128)S(1)} fusion(bf16[2048,1536]{1,0:T(8,128)(2,1)} %bitcast.350, bf16[1536,1536]{1,0:T(8,128)(2,1)} %all-gather.16.cloned.1.call-done), kind=kOutput, calls=%fused_computation.57 | convolution fusion | flops 4831838208 | bytes 14942208 | tf_op jit(solution)/shard_map/dot_general | solution.py:21
  373.3 8.5 multiply_convert_fusion.2
  381.8 9.2 %convolution_convert_fusion.9 = bf16[1536,768]{1,0:T(8,128)(2,1)} fusion(bf16[2048,1536]{1,0:T(8,128)(2,1)} %bitcast.70, bf16[2048,768]{0,1:T(8,128)(2,1)} %get-tuple-element.136), kind=kOutput, calls=%fused_computation.32 | convolution fusion | flops 4833017856 | bytes 11796480 | tf_op jit(solution)/shard_map/dot_general | solution.py:29
  391.0 13.1 %multiply_convert_fusion.1 = (bf16[2048,768]{0,1:T(8,128)(2,1)S(1)}, bf16[2048,768]{0,1:T(8,128)(2,1)S(1)}) fusion(f32[2048,768]{0,1:T(8,128)} %copy-done.77, f32[2048,768]{0,1:T(8,128)} %get-tuple-element.137, bf16[2048,1536]{1,0:T(8,128)(2,1)} %bitcast.70, bf16[1536,768]{1,0:T(8,128)(2,1)} %all-gather.18.cloned.1.call-done), kind=kOutput, calls=%fused_computation.13 | convolution fusion | flops 4852285440 | bytes 27525120 | tf_op jit(solution)/shard_map/dot_general | solution.py:21
  406.8 13.5 %convolution_convert_fusion.3 = bf16[1536,1536]{1,0:T(8,128)(2,1)} fusion(bf16[2048,1536]{1,0:T(8,128)(2,1)} %bitcast.351, bf16[2048,768]{0,1:T(8,128)(2,1)S(1)} %get-tuple-element.72, bf16[2048,768]{0,1:T(8,128)(2,1)S(1)} %get-tuple-element.71), kind=kOutput, calls=%fused_computation.5 | convolution fusion | flops 9678618624 | bytes 17301504 | tf_op jit(solution)/shard_map/dot_general | solution.py:29
  420.2 13.7 %convolution_convert_fusion.2 = bf16[2048,1536]{1,0:T(8,128)(2,1)S(1)} fusion(bf16[1536,1536]{1,0:T(8,128)(2,1)} %all-gather.16.cloned.1.call-done, bf16[2048,768]{0,1:T(8,128)(2,1)} %copy-done.79, bf16[2048,768]{0,1:T(8,128)(2,1)} %copy-done.78), kind=kOutput, calls=%fused_computation.4 | convolution fusion | flops 9679405056 | bytes 17301504 | tf_op jit(solution)/shard_map/dot_general | solution.py:25
  438.4 7.9 convolution_convert_fusion.1
  454.8 8.7 %collective-permute-done.51 = bf16[128,1536]{1,0:T(8,128)(2,1)S(1)} collective-permute-done((bf16[128,1536]{1,0:T(8,128)(2,1)S(1)}, bf16[128,1536]{1,0:T(8,128)(2,1)S(1)}, u32[]{:S(2)}, u32[]{:S(2)}) %collective-permute-start.51) | collective-permute-done | bytes 393248 | tf_op jit(solution)/shard_map/ppermute | solution.py:39
  466.0 5.6 collective-permute-done.35
  477.4 15.0 %collective-permute-done.52 = bf16[256,1536]{1,0:T(8,128)(2,1)S(1)} collective-permute-done((bf16[256,1536]{1,0:T(8,128)(2,1)S(1)}, bf16[256,1536]{1,0:T(8,128)(2,1)S(1)}, u32[]{:S(2)}, u32[]{:S(2)}) %collective-permute-start.52) | collective-permute-done | bytes 786464 | tf_op jit(solution)/shard_map/ppermute | solution.py:34
  494.0 13.6 %collective-permute-done.36 = bf16[256,1536]{1,0:T(8,128)(2,1)S(1)} collective-permute-done((bf16[256,1536]{1,0:T(8,128)(2,1)S(1)}, bf16[256,1536]{1,0:T(8,128)(2,1)S(1)}, u32[]{:S(2)}, u32[]{:S(2)}) %collective-permute-start.36) | collective-permute-done | bytes 786464 | tf_op jit(solution)/shard_map/ppermute | solution.py:34
  511.0 18.0 %collective-permute-done.57 = bf16[256,1536]{1,0:T(8,128)(2,1)S(1)} collective-permute-done((bf16[256,1536]{1,0:T(8,128)(2,1)S(1)}, bf16[256,1536]{1,0:T(8,128)(2,1)S(1)}, u32[]{:S(2)}, u32[]{:S(2)}) %collective-permute-start.57) | collective-permute-done | bytes 786464 | tf_op jit(solution)/shard_map/ppermute | solution.py:34
  531.8 4.8 convolution_convert_fusion.15
  536.6 10.5 %cross_backward.1 = (bf16[4,2,128,384]{3,2,1,0:T(8,128)(2,1)}, bf16[4,2,32,768]{3,2,1,0:T(8,128)(2,1)}) custom-call(f32[2,1,128]{2,1,0:T(1,128)} %compare_convert_fusion.1.ok_ref, bf16[4,2,128,384]{3,2,1,0:T(8,128)(2,1)} %bitcast.342, bf16[4,2,32,768]{3,2,1,0:T(8,128)(2,1)} %bitcast.328, bf16[4,2,32,768]{3,2,1,0:T(8,128)(2,1)} %bitcast.329, ...), custom_call_target="tpu_custom_call" | custom-call | flops 1006632960 | bytes 3145728 | tf_op jit(solution)/shard_map/cross_backward/pallas_call | solution.py:474
  553.0 3.7 convolution_convert_fusion.12
  561.7 16.2 %collective-permute-done.61 = bf16[256,1536]{1,0:T(8,128)(2,1)S(1)} collective-permute-done((bf16[256,1536]{1,0:T(8,128)(2,1)S(1)}, bf16[256,1536]{1,0:T(8,128)(2,1)S(1)}, u32[]{:S(2)}, u32[]{:S(2)}) %collective-permute-start.61) | collective-permute-done | bytes 786464 | tf_op jit(solution)/shard_map/ppermute | solution.py:34
  583.1 17.5 %collective-permute-done.63 = bf16[256,1536]{1,0:T(8,128)(2,1)S(1)} collective-permute-done((bf16[256,1536]{1,0:T(8,128)(2,1)}, bf16[256,1536]{1,0:T(8,128)(2,1)S(1)}, u32[]{:S(2)}, u32[]{:S(2)}) %collective-permute-start.63) | collective-permute-done | bytes 786464 | tf_op jit(solution)/shard_map/ppermute | solution.py:34
  606.5 5.8 copy.78
  624.2 30.8 %collective-permute-done.78 = bf16[4,192,1152]{2,1,0:T(8,128)(2,1)S(1)} collective-permute-done((bf16[4,192,1152]{2,1,0:T(8,128)(2,1)S(1)}, bf16[4,192,1152]{2,1,0:T(8,128)(2,1)S(1)}, u32[]{:S(2)}, u32[]{:S(2)}) %collective-permute-start.78) | collective-permute-done | bytes 1769504 | tf_op jit(solution)/shard_map/ppermute | solution.py:39
  661.3 4.0 convolution_convert_fusion.14
  665.3 19.9 %self_backward.1 = bf16[4,2,128,1152]{3,2,1,0:T(8,128)(2,1)} custom-call(f32[2,1,512]{2,1,0:T(1,128)} %compare_convert_fusion.ok_ref, f32[4,128,128]{2,1,0:T(8,128)} %concatenate.76.cos_ref, f32[4,128,128]{2,1,0:T(8,128)} %concatenate.77.up_ref, f32[4,128,128]{2,1,0:T(8,128)} %concatenate.78.down_ref, bf16[4,2,128,384]{3,2,1,0:T(8,128)(2,1)} %get-tuple-element.39.q_ref, ...), custom_call_target="tpu_custom_call" | custom-call | flops 4026531840 | bytes 3145728 | tf_op jit(solution)/shard_map/self_backward/pallas_call | solution.py:446
  685.2 6.9 convolution_convert_fusion
  701.9 7.0 convolution_convert_fusion.7
  717.9 17.2 %collective-permute-done.76 = bf16[4,192,1152]{2,1,0:T(8,128)(2,1)} collective-permute-done((bf16[4,192,1152]{2,1,0:T(8,128)(2,1)}, bf16[4,192,1152]{2,1,0:T(8,128)(2,1)}, u32[]{:S(2)}, u32[]{:S(2)}) %collective-permute-start.76) | collective-permute-done | bytes 1769504 | tf_op jit(solution)/shard_map/ppermute | solution.py:39
  751.4 19.6 %collective-permute-done.73 = f32[3,1536]{1,0:T(4,128)S(1)} collective-permute-done((f32[3,1536]{1,0:T(4,128)S(1)}, f32[3,1536]{1,0:T(4,128)S(1)}, u32[]{:S(2)}, u32[]{:S(2)}) %collective-permute-start.73) | collective-permute-done | bytes 18464 | tf_op jit(solution)/shard_map/ppermute | solution.py:39
  775.1 4.1 all-to-all-start.4
  782.0 5.2 all-to-all-done.4
  787.2 4.2 all-to-all-start.3
  794.0 10.5 %all-to-all-done.3 = bf16[4,48,1152]{2,1,0:T(8,128)(2,1)} async-done(((bf16[4,48,1152]{2,1,0:T(8,128)(2,1)}), bf16[4,48,1152]{2,1,0:T(8,128)(2,1)}, u32[]{:S(2)}, u32[]{:S(2)}) %all-to-all-start.3) | async-done | bytes 442400 | tf_op jit(solution)/shard_map/all_to_all | solution.py:223
  804.6 4.9 all-to-all-start.5
  825.4 6.2 all-to-all-done.5
  831.6 3.7 reshape.779
  (571 shorter events, 298.2 us)
Async XLA Ops:
  7.2 39.8 %all-gather.12.cloned.1.call-start = ((), (), s32[]{:S(2)}) async-start(), calls=%async_computation.12 | async-start | bytes 1474560 | tf_op jit(solution)/shard_map/all_gather | solution.py:252
  9.0 124.0 %all-gather.10.cloned.1.call-start = ((), (), s32[]{:S(2)}) async-start(), calls=%async_computation.11 | async-start | bytes 2211840 | tf_op jit(solution)/shard_map/all_gather | solution.py:113
  27.7 77.2 %collective-permute-start.18 = (bf16[64,1536]{1,0:T(8,128)(2,1)}, bf16[64,1536]{1,0:T(8,128)(2,1)}, u32[]{:S(2)}, u32[]{:S(2)}) collective-permute-start(bf16[64,1536]{1,0:T(8,128)(2,1)} %bitcast.43), channel_id=1, source_target_pairs={{0,2},{1,3},{2,0},{3,1},{4,6},{5,7},{6,4},{7,5},{8,10},{9,11},{10,... | collective-permute-start | bytes 589832 | tf_op jit(solution)/shard_map/ppermute | solution.py:34
  27.9 79.1 %collective-permute-start.17 = (bf16[64,1536]{1,0:T(8,128)(2,1)}, bf16[64,1536]{1,0:T(8,128)(2,1)}, u32[]{:S(2)}, u32[]{:S(2)}) collective-permute-start(bf16[64,1536]{1,0:T(8,128)(2,1)} %bitcast.43), channel_id=1, source_target_pairs={{0,1},{1,0},{2,3},{3,2},{4,5},{5,4},{6,7},{7,6},{8,9},{9,8},{10,11... | collective-permute-start | bytes 589832 | tf_op jit(solution)/shard_map/ppermute | solution.py:34
  28.1 26.2 %collective-permute-start.3 = (f32[3,1536]{1,0:T(4,128)S(1)}, f32[3,1536]{1,0:T(4,128)S(1)}, u32[]{:S(2)}, u32[]{:S(2)}) collective-permute-start(f32[3,1536]{1,0:T(4,128)S(1)} %dynamic_update_slice.29), channel_id=1, source_target_pairs={{0,1},{1,0},{2,3},{3,2},{4,5},{5,4},{6,7},{7,6},{8,9},{9,8},{10,11... | collective-permute-start | bytes 55304 | tf_op jit(solution)/shard_map/ppermute | solution.py:34
  28.7 80.3 %collective-permute-start.1 = (bf16[256,1536]{1,0:T(8,128)(2,1)S(1)}, bf16[256,1536]{1,0:T(8,128)(2,1)S(1)}, u32[]{:S(2)}, u32[]{:S(2)}) collective-permute-start(bf16[256,1536]{1,0:T(8,128)(2,1)S(1)} %bitcast.273), channel_id=1, source_target_pairs={{0,2},{1,3},{2,0},{3,1},{4,6},{5,7},{6,4},{7,5},{8,10},{9,11},{10,... | collective-permute-start | bytes 2359304 | tf_op jit(solution)/shard_map/ppermute | solution.py:34
  37.2 53.5 %all-to-all-start.1 = ((bf16[4,48,1152]{2,1,0:T(8,128)(2,1)}), bf16[4,48,1152]{2,1,0:T(8,128)(2,1)}, u32[]{:S(2)}, u32[]{:S(2)}) async-start(bf16[4,48,1152]{2,1,0:T(8,128)(2,1)} %pad_maximum_fusion.19), calls=%async_computation.1 | async-start | bytes 884736 | tf_op jit(solution)/shard_map/all_to_all | solution.py:217
  41.3 97.3 %all-gather.20.cloned.1.call-start = ((), (), s32[]{:S(2)}) async-start(), calls=%async_computation.21 | async-start | bytes 1966080 | tf_op jit(solution)/shard_map/all_gather | solution.py:113
  41.4 70.9 %collective-permute-start.41 = (bf16[256,1536]{1,0:T(8,128)(2,1)}, bf16[256,1536]{1,0:T(8,128)(2,1)}, u32[]{:S(2)}, u32[]{:S(2)}) collective-permute-start(bf16[256,1536]{1,0:T(8,128)(2,1)} %bitcast.61), channel_id=1, source_target_pairs={{0,2},{1,3},{2,0},{3,1},{4,6},{5,7},{6,4},{7,5},{8,10},{9,11},{10,... | collective-permute-start | bytes 2359304 | tf_op jit(solution)/shard_map/ppermute | solution.py:34
  82.1 22.6 %collective-permute-start.7 = (f32[3,1536]{1,0:T(4,128)S(1)}, f32[3,1536]{1,0:T(4,128)S(1)}, u32[]{:S(2)}, u32[]{:S(2)}) collective-permute-start(f32[3,1536]{1,0:T(4,128)S(1)} %add.542), channel_id=1, source_target_pairs={{0,16},{4,20},{8,24},{12,28},{16,0},{20,4},{24,8},{28,12},{1,17},{... | collective-permute-start | bytes 55304 | tf_op jit(solution)/shard_map/ppermute | solution.py:39
  90.7 40.4 %all-to-all-start.2 = ((bf16[4,48,4608]{2,1,0:T(8,128)(2,1)}), bf16[4,48,4608]{2,1,0:T(8,128)(2,1)S(1)}, u32[]{:S(2)}, u32[]{:S(2)}) async-start(bf16[4,48,4608]{2,1,0:T(8,128)(2,1)} %copy.86), calls=%async_computation.2 | async-start | bytes 3538944 | tf_op jit(solution)/shard_map/all_to_all | solution.py:217
  94.3 132.0 %all-gather.14.cloned.1.call-start = ((), (), s32[]{:S(2)}) async-start(), calls=%async_computation.13 | async-start | bytes 2211840 | tf_op jit(solution)/shard_map/all_gather | solution.py:113
  104.7 24.4 %collective-permute-start.40 = (bf16[256,1536]{1,0:T(8,128)(2,1)}, bf16[256,1536]{1,0:T(8,128)(2,1)}, u32[]{:S(2)}, u32[]{:S(2)}) collective-permute-start(bf16[256,1536]{1,0:T(8,128)(2,1)} %bitcast.61), channel_id=1, source_target_pairs={{0,1},{1,0},{2,3},{3,2},{4,5},{5,4},{6,7},{7,6},{8,9},{9,8},{10,11... | collective-permute-start | bytes 2359304 | tf_op jit(solution)/shard_map/ppermute | solution.py:34
  108.7 25.8 %collective-permute-start = (bf16[256,1536]{1,0:T(8,128)(2,1)S(1)}, bf16[256,1536]{1,0:T(8,128)(2,1)}, u32[]{:S(2)}, u32[]{:S(2)}) collective-permute-start(bf16[256,1536]{1,0:T(8,128)(2,1)S(1)} %bitcast.274), channel_id=1, source_target_pairs={{0,1},{1,0},{2,3},{3,2},{4,5},{5,4},{6,7},{7,6},{8,9},{9,8},{10,11... | collective-permute-start | bytes 2359304 | tf_op jit(solution)/shard_map/ppermute | solution.py:34
  109.0 25.5 %collective-permute-start.2 = (bf16[256,1536]{1,0:T(8,128)(2,1)S(1)}, bf16[256,1536]{1,0:T(8,128)(2,1)}, u32[]{:S(2)}, u32[]{:S(2)}) collective-permute-start(bf16[256,1536]{1,0:T(8,128)(2,1)S(1)} %collective-permute-done.1), channel_id=1, source_target_pairs={{0,1},{1,0},{2,3},{3,2},{4,5},{5,4},{6,7},{7,6},{8,9},{9,8},{10,11... | collective-permute-start | bytes 2359304 | tf_op jit(solution)/shard_map/ppermute | solution.py:34
  109.9 254.6 %all-gather.16.cloned.1.call-start = ((), (), s32[]{:S(2)}) async-start(), calls=%async_computation.14 | async-start | bytes 5898240 | tf_op jit(solution)/shard_map/all_gather | solution.py:176
  114.1 189.0 %collective-permute-start.45 = (bf16[128,1536]{1,0:T(8,128)(2,1)}, bf16[128,1536]{1,0:T(8,128)(2,1)}, u32[]{:S(2)}, u32[]{:S(2)}) collective-permute-start(bf16[128,1536]{1,0:T(8,128)(2,1)} %slice.430), channel_id=1, source_target_pairs={{0,4},{4,0},{8,12},{12,8},{16,20},{20,16},{24,28},{28,24},{1,5},{5... | collective-permute-start | bytes 1179656 | tf_op jit(solution)/shard_map/ppermute | solution.py:39
  127.4 176.6 %collective-permute-start.46 = (bf16[128,1536]{1,0:T(8,128)(2,1)}, bf16[128,1536]{1,0:T(8,128)(2,1)}, u32[]{:S(2)}, u32[]{:S(2)}) collective-permute-start(bf16[128,1536]{1,0:T(8,128)(2,1)} %slice.431), channel_id=1, source_target_pairs={{0,2},{1,3},{2,0},{3,1},{4,6},{5,7},{6,4},{7,5},{8,10},{9,11},{10,... | collective-permute-start | bytes 1179656 | tf_op jit(solution)/shard_map/ppermute | solution.py:34
  133.0 41.8 %collective-permute-start.8 = (bf16[4,192,1152]{2,1,0:T(8,128)(2,1)}, bf16[4,192,1152]{2,1,0:T(8,128)(2,1)}, u32[]{:S(2)}, u32[]{:S(2)}) collective-permute-start(bf16[4,192,1152]{2,1,0:T(8,128)(2,1)} %all-gather.10.cloned.1.call-done), channel_id=1, source_target_pairs={{0,4},{4,0},{8,12},{12,8},{16,20},{20,16},{24,28},{28,24},{1,5},{5... | collective-permute-start | bytes 5308424 | tf_op jit(solution)/shard_map/ppermute | solution.py:39
  138.7 67.6 %collective-permute-start.9 = (bf16[4,64,3072]{2,1,0:T(8,128)(2,1)}, bf16[4,64,3072]{2,1,0:T(8,128)(2,1)}, u32[]{:S(2)}, u32[]{:S(2)}) collective-permute-start(bf16[4,64,3072]{2,1,0:T(8,128)(2,1)} %bitcast.318), channel_id=1, source_target_pairs={{0,4},{4,0},{8,12},{12,8},{16,20},{20,16},{24,28},{28,24},{1,5},{5... | collective-permute-start | bytes 4718600 | tf_op jit(solution)/shard_map/ppermute | solution.py:39
  222.8 22.7 %collective-permute-start.31 = (bf16[192,2304]{1,0:T(8,128)(2,1)}, bf16[192,2304]{1,0:T(8,128)(2,1)S(1)}, u32[]{:S(2)}, u32[]{:S(2)}) collective-permute-start(bf16[192,2304]{1,0:T(8,128)(2,1)} %bitcast.265), channel_id=1, source_target_pairs={{0,4},{4,0},{8,12},{12,8},{16,20},{20,16},{24,28},{28,24},{1,5},{5... | collective-permute-start | bytes 2654216 | tf_op jit(solution)/shard_map/ppermute | solution.py:39
  226.3 56.2 %collective-permute-start.16 = (bf16[4,192,1152]{2,1,0:T(8,128)(2,1)}, bf16[4,192,1152]{2,1,0:T(8,128)(2,1)}, u32[]{:S(2)}, u32[]{:S(2)}) collective-permute-start(bf16[4,192,1152]{2,1,0:T(8,128)(2,1)} %all-gather.14.cloned.1.call-done), channel_id=1, source_target_pairs={{0,4},{4,0},{8,12},{12,8},{16,20},{20,16},{24,28},{28,24},{1,5},{5... | collective-permute-start | bytes 5308424 | tf_op jit(solution)/shard_map/ppermute | solution.py:39
  248.5 142.5 %all-gather.18.cloned.1.call-start = ((), (), s32[]{:S(2)}) async-start(), calls=%async_computation.15 | async-start | bytes 2949120 | tf_op jit(solution)/shard_map/all_gather | solution.py:176
  248.5 57.0 %collective-permute-start.42 = (bf16[256,1536]{1,0:T(8,128)(2,1)}, bf16[256,1536]{1,0:T(8,128)(2,1)S(1)}, u32[]{:S(2)}, u32[]{:S(2)}) collective-permute-start(bf16[256,1536]{1,0:T(8,128)(2,1)} %collective-permute-done.41), channel_id=1, source_target_pairs={{0,1},{1,0},{2,3},{3,2},{4,5},{5,4},{6,7},{7,6},{8,9},{9,8},{10,11... | collective-permute-start | bytes 2359304 | tf_op jit(solution)/shard_map/ppermute | solution.py:34
  287.3 22.2 %collective-permute-start.44 = (bf16[256,1536]{1,0:T(8,128)(2,1)}, bf16[256,1536]{1,0:T(8,128)(2,1)S(1)}, u32[]{:S(2)}, u32[]{:S(2)}) collective-permute-start(bf16[256,1536]{1,0:T(8,128)(2,1)} %collective-permute-done.43), channel_id=1, source_target_pairs={{0,1},{1,0},{2,3},{3,2},{4,5},{5,4},{6,7},{7,6},{8,9},{9,8},{10,11... | collective-permute-start | bytes 2359304 | tf_op jit(solution)/shard_map/ppermute | solution.py:34
  305.1 26.9 %collective-permute-start.47 = (bf16[256,1536]{1,0:T(8,128)(2,1)S(1)}, bf16[256,1536]{1,0:T(8,128)(2,1)S(1)}, u32[]{:S(2)}, u32[]{:S(2)}) collective-permute-start(bf16[256,1536]{1,0:T(8,128)(2,1)S(1)} %constant_dynamic-update-slice_fusion.2), channel_id=1, source_target_pairs={{0,1},{1,0},{2,3},{3,2},{4,5},{5,4},{6,7},{7,6},{8,9},{9,8},{10,11... | collective-permute-start | bytes 2359304 | tf_op jit(solution)/shard_map/ppermute | solution.py:34
  333.9 413.5 %reduce-scatter.14.cloned.1.call-start = ((), (), s32[]{:S(2)}) async-start(), calls=%async_computation.20 | async-start | bytes 2949120 | tf_op jit(solution)/shard_map/reduce_scatter | solution.py:182
  438.3 37.7 %collective-permute-start.48 = (bf16[256,1536]{1,0:T(8,128)(2,1)S(1)}, bf16[256,1536]{1,0:T(8,128)(2,1)S(1)}, u32[]{:S(2)}, u32[]{:S(2)}) collective-permute-start(bf16[256,1536]{1,0:T(8,128)(2,1)S(1)} %get-tuple-element.73), channel_id=1, source_target_pairs={{0,1},{1,0},{2,3},{3,2},{4,5},{5,4},{6,7},{7,6},{8,9},{9,8},{10,11... | collective-permute-start | bytes 2359304 | tf_op jit(solution)/shard_map/ppermute | solution.py:34
  438.4 309.0 %reduce-scatter.12.cloned.1.call-start = ((), (), s32[]{:S(2)}) async-start(), calls=%async_computation.19 | async-start | bytes 5898240 | tf_op jit(solution)/shard_map/reduce_scatter | solution.py:182
  447.7 46.4 %collective-permute-start.32 = (bf16[256,1536]{1,0:T(8,128)(2,1)S(1)}, bf16[256,1536]{1,0:T(8,128)(2,1)S(1)}, u32[]{:S(2)}, u32[]{:S(2)}) collective-permute-start(bf16[256,1536]{1,0:T(8,128)(2,1)S(1)} %get-tuple-element.80), channel_id=1, source_target_pairs={{0,1},{1,0},{2,3},{3,2},{4,5},{5,4},{6,7},{7,6},{8,9},{9,8},{10,11... | collective-permute-start | bytes 2359304 | tf_op jit(solution)/shard_map/ppermute | solution.py:34
  464.1 28.3 %collective-permute-start.52 = (bf16[256,1536]{1,0:T(8,128)(2,1)S(1)}, bf16[256,1536]{1,0:T(8,128)(2,1)S(1)}, u32[]{:S(2)}, u32[]{:S(2)}) collective-permute-start(bf16[256,1536]{1,0:T(8,128)(2,1)S(1)} %pad_maximum_fusion.15), channel_id=1, source_target_pairs={{0,2},{1,3},{2,0},{3,1},{4,6},{5,7},{6,4},{7,5},{8,10},{9,11},{10,... | collective-permute-start | bytes 2359304 | tf_op jit(solution)/shard_map/ppermute | solution.py:34
  475.5 32.1 %collective-permute-start.36 = (bf16[256,1536]{1,0:T(8,128)(2,1)S(1)}, bf16[256,1536]{1,0:T(8,128)(2,1)S(1)}, u32[]{:S(2)}, u32[]{:S(2)}) collective-permute-start(bf16[256,1536]{1,0:T(8,128)(2,1)S(1)} %pad_maximum_fusion.13), channel_id=1, source_target_pairs={{0,2},{1,3},{2,0},{3,1},{4,6},{5,7},{6,4},{7,5},{8,10},{9,11},{10,... | collective-permute-start | bytes 2359304 | tf_op jit(solution)/shard_map/ppermute | solution.py:34
  476.1 31.6 %collective-permute-start.39 = (bf16[256,1536]{1,0:T(8,128)(2,1)S(1)}, bf16[256,1536]{1,0:T(8,128)(2,1)S(1)}, u32[]{:S(2)}, u32[]{:S(2)}) collective-permute-start(bf16[256,1536]{1,0:T(8,128)(2,1)S(1)} %pad_maximum_fusion.14), channel_id=1, source_target_pairs={{0,4},{4,0},{8,12},{12,8},{16,20},{20,16},{24,28},{28,24},{1,5},{5... | collective-permute-start | bytes 2359304 | tf_op jit(solution)/shard_map/ppermute | solution.py:39
  552.5 222.6 %reduce-scatter.10.cloned.1.call-start = ((), (), s32[]{:S(2)}) async-start(), calls=%async_computation.18 | async-start | bytes 2211840 | tf_op jit(solution)/shard_map/reduce_scatter | solution.py:139
  583.0 31.4 %collective-permute-start.62 = (bf16[256,1536]{1,0:T(8,128)(2,1)}, bf16[256,1536]{1,0:T(8,128)(2,1)S(1)}, u32[]{:S(2)}, u32[]{:S(2)}) collective-permute-start(bf16[256,1536]{1,0:T(8,128)(2,1)} %get-tuple-element.61), channel_id=1, source_target_pairs={{0,1},{1,0},{2,3},{3,2},{4,5},{5,4},{6,7},{7,6},{8,9},{9,8},{10,11... | collective-permute-start | bytes 2359304 | tf_op jit(solution)/shard_map/ppermute | solution.py:34
  613.9 41.1 %collective-permute-start.78 = (bf16[4,192,1152]{2,1,0:T(8,128)(2,1)S(1)}, bf16[4,192,1152]{2,1,0:T(8,128)(2,1)S(1)}, u32[]{:S(2)}, u32[]{:S(2)}) collective-permute-start(bf16[4,192,1152]{2,1,0:T(8,128)(2,1)S(1)} %dynamic-slice_bitcast_fusion), channel_id=1, source_target_pairs={{0,4},{4,0},{8,12},{12,8},{16,20},{20,16},{24,28},{28,24},{1,5},{5... | collective-permute-start | bytes 5308424 | tf_op jit(solution)/shard_map/ppermute | solution.py:39
  656.7 122.6 %reduce-scatter.8.cloned.1.call-start = ((), (), s32[]{:S(2)}) async-start(), calls=%async_computation.17 | async-start | bytes 1966080 | tf_op jit(solution)/shard_map/reduce_scatter | solution.py:139
  661.0 37.5 %collective-permute-start.77 = (bf16[4,64,3072]{2,1,0:T(8,128)(2,1)}, bf16[4,64,3072]{2,1,0:T(8,128)(2,1)S(1)}, u32[]{:S(2)}, u32[]{:S(2)}) collective-permute-start(bf16[4,64,3072]{2,1,0:T(8,128)(2,1)} %dynamic-slice_bitcast_fusion.2), channel_id=1, source_target_pairs={{0,4},{4,0},{8,12},{12,8},{16,20},{20,16},{24,28},{28,24},{1,5},{5... | collective-permute-start | bytes 4718600 | tf_op jit(solution)/shard_map/ppermute | solution.py:39
  693.6 41.5 %collective-permute-start.76 = (bf16[4,192,1152]{2,1,0:T(8,128)(2,1)}, bf16[4,192,1152]{2,1,0:T(8,128)(2,1)}, u32[]{:S(2)}, u32[]{:S(2)}) collective-permute-start(bf16[4,192,1152]{2,1,0:T(8,128)(2,1)} %dynamic-slice_bitcast_fusion.1), channel_id=1, source_target_pairs={{0,4},{4,0},{8,12},{12,8},{16,20},{20,16},{24,28},{28,24},{1,5},{5... | collective-permute-start | bytes 5308424 | tf_op jit(solution)/shard_map/ppermute | solution.py:39
  701.6 85.6 %reduce-scatter.6.cloned.1.call-start = ((), (), s32[]{:S(2)}) async-start(), calls=%async_computation.16 | async-start | bytes 2211840 | tf_op jit(solution)/shard_map/reduce_scatter | solution.py:139
  714.3 24.0 %collective-permute-start.69 = (bf16[64,1536]{1,0:T(8,128)(2,1)S(1)}, bf16[64,1536]{1,0:T(8,128)(2,1)}, u32[]{:S(2)}, u32[]{:S(2)}) collective-permute-start(bf16[64,1536]{1,0:T(8,128)(2,1)S(1)} %get-tuple-element.113), channel_id=1, source_target_pairs={{0,1},{1,0},{2,3},{3,2},{4,5},{5,4},{6,7},{7,6},{8,9},{9,8},{10,11... | collective-permute-start | bytes 589832 | tf_op jit(solution)/shard_map/ppermute | solution.py:34
  714.7 28.5 %collective-permute-start.68 = (bf16[64,1536]{1,0:T(8,128)(2,1)S(1)}, bf16[64,1536]{1,0:T(8,128)(2,1)}, u32[]{:S(2)}, u32[]{:S(2)}) collective-permute-start(bf16[64,1536]{1,0:T(8,128)(2,1)S(1)} %get-tuple-element.112), channel_id=1, source_target_pairs={{0,1},{1,0},{2,3},{3,2},{4,5},{5,4},{6,7},{7,6},{8,9},{9,8},{10,11... | collective-permute-start | bytes 589832 | tf_op jit(solution)/shard_map/ppermute | solution.py:34
  715.2 25.2 %collective-permute-start.65 = (bf16[256,1536]{1,0:T(8,128)(2,1)S(1)}, bf16[256,1536]{1,0:T(8,128)(2,1)S(1)}, u32[]{:S(2)}, u32[]{:S(2)}) collective-permute-start(bf16[256,1536]{1,0:T(8,128)(2,1)S(1)} %get-tuple-element.91), channel_id=1, source_target_pairs={{0,1},{1,0},{2,3},{3,2},{4,5},{5,4},{6,7},{7,6},{8,9},{9,8},{10,11... | collective-permute-start | bytes 2359304 | tf_op jit(solution)/shard_map/ppermute | solution.py:34
  717.9 22.4 %collective-permute-start.67 = (bf16[256,1536]{1,0:T(8,128)(2,1)}, bf16[256,1536]{1,0:T(8,128)(2,1)S(1)}, u32[]{:S(2)}, u32[]{:S(2)}) collective-permute-start(bf16[256,1536]{1,0:T(8,128)(2,1)} %add_convert_fusion), channel_id=1, source_target_pairs={{0,2},{1,3},{2,0},{3,1},{4,6},{5,7},{6,4},{7,5},{8,10},{9,11},{10,... | collective-permute-start | bytes 2359304 | tf_op jit(solution)/shard_map/ppermute | solution.py:34
  749.1 30.7 %collective-permute-start.79 = (bf16[192,2304]{1,0:T(8,128)(2,1)S(1)}, bf16[192,2304]{1,0:T(8,128)(2,1)}, u32[]{:S(2)}, u32[]{:S(2)}) collective-permute-start(bf16[192,2304]{1,0:T(8,128)(2,1)S(1)} %dynamic-slice_bitcast_fusion.3), channel_id=1, source_target_pairs={{0,4},{4,0},{8,12},{12,8},{16,20},{20,16},{24,28},{28,24},{1,5},{5... | collective-permute-start | bytes 2654216 | tf_op jit(solution)/shard_map/ppermute | solution.py:39
  774.9 37.9 %collective-permute-start.75 = (f32[3,1536]{1,0:T(4,128)S(1)}, f32[3,1536]{1,0:T(4,128)S(1)}, u32[]{:S(2)}, u32[]{:S(2)}) collective-permute-start(f32[3,1536]{1,0:T(4,128)S(1)} %add.635), channel_id=1, source_target_pairs={{0,16},{4,20},{8,24},{12,28},{16,0},{20,4},{24,8},{28,12},{1,17},{... | collective-permute-start | bytes 55304 | tf_op jit(solution)/shard_map/ppermute | solution.py:39
  779.2 67.3 %all-gather.22.cloned.1.call-start = ((), (), s32[]{:S(2)}) async-start(), calls=%async_computation.22 | async-start | bytes 1966080 | tf_op jit(solution)/shard_map/all_gather | solution.py:284
  804.6 27.1 %all-to-all-start.5 = ((bf16[4,48,4608]{2,1,0:T(8,128)(2,1)}), bf16[4,48,4608]{2,1,0:T(8,128)(2,1)}, u32[]{:S(2)}, u32[]{:S(2)}) async-start(bf16[4,48,4608]{2,1,0:T(8,128)(2,1)} %bitcast.129), calls=%async_computation.10 | async-start | bytes 3538944 | tf_op jit(solution)/shard_map/all_to_all | solution.py:223
  (129 other events, 1746.6 us)
Sparse Core Ops, SparseCore 0:
  10.1 22.7 all-gather.11
  34.5 40.5 all-gather.9
  77.3 36.1 all-gather.19
  114.9 39.2 all-gather.13
  248.6 88.4 all-gather.15
  339.1 48.3 all-gather.17
  438.5 45.5 reduce-scatter.13
  552.6 82.8 reduce-scatter.11
  656.8 35.7 reduce-scatter.9
  701.7 32.3 reduce-scatter.7
  738.4 35.9 reduce-scatter.5
  781.3 25.1 all-gather.21

commit v3 on v2

--- a/solution.py
+++ b/solution.py
@@ -39,38 +39,59 @@
     return lax.ppermute(x, "dp", [(i, i ^ mask) for i in range(n)])
 
 
-def all_sum(v):
-    for mask in (1, 2):
-        v = v + seq_swap(v, mask)
-    mask = 1
-    while mask < lax.axis_size("dp"):
+def all_sum_dp(v):
+    mask = lax.axis_size("dp") // 2
+    while mask:
         v = v + dp_swap(v, mask)
-        mask *= 2
+        mask //= 2
     return v
 
 
-def gather_seq(x):
+def gather_seq(x, beside=()):
     core = seq_swap(x, 1)
     far = seq_swap(x, 2)
+    if beside:
+        far, *beside = together(far, *beside)
     diag = seq_swap(far, 1)
-    return jnp.stack([x, core, far, diag])
-
-
-def scatter_seq(partial):
+    blocks = jnp.stack([x, core, far, diag])
+    return (blocks, *beside) if beside else blocks
+
+
+def scatter_seq(partial, beside=()):
     far = partial[2].astype(F32) + seq_swap(partial[3], 1).astype(F32)
     arrived = seq_swap(far.astype(BF), 2)
+    arrived, *beside = together(arrived, *beside)
     near = partial[0].astype(F32) + seq_swap(partial[1], 1).astype(F32)
-    return near + arrived.astype(F32)
+    total = near + arrived.astype(F32)
+    return (total, *beside) if beside else total
 
 
 def x_swap(x):
     return dp_swap(x, 1)
 
 
+def all_sum(v):
+    for mask in (2, 1):
+        v = v + seq_swap(v, mask)
+    return all_sum_dp(v)
+
+
+def natural(blocks):
+    s = lax.axis_index("seq")
+    n = lax.axis_size("seq")
+    return [lax.dynamic_index_in_dim(blocks, k ^ s, 0, keepdims=False) for k in range(n)]
+
+
+def gather_eight_first(x):
+    return x, seq_swap(x, 2), x_swap(x)
+
+
 def gather_eight(x):
+    return gather_eight_last(*gather_eight_first(x))
+
+
+def gather_eight_last(x, far, side):
     half = x.shape[0] // 2
-    far = seq_swap(x, 2)
-    side = x_swap(x)
     corner = jnp.concatenate([x_swap(far[:half]), seq_swap(side[half:], 2)])
     blocks = []
     for near in (x, far, side, corner):
@@ -78,20 +99,41 @@
     return jnp.stack(blocks)
 
 
-def scatter_eight(partial):
+def scatter_eight(partial, first=None, second=None):
     half = partial.shape[1] // 2
 
     def with_core(k):
         return partial[k].astype(F32) + seq_swap(partial[k + 1], 1).astype(F32)
 
     corner = with_core(6).astype(BF)
+    corner, partial = together(corner, partial)
     from_x, from_y = x_swap(corner[:half]), seq_swap(corner[half:], 2)
+    out = []
+    if first is not None:
+        value = first(corner)
+        from_x, from_y, value = together(from_x, from_y, value)
+        out.append(value)
     far = with_core(2)
     far = jnp.concatenate([far[:half] + from_x.astype(F32), far[half:]]).astype(BF)
     side = with_core(4)
     side = jnp.concatenate([side[:half], side[half:] + from_y.astype(F32)]).astype(BF)
+    far, side = together(far, side)
     from_y, from_x = seq_swap(far, 2), x_swap(side)
-    return with_core(0) + from_y.astype(F32) + from_x.astype(F32)
+    if second is not None:
+        value = second(far)
+        from_y, from_x, value = together(from_y, from_x, value)
+        out.append(value)
+    return (with_core(0) + from_y.astype(F32) + from_x.astype(F32), *out)
+
+
+def scatter_eight_x(partial):
+    def with_core(k):
+        return partial[k].astype(F32) + seq_swap(partial[k + 1], 1).astype(F32)
+
+    away = jnp.stack([with_core(4).astype(BF), with_core(6).astype(BF)])
+    arrived = x_swap(away)
+    near = with_core(0) + arrived[0].astype(F32)
+    return near, (with_core(2) + arrived[1].astype(F32)).astype(BF)
 
 
 def together(*values):
@@ -113,36 +155,62 @@
     return lax.all_gather(chunk, "dp", axis=0, axis_index_groups=z_groups())
 
 
-def gather_dp(chunk):
+def gather_dp_z(chunk):
     if not ringed():
         return lax.all_gather(chunk, "dp", axis=0, tiled=True)
-    rows, cols = chunk.shape
+    return gather_z(chunk)
+
+
+def pair_x(chunk):
+    if not ringed():
+        return chunk
+    other = x_swap(chunk)
     first = lax.axis_index("dp") % RING_X == 0
-    own = gather_z(chunk)
-    other = dp_swap(own, 1)
+    return jnp.concatenate([jnp.where(first, chunk, other), jnp.where(first, other, chunk)])
+
+
+def gather_dp_x(own, other=None):
+    if not ringed():
+        return own
+    cols = own.shape[2]
+    first = lax.axis_index("dp") % RING_X == 0
+    other = dp_swap(own, 1) if other is None else other
     both = jnp.stack([jnp.where(first, own, other), jnp.where(first, other, own)], axis=1)
     return both.reshape(-1, cols)
 
 
-def reduce_dp(slots):
+def reduce_dp_x(slots):
+    kept, away = split_x(slots)
+    return join_x(kept, x_swap(away) if ringed() else None)
+
+
+def split_x(slots):
     n, rows, cols = slots.shape
     if not ringed():
-        return lax.psum_scatter(
-            slots.reshape(n * rows, cols), "dp", scatter_dimension=0, tiled=True
-        )
+        return slots, slots
     xx = lax.axis_index("dp") % RING_X
     split = slots.reshape(RING_Z, RING_X, rows, cols)
     away = lax.dynamic_index_in_dim(split, 1 - xx, axis=1, keepdims=False)
     kept = lax.dynamic_index_in_dim(split, xx, axis=1, keepdims=False)
-    arrived = dp_swap(away, 1)
-    both = (kept.astype(F32) + arrived.astype(F32)).astype(BF)
+    return kept, away
+
+
+def join_x(kept, arrived):
+    if ringed():
+        kept = (kept.astype(F32) + arrived.astype(F32)).astype(BF)
+    return kept.reshape(-1, kept.shape[-1])
+
+
+def reduce_dp_z(both):
+    if not ringed():
+        return lax.psum_scatter(both, "dp", scatter_dimension=0, tiled=True)
     return lax.psum_scatter(
-        both.reshape(RING_Z * rows, cols),
-        "dp",
-        scatter_dimension=0,
-        tiled=True,
-        axis_index_groups=z_groups(),
-    )
+        both, "dp", scatter_dimension=0, tiled=True, axis_index_groups=z_groups()
+    )
+
+
+def reduce_dp(slots):
+    return reduce_dp_z(reduce_dp_x(slots))
 
 
 def wide():
@@ -157,8 +225,7 @@
     return jnp.concatenate(cut, axis=3).transpose(1, 0, 2, 3).reshape(n, rows, -1)
 
 
-def deal_hidden(x):
-    got = deal(x)
+def deal_hidden_x(got):
     if not ringed():
         return got
     rows = got.shape[0]
@@ -184,19 +251,23 @@
     )
 
 
-def collect_hidden(x, count):
+def split_rows(x):
+    xx = lax.axis_index("dp") % RING_X
+    cut = x.reshape(RING_X, -1, x.shape[1])
+    kept = lax.dynamic_index_in_dim(cut, xx, 0, keepdims=False)
+    return kept, lax.dynamic_index_in_dim(cut, 1 - xx, 0, keepdims=False)
+
+
+def join_hidden(kept, arrived):
+    first = lax.axis_index("dp") % RING_X == 0
+    return jnp.concatenate(
+        [jnp.where(first, kept, arrived), jnp.where(first, arrived, kept)], axis=1
+    )
+
+
+def part_hidden(got, count):
     n = lax.axis_size("seq")
     parts = wide() // n
-    if ringed():
-        xx = lax.axis_index("dp") % RING_X
-        cut = x.reshape(RING_X, -1, x.shape[1])
-        kept = lax.dynamic_index_in_dim(cut, xx, 0, keepdims=False)
-        arrived = x_swap(lax.dynamic_index_in_dim(cut, 1 - xx, 0, keepdims=False))
-        first = xx == 0
-        x = jnp.concatenate(
-            [jnp.where(first, kept, arrived), jnp.where(first, arrived, kept)], axis=1
-        )
-    got = collect(x)
     rows = got.shape[1]
     got = got.reshape(n, rows, parts, count, -1)
     return [got[:, :, :, i].transpose(1, 0, 2, 3).reshape(rows, -1) for i in range(count)]
@@ -240,53 +311,71 @@
     return jnp.where(j < per, (per * d + j - s) // n, HEADS // n)
 
 
-def gather_head_rows(x):
+def head_piece(x):
+    if not ringed():
+        return x
+    rows = natural(gather_seq(x))
+    rows = jnp.concatenate(rows + [jnp.zeros((HEAD, x.shape[1]), x.dtype)])
+    return lax.dynamic_slice(rows, (head_slot()[0] * HEAD, 0), (HEAD, x.shape[1]))
+
+
+def gather_head_rows(piece):
+    n = lax.axis_size("seq")
+    s = lax.axis_index("seq")
+    rows, cols = piece.shape
+    mine = HEADS // n
+    if not ringed():
+        full = lax.all_gather(piece, ("dp", "seq"), axis=0, tiled=True)
+        picked = lax.dynamic_index_in_dim(full.reshape(mine, n, HEAD, cols), s, 1, keepdims=False)
+        return picked.reshape(mine * HEAD, cols)
+    owners = gather_z(pair_x(piece)).reshape(RING_Z * RING_X, HEAD, cols)
+    per = head_slot()[1]
+    return jnp.concatenate(
+        [
+            lax.dynamic_index_in_dim(owners, (n * p + s) // per, 0, keepdims=False)
+            for p in range(mine)
+        ]
+    )
+
+
+def split_head_rows(x):
     n = lax.axis_size("seq")
     s = lax.axis_index("seq")
     cols = x.shape[1]
     mine = HEADS // n
     if not ringed():
-        full = lax.all_gather(x, ("dp", "seq"), axis=0, tiled=True)
-        picked = lax.dynamic_index_in_dim(full.reshape(mine, n, HEAD, cols), s, 1, keepdims=False)
-        return picked.reshape(mine * HEAD, cols)
-    rows = lax.all_gather(x, "seq", axis=0, tiled=True)
-    j, per, _ = head_slot()
-    rows = jnp.concatenate([rows, jnp.zeros((HEAD, cols), x.dtype)])
-    piece = lax.dynamic_slice(rows, (j * HEAD, 0), (HEAD, cols))
-    out = jnp.zeros(((mine + 1) * HEAD, cols), x.dtype)
-    own = gather_z(piece)
-    other = dp_swap(own, 1)
-    xx = lax.axis_index("dp") % RING_X
-    for z in range(RING_Z):
-        for held, x_of in ((own, xx), (other, 1 - xx)):
-            place = slot_place(z * RING_X + x_of) * HEAD
-            out = lax.dynamic_update_slice(out, held[z], (place, 0))
-    return out[: mine * HEAD]
-
-
-def reduce_head_rows(x):
+        full = jnp.zeros((mine, n, HEAD, cols), BF)
+        full = lax.dynamic_update_index_in_dim(full, x.reshape(mine, 1, HEAD, cols), s, 1)
+        return full.reshape(-1, cols), full.reshape(-1, cols)
+    padded = jnp.concatenate([x, jnp.zeros((HEAD, cols), x.dtype)])
+    slots = jnp.stack(
+        [
+            lax.dynamic_slice(padded, (slot_place(d) * HEAD, 0), (HEAD, cols))
+            for d in range(lax.axis_size("dp"))
+        ]
+    )
+    return split_x(slots)
+
+
+def reduce_out_z(both):
+    if not ringed():
+        return lax.psum_scatter(both, ("dp", "seq"), scatter_dimension=0, tiled=True)
+    return reduce_dp_z(both)
+
+
+def head_rows_out(own):
     n = lax.axis_size("seq")
     s = lax.axis_index("seq")
     size = lax.axis_size("dp")
-    cols = x.shape[1]
-    mine = HEADS // n
-    if not ringed():
-        full = jnp.zeros((mine, n, HEAD, cols), BF)
-        full = lax.dynamic_update_index_in_dim(full, x.reshape(mine, 1, HEAD, cols), s, 1)
-        return lax.psum_scatter(
-            full.reshape(-1, cols), ("dp", "seq"), scatter_dimension=0, tiled=True
-        ).astype(F32)
-    padded = jnp.concatenate([x, jnp.zeros((HEAD, cols), x.dtype)])
-    slots = jnp.stack(
-        [lax.dynamic_slice(padded, (slot_place(d) * HEAD, 0), (HEAD, cols)) for d in range(size)]
-    )
-    own = reduce_dp(slots)
-    pieces = lax.all_gather(own, "seq", axis=0, tiled=False)
+    cols = own.shape[-1]
+    if not ringed():
+        return own.astype(F32)
+    pieces = gather_seq(own)
     per = HEADS // size
     d = lax.axis_index("dp")
     rows = jnp.concatenate(
         [
-            lax.dynamic_index_in_dim(pieces, (per * d + j) % n, 0, keepdims=False)
+            lax.dynamic_index_in_dim(pieces, ((per * d + j) % n) ^ s, 0, keepdims=False)
             for j in range(per)
         ]
     )
@@ -423,21 +512,21 @@
     )
 
 
-def self_forward(ok, tables, qkv):
-    r, b, t, width = qkv.shape
-    pairs = width // (3 * PAIR)
+def self_forward(ok, tables, qk, v):
+    r, b, t, width = v.shape
+    pairs = width // PAIR
     shape = jax.ShapeDtypeStruct((r, b, t, pairs * PAIR), BF)
     return pl.pallas_call(
         self_forward_kernel,
         grid=(b, pairs),
         in_specs=[ok_spec(ok)]
         + [table_spec(x) for x in tables]
-        + [pair_spec(qkv, i * pairs) for i in range(3)],
+        + [pair_spec(qk), pair_spec(qk, pairs), pair_spec(v)],
         out_specs=[pair_spec(shape)] * 4,
         out_shape=[shape] * 4,
         cost_estimate=cost(shape, r * t, 2),
         name="self_forward",
-    )(ok, *tables, qkv, qkv, qkv)
+    )(ok, *tables, qk, qk, v)
 
 
 def self_backward(ok, tables, q, k, v, g):
@@ -533,53 +622,86 @@
 
     gain_rows = jnp.stack([gain_self, gain_cross, gain_mlp]).astype(F32)
     share = gain_rows.shape[1]
-    gains = all_sum(
-        lax.dynamic_update_slice(jnp.zeros((3, width), F32), gain_rows, (0, (d * n + s) * share))
-    )
-    gain_one, gain_two, gain_three = gains[0], gains[1], gains[2]
-
+    placed = lax.dynamic_update_slice(jnp.zeros((3, width), F32), gain_rows, (0, (d * n + s) * share))
+    placed = placed + seq_swap(placed, 2)
     rows = batch * tokens_dev
     total = n * rows
-    qkv_w = gather_dp(
-        deal(jnp.concatenate([columns_out(w) for w in (w_query, w_key, w_value)], axis=2))
-    )
-    out_w = gather_head_rows(jnp.concatenate([w_output, c_output], axis=1))
-    w_out, c_out = out_w[:, :width], out_w[:, width:]
-    cross_w = gather_dp(
-        deal(jnp.concatenate([columns_out(w) for w in (c_query, c_key, c_value)], axis=2))
-    )
-    cq_w, ckv_w = cross_w[:, :mine], cross_w[:, mine:]
-    ffn_w = deal_hidden(hidden_out([w_gate, w_up, w_down]))
+
+    def cut(*mats):
+        return jnp.concatenate([columns_out(w) for w in mats], axis=2)
+
+    qk_part = deal(cut(w_query, w_key))
+    qk_part, w_value, c_query, w_output, c_output = together(
+        qk_part, w_value, c_query, w_output, c_output
+    )
+
+    qk_z = gather_dp_z(qk_part)
+    vcq_z = gather_dp_z(deal(cut(w_value, c_query)))
+    piece = head_piece(jnp.concatenate([w_output, c_output], axis=1))
+    out_w = gather_head_rows(piece)
+    qk_z, placed, tokens, given, c_key, c_value, w_gate, w_up, w_down = together(
+        qk_z,
+        placed,
+        inputs.reshape(rows, width),
+        conditioning.reshape(batch * cond_dev, width),
+        c_key,
+        c_value,
+        w_gate,
+        w_up,
+        w_down,
+    )
+    qk_w = gather_dp_x(qk_z)
+    gains = all_sum_dp(placed + seq_swap(placed, 1))
+    tokens_all = gather_seq(tokens)
+    gain_one, gain_two, gain_three = gains[0], gains[1], gains[2]
+    ckv_z = gather_dp_z(deal(cut(c_key, c_value)))
+    ffn_part = deal(hidden_out([w_gate, w_up, w_down]))
+    cond_all = gather_seq(given).reshape(-1, width)
     hid = w_gate.shape[1] // wide()
+    gather_ffn = gather_eight if ringed() else gather_seq
+    shared = wide()
+
+    normed_one = norm_forward(tokens_all.reshape(total, width).astype(F32), gain_one)[2]
+    vcq_w = gather_dp_x(vcq_z)
+    v_w, cq_w = vcq_w[:, :mine], vcq_w[:, mine:]
+    qk = mm(normed_one, qk_w).reshape(n, batch, tokens_dev, 2 * mine)
+    v_own = mm(normed_one, v_w).reshape(n, batch, tokens_dev, mine)
+    qk, v_own, ffn_part = together(qk, v_own, ffn_part)
+    attended, q_rot, k_rot, v_low = self_forward(key_ok, tables, qk, v_own)
+    attended = attended.reshape(total, mine)
+    ffn_w = deal_hidden_x(ffn_part)
     gu_w = gather_hidden(ffn_w[:, : 2 * hid])
     down_w = gather_hidden(ffn_w[:, 2 * hid :])
-    gather_ffn, scatter_ffn = (
-        (gather_eight, scatter_eight) if ringed() else (gather_seq, scatter_seq)
-    )
-    shared = wide()
-
-    tokens = inputs.reshape(rows, width)
-    incoming = cotangent.reshape(rows, width)
-    tokens_all = gather_seq(tokens)
-    cond_all = gather_seq(conditioning.reshape(batch * cond_dev, width)).reshape(-1, width)
-    incoming_all = gather_ffn(incoming).reshape(shared * rows, width)
-
-    normed_one = norm_forward(tokens_all.reshape(total, width).astype(F32), gain_one)[2]
-    qkv = mm(normed_one, qkv_w).reshape(n, batch, tokens_dev, 3 * mine)
-    attended, q_rot, k_rot, v_low = self_forward(key_ok, tables, qkv)
-    attended = attended.reshape(total, mine)
+    attended, ffn_w, out_w = together(attended, ffn_w, out_w)
+    w_out, c_out = out_w[:, :width], out_w[:, width:]
     partial = mm(attended, w_out).astype(BF).reshape(n, rows, width)
-    after_self = tokens.astype(F32) + scatter_seq(partial)
+    partial, ckv_z = scatter_seq(partial, (ckv_z,))
+    after_self = tokens.astype(F32) + partial
     normal_two, inv_two, own_two = norm_forward(after_self, gain_two)
-    normed_two = gather_seq(own_two).reshape(total, width)
+    if ringed():
+        normed_two, ckv_other = gather_seq(own_two, (x_swap(ckv_z),))
+        ckv_w = gather_dp_x(ckv_z, ckv_other)
+    else:
+        normed_two, ckv_w = gather_seq(own_two), ckv_z
+    normed_two = normed_two.reshape(total, width)
     cq = mm(normed_two, cq_w).astype(BF).reshape(n, batch, tokens_dev, mine)
     ckv = mm(cond_all, ckv_w).astype(BF).reshape(n, batch, cond_dev, 2 * mine)
+    cq, incoming = together(cq, cotangent.reshape(rows, width))
     cross_att = cross_forward(cond_ok, cq, ckv).reshape(total, mine)
+    if ringed():
+        cross_att, *incoming_first = together(cross_att, *gather_eight_first(incoming))
     partial = mm(cross_att, c_out).astype(BF).reshape(n, rows, width)
     after_cross = after_self + scatter_seq(partial)
+    after_cross, gu_w = together(after_cross, gu_w)
     normal_three, inv_three, own_three = norm_forward(after_cross, gain_three)
     normed_three = gather_ffn(own_three).reshape(shared * rows, width)
+    if ringed():
+        normed_three, *incoming_first = together(normed_three, *incoming_first)
+        incoming_all = gather_eight_last(*incoming_first).reshape(shared * rows, width)
+    else:
+        incoming_all = gather_seq(incoming).reshape(total, width)
     gate = mm(normed_three, gu_w[:, :hid])
+    gate, incoming_all = together(gate, incoming_all)
     up = mm(normed_three, gu_w[:, hid:])
     sig = jax.nn.sigmoid(gate)
     hidden = (gate * sig * up).astype(BF)
@@ -589,12 +711,24 @@
     d_gate = (d_hidden * up * sig * (1.0 + gate * (1.0 - sig))).astype(BF)
     d_up = (d_hidden * gate * sig).astype(BF)
     d_gu = jnp.concatenate([d_gate, d_up], axis=1)
+    own_down = reduce_hidden(grad_down)
     partial = mm_t(d_gu, gu_w).astype(BF).reshape(shared, rows, width)
-    d_norm3 = scatter_ffn(partial)
-    grad_gu = t_mm(normed_three, d_gu).astype(BF)
-    d_norm3, grad_gu = together(d_norm3, grad_gu)
-    partial = mm_t(hidden, down_w).astype(BF).reshape(shared, rows, width)
-    block = (after_cross + scatter_ffn(partial)).astype(BF)
+
+    def block_product(now):
+        _, late = together(now, hidden)
+        return mm_t(late, down_w).astype(BF).reshape(shared, rows, width)
+
+    def gu_product(now):
+        _, late = together(now, d_gu)
+        return t_mm(normed_three, late).astype(BF)
+
+    if ringed():
+        d_norm3, block_part, grad_gu = scatter_eight(partial, block_product, gu_product)
+    else:
+        d_norm3 = scatter_seq(partial)
+        block_part, grad_gu = block_product(partial), gu_product(partial)
+    d_norm3, own_down = together(d_norm3, own_down)
+    own_gu = reduce_hidden(grad_gu)
     back, gain_grad_three = norm_backward(d_norm3, normal_three, inv_three, gain_three)
     d_after_cross = incoming.astype(F32) + back
     dc_low = gather_seq(d_after_cross.astype(BF)).reshape(total, width)
@@ -604,35 +738,67 @@
     d_cq = d_cq.reshape(total, mine)
     d_ckv = d_ckv.reshape(n * batch * cond_dev, 2 * mine)
     partial = mm_t(d_cq, cq_w).astype(BF).reshape(n, rows, width)
-    d_norm2 = scatter_seq(partial)
     grad_cross = jnp.concatenate([t_mm(normed_two, d_cq), t_mm(cond_all, d_ckv)], axis=1).astype(BF)
-    d_norm2, grad_cross = together(d_norm2, grad_cross)
+    d_norm2, grad_cross = scatter_seq(partial, (grad_cross,))
+    cross_both = reduce_hidden(grad_cross)
     partial = mm_t(d_ckv, ckv_w).astype(BF).reshape(n, batch * cond_dev, width)
     grad_cond = scatter_seq(partial)
     back, gain_grad_two = norm_backward(d_norm2, normal_two, inv_two, gain_two)
     d_after_self = d_after_cross + back
-    ds_low = gather_seq(d_after_self.astype(BF)).reshape(total, width)
+    if ringed():
+        block_near, block_far = scatter_eight_x(block_part)
+        ds_low, block_near, block_far = gather_seq(
+            d_after_self.astype(BF), (block_near, block_far)
+        )
+    else:
+        ds_low = gather_seq(d_after_self.astype(BF))
+    ds_low = ds_low.reshape(total, width)
+    ds_low, own_gu = together(ds_low, own_gu)
     ds_low, grad_c_out = together(ds_low, grad_c_out)
     d_att = mm_t(ds_low, w_out).astype(BF).reshape(n, batch, tokens_dev, mine)
     grad_out = t_mm(attended, ds_low).astype(BF)
+    out_kept, out_away = split_head_rows(jnp.concatenate([grad_out, grad_c_out], axis=1))
+    d_att, out_kept, out_away = together(d_att, out_kept, out_away)
+    out_arrived = x_swap(out_away) if ringed() else out_away
     d_qkv = self_backward(key_ok, tables, q_rot, k_rot, v_low, d_att).reshape(total, 3 * mine)
     grad_qkv = t_mm(normed_one, d_qkv).astype(BF)
     d_qkv, grad_qkv = together(d_qkv, grad_qkv)
-    partial = mm_t(d_qkv, qkv_w).astype(BF).reshape(n, rows, width)
-    d_norm1 = scatter_seq(partial)
+    qkv_kept, qkv_away = split_x(grad_qkv.reshape(dp, width // dp, grad_qkv.shape[1]))
+    qkv_away, d_qkv = together(qkv_away, d_qkv)
+    partial = mm_t(d_qkv, jnp.concatenate([qk_w, v_w], axis=1))
+    partial = partial.astype(BF).reshape(n, rows, width)
+    partial, out_arrived = together(partial, out_arrived)
+    own_out = reduce_out_z(join_x(out_kept, out_arrived))
+    qkv_arrived = dp_swap(qkv_away, 1) if ringed() else None
+    if ringed():
+        d_norm1, qkv_arrived, cross_both, own_out, block_arrived = scatter_seq(
+            partial, (qkv_arrived, cross_both, own_out, seq_swap(block_far, 2))
+        )
+        block_sum = block_near + block_arrived.astype(F32)
+    else:
+        d_norm1 = scatter_seq(partial)
+    qkv_both = join_x(qkv_kept, qkv_arrived)
+    own_qkv = reduce_dp_z(qkv_both)
+    own_ffn = jnp.concatenate([own_gu, own_down], axis=1)
+    if ringed():
+        qkv_both, own_ffn, cross_both = together(qkv_both, own_ffn, cross_both)
+        ffn_kept, ffn_away = split_rows(own_ffn)
+        own_ffn = join_hidden(ffn_kept, x_swap(ffn_away))
+        cross_kept, cross_away = split_rows(cross_both)
+        own_cross = join_x(cross_kept, x_swap(cross_away))
+    else:
+        block_sum, own_cross = scatter_seq(block_part), cross_both
+    block = (after_cross + block_sum).astype(BF)
+    own_ffn = collect(own_ffn)
+    own_ffn, own_qkv = together(own_ffn, own_qkv)
     normal_one, inv_one, _ = norm_forward(tokens.astype(F32), gain_one)
     back, gain_grad_one = norm_backward(d_norm1, normal_one, inv_one, gain_one)
     grad_in = d_after_self + back
 
-    def owned(grad):
-        return collect(reduce_dp(grad.reshape(dp, width // dp, grad.shape[1])))
-
-    own_down = reduce_hidden(grad_down)
-    own_gu = reduce_hidden(grad_gu)
-    own_gate, own_up, own_down = collect_hidden(jnp.concatenate([own_gu, own_down], axis=1), 3)
-    own_cross = owned(grad_cross)
-    own_out = reduce_head_rows(jnp.concatenate([grad_out, grad_c_out], axis=1))
-    own_qkv = owned(grad_qkv)
+    own_gate, own_up, own_down = part_hidden(own_ffn, 3)
+    own_cross = collect(own_cross)
+    own_out = head_rows_out(own_out)
+    own_qkv = collect(own_qkv)
     g_q, g_k, g_v = (columns_back(own_qkv[:, :, i * mine : (i + 1) * mine]) for i in range(3))
     g_cq, g_ck, g_cv = (columns_back(own_cross[:, :, i * mine : (i + 1) * mine]) for i in range(3))
     gain_grads = all_sum(jnp.stack([gain_grad_one, gain_grad_two, gain_grad_three]))

time: 866 us -> 772 us (0.89)
  waiting for transfers between devices: 351 us -> 259 us
  local copies, waits for them, and re-layouts: 135 us -> 112 us
  other arithmetic: 86.8 us -> 105 us
  starting transfers between devices: 68.7 us -> 83.1 us
    ppermute x22, waiting for transfers between devices: 173 us -> 68.4 us  [dp_swap(): return lax.ppermute(x, 'dp', [(i, i ^ mask) for i in range(n)])]
    all_gather x2, waiting for transfers between devices: 0.01 us -> 12.4 us  [gather_hidden(): lax.all_gather(x, 'dp', axis=0, tiled=True, axis_index_groups=z_groups())]
    ppermute x58 -> x63, waiting for transfers between devices: 155 us -> 144 us  [seq_swap(): return lax.ppermute(x, 'seq', [(i, i ^ mask) for i in range(n)])]
    ppermute x58 -> x63, starting transfers between devices: 21.2 us -> 29.9 us  [seq_swap(): return lax.ppermute(x, 'seq', [(i, i ^ mask) for i in range(n)])]
    convert_element_type x5 -> x8, other arithmetic: 10.1 us -> 18.8 us  [the longest x3 7.74 us: join_x(): kept = (kept.astype(F32) + arrived.astype(F32)).astype(BF)]
    another operation x13 -> x17, other arithmetic: 9.81 us -> 18.3 us  [the longest x7 9.24 us: gather_seq(): blocks = jnp.stack([x, core, far, diag])]
    unnamed x183 -> x226, local copies, waits for them, and re-layouts: 43.5 us -> 35.5 us
    dot_general x8 -> x9, matrix products: 47.7 us -> 51.1 us  [mm(): return jnp.dot(left, right, preferred_element_type=F32)]
  transfers between devices with their start and end apart: 97 -> 102, of which waited for: 33 -> 37; matrix products, arithmetic and copies ran while one was open for 34% -> 36% of each run, Pallas kernels for 6% -> 7%
where the time goes in v3:
time: 772 us; the launch traced here: 761 us
  waiting for transfers between devices  259 us (34%)
  matrix products  122 us (16%)
  local copies, waits for them, and re-layouts  112 us (15%)
  other arithmetic  105 us (14%)
  starting transfers between devices  83.1 us (11%)
  Pallas kernels  53.7 us (7%)
  between operations  16.3 us (2%)
  blocking collectives  10.5 us (1%)
    ppermute x63, waiting for transfers between devices, seq_swap(): return lax.ppermute(x, 'seq', [(i, i ^ mask) for i in range(n)])  144 us
    ppermute x22, waiting for transfers between devices, dp_swap(): return lax.ppermute(x, 'dp', [(i, i ^ mask) for i in range(n)])  68.4 us
    dot_general x9, matrix products, mm(): return jnp.dot(left, right, preferred_element_type=F32)  51.1 us
    dot_general x7, matrix products, mm_t(): lax.dot_general(left, right, (((1,), (1,)), ((), ())), preferred_element_...  37.9 us
    unnamed x226, local copies, waits for them, and re-layouts  35.5 us
    dot_general x7, matrix products, t_mm(): lax.dot_general(left, right, (((0,), (0,)), ((), ())), preferred_element_...  33 us
    ppermute x63, starting transfers between devices, seq_swap(): return lax.ppermute(x, 'seq', [(i, i ^ mask) for i in range(n)])  29.9 us
    ppermute x22, starting transfers between devices, dp_swap(): return lax.ppermute(x, 'dp', [(i, i ^ mask) for i in range(n)])  27.8 us
  transfers between devices with their start and end apart: 102, of which 37 were waited for; matrix products, arithmetic and copies ran while one was open for 36% of the time, Pallas kernels for 7%

profile of v3, /device:TPU:0, one launch (start us, length us, event | category | flops | bytes accessed | tf_op | source)
XLA Modules:
  0.0 761.2 jit_solution(5133783548111875430)
XLA Ops:
  10.3 10.5 %all_to_all.35 = bf16[4,48,768]{2,1,0:T(8,128)(2,1)} all-to-all(bf16[4,48,768]{2,1,0:T(8,128)(2,1)S(1)} %pad_maximum_fusion.20), channel_id=1, replica_groups=mesh['dp'=8,'seq'=4] {'seq'}, dimensions={0} | all-to-all | bytes 589824 | tf_op jit(solution)/shard_map/all_to_all | solution.py:288
  22.5 7.3 collective-permute-done.12
  34.1 6.2 all-to-all-done.1
  43.5 8.9 %collective-permute-done.14 = bf16[64,3072]{1,0:T(8,128)(2,1)S(1)} collective-permute-done((bf16[64,3072]{1,0:T(8,128)(2,1)S(1)}, bf16[64,3072]{1,0:T(8,128)(2,1)S(1)}, u32[]{:S(2)}, u32[]{:S(2)}) %collective-permute-start.14) | collective-permute-done | bytes 393248 | tf_op jit(solution)/shard_map/ppermute | solution.py:39
  77.8 4.1 all-to-all-start.3
  91.4 4.5 all-to-all-start.2
  100.8 13.0 %collective-permute-done.9 = bf16[4,192,768]{2,1,0:T(8,128)(2,1)} collective-permute-done((bf16[4,192,768]{2,1,0:T(8,128)(2,1)}, bf16[4,192,768]{2,1,0:T(8,128)(2,1)}, u32[]{:S(2)}, u32[]{:S(2)}) %collective-permute-start.9) | collective-permute-done | bytes 1179680 | tf_op jit(solution)/shard_map/ppermute | solution.py:39
  121.0 4.7 fusion.35.v_ref
  125.7 5.6 fusion.62.q_ref.k_ref
  133.8 15.8 %self_forward.1 = (bf16[4,2,128,384]{3,2,1,0:T(8,128)(2,1)}, bf16[4,2,128,384]{3,2,1,0:T(8,128)(2,1)}, bf16[4,2,128,384]{3,2,1,0:T(8,128)(2,1)}, bf16[4,2,128,384]{3,2,1,0:T(8,128)(2,1)}) custom-call(f32[2,1,512]{2,1,0:T(1,128)} %compare_convert_fusion.ok_ref, f32[4,128,128]{2,1,0:T(8,128)} %concatenate.82.cos_ref, f32[4,128,128]{2,1,0:T(8,128)} %concatenate.83.up_ref, ...), custom_call_target="tpu_custom_call" | custom-call | flops 1610612736 | bytes 3145728 | tf_op jit(solution)/shard_map/self_forward/pallas_call | solution.py:519
  157.9 3.6 constant_dynamic-slice_fusion.4
  166.2 17.6 %collective-permute-done.10 = bf16[192,2304]{1,0:T(8,128)(2,1)S(1)} collective-permute-done((bf16[192,2304]{1,0:T(8,128)(2,1)S(1)}, bf16[192,2304]{1,0:T(8,128)(2,1)S(1)}, u32[]{:S(2)}, u32[]{:S(2)}) %collective-permute-start.10) | collective-permute-done | bytes 884768 | tf_op jit(solution)/shard_map/ppermute | solution.py:39
  195.6 19.8 %collective-permute-done.23 = bf16[64,1536]{1,0:T(8,128)(2,1)S(1)} collective-permute-done((bf16[64,1536]{1,0:T(8,128)(2,1)S(1)}, bf16[64,1536]{1,0:T(8,128)(2,1)S(1)}, u32[]{:S(2)}, u32[]{:S(2)}) %collective-permute-start.23) | collective-permute-done | bytes 196640 | tf_op jit(solution)/shard_map/ppermute | solution.py:34
  230.4 7.8 %cross_forward.1 = bf16[4,2,128,384]{3,2,1,0:T(8,128)(2,1)} custom-call(f32[2,1,128]{2,1,0:T(1,128)} %compare_convert_fusion.1.ok_ref, bf16[4,2,128,384]{3,2,1,0:T(8,128)(2,1)} %bitcast.454, bf16[4,2,32,768]{3,2,1,0:T(8,128)(2,1)} %bitcast.438, bf16[4,2,32,768]{3,2,1,0:T(8,128)(2,1)} %bitcast.439), custom_call_target="tpu_custom_call" | custom-call | flops 402653184 | bytes 3145728 | tf_op jit(solution)/shard_map/cross_forward/pallas_call | solution.py:549
  238.2 5.8 collective-permute-done.25
  245.0 3.6 convolution_convert_fusion.5
  252.0 18.9 %collective-permute-done.29 = bf16[256,1536]{1,0:T(8,128)(2,1)S(1)} collective-permute-done((bf16[256,1536]{1,0:T(8,128)(2,1)S(1)}, bf16[256,1536]{1,0:T(8,128)(2,1)S(1)}, u32[]{:S(2)}, u32[]{:S(2)}) %collective-permute-start.29) | collective-permute-done | bytes 786464 | tf_op jit(solution)/shard_map/ppermute | solution.py:34
  271.3 12.4 %all-gather.13.cloned.1.call-done = bf16[1536,1536]{1,0:T(8,128)(2,1)} async-done(((bf16[384,1536]{1,0:T(8,128)(2,1)}), bf16[1536,1536]{1,0:T(8,128)(2,1)}) %all-gather.13.cloned.1.call-update) | async-done | bytes 4718608 | tf_op jit(solution)/shard_map/all_gather | solution.py:243
  289.5 15.7 %collective-permute-done.31 = bf16[256,1536]{1,0:T(8,128)(2,1)} collective-permute-done((bf16[256,1536]{1,0:T(8,128)(2,1)}, bf16[256,1536]{1,0:T(8,128)(2,1)}, u32[]{:S(2)}, u32[]{:S(2)}) %collective-permute-start.31) | collective-permute-done | bytes 786464 | tf_op jit(solution)/shard_map/ppermute | solution.py:34
  328.4 9.7 %fusion.14 = f32[2048,768]{1,0:T(8,128)} fusion(bf16[2048,1536]{1,0:T(8,128)(2,1)} %bitcast.473, bf16[1536,1536]{1,0:T(8,128)(2,1)} %all-gather.13.cloned.1.call-done), kind=kOutput, calls=%fused_computation.50 | convolution fusion | flops 4831838208 | bytes 14942208 | tf_op jit(solution)/shard_map/dot_general | solution.py:21
  342.7 9.7 %multiply_convert_fusion.2 = (bf16[2048,768]{1,0:T(8,128)(2,1)S(1)}, f32[2048,768]{1,0:T(8,128)}) fusion(f32[2048,768]{1,0:T(8,128)} %fusion.14, bf16[2048,1536]{1,0:T(8,128)(2,1)S(1)} %bitcast.476, bf16[1536,1536]{1,0:T(8,128)(2,1)S(1)} %bitcast.487), kind=kOutput, calls=%fused_computation.14 | convolution fusion | flops 4841275392 | bytes 24379392 | tf_op jit(solution)/shard_map/dot_general | solution.py:21
  354.0 6.5 convolution_convert_fusion.9
  360.5 11.8 %multiply_convert_fusion.1 = (bf16[2048,768]{1,0:T(8,128)(2,1)S(1)}, bf16[2048,768]{1,0:T(8,128)(2,1)S(1)}) fusion(f32[2048,768]{1,0:T(8,128)} %fusion.14, f32[2048,768]{1,0:T(8,128)} %get-tuple-element.276, bf16[2048,1536]{1,0:T(8,128)(2,1)} %bitcast.472, bf16[1536,768]{1,0:T(8,128)(2,1)} %all-gather.15.cloned.1.call-done), kind=kOutput, calls=%fused_computation.13 | convolution fusion | flops 4852285440 | bytes 27525120 | tf_op jit(solution)/shard_map/dot_general | solution.py:21
  372.3 14.5 %convolution_convert_fusion.2 = bf16[2048,1536]{1,0:T(8,128)(2,1)S(1)} fusion(bf16[1536,1536]{1,0:T(8,128)(2,1)} %all-gather.13.cloned.1.call-done, bf16[2048,768]{1,0:T(8,128)(2,1)S(1)} %get-tuple-element.210, bf16[2048,768]{1,0:T(8,128)(2,1)S(1)} %get-tuple-element.209), kind=kOutput, calls=%fused_computation.4 | convolution fusion | flops 9679405056 | bytes 17301504 | tf_op jit(solution)/shard_map/dot_general | solution.py:25
  401.4 7.2 convolution_convert_fusion.1
  414.7 11.6 %convolution_convert_fusion.3 = bf16[1536,1536]{1,0:T(8,128)(2,1)} fusion(bf16[2048,1536]{1,0:T(8,128)(2,1)S(1)} %bitcast.479, bf16[2048,1536]{1,0:T(8,128)(2,1)S(1)} %pad_maximum_fusion), kind=kOutput, calls=%fused_computation.5 | convolution fusion | flops 9666035712 | bytes 17301504 | tf_op jit(solution)/shard_map/dot_general | solution.py:29
  426.3 6.7 collective-permute-done.50
  442.7 17.8 %collective-permute-done.53 = bf16[256,1536]{1,0:T(8,128)(2,1)} collective-permute-done((bf16[256,1536]{1,0:T(8,128)(2,1)}, bf16[256,1536]{1,0:T(8,128)(2,1)}, u32[]{:S(2)}, u32[]{:S(2)}) %collective-permute-start.53) | collective-permute-done | bytes 786464 | tf_op jit(solution)/shard_map/ppermute | solution.py:34
  470.0 10.3 %cross_backward.1 = (bf16[4,2,128,384]{3,2,1,0:T(8,128)(2,1)}, bf16[4,2,32,768]{3,2,1,0:T(8,128)(2,1)}) custom-call(f32[2,1,128]{2,1,0:T(1,128)} %compare_convert_fusion.1.ok_ref, bf16[4,2,128,384]{3,2,1,0:T(8,128)(2,1)} %bitcast.455, bf16[4,2,32,768]{3,2,1,0:T(8,128)(2,1)} %bitcast.440, bf16[4,2,32,768]{3,2,1,0:T(8,128)(2,1)} %bitcast.441, ...), custom_call_target="tpu_custom_call" | custom-call | flops 1006632960 | bytes 3145728 | tf_op jit(solution)/shard_map/cross_backward/pallas_call | solution.py:563
  495.3 15.6 %collective-permute-done.57 = bf16[256,1536]{1,0:T(8,128)(2,1)S(1)} collective-permute-done((bf16[256,1536]{1,0:T(8,128)(2,1)S(1)}, bf16[256,1536]{1,0:T(8,128)(2,1)S(1)}, u32[]{:S(2)}, u32[]{:S(2)}) %collective-permute-start.57) | collective-permute-done | bytes 786464 | tf_op jit(solution)/shard_map/ppermute | solution.py:34
  518.4 6.2 collective-permute-done.62
  524.6 4.4 fusion.29
  529.0 5.0 collective-permute-done.58
  541.1 5.8 copy.116
  550.4 4.2 convolution_convert_fusion.10
  561.7 19.7 %self_backward.1 = bf16[4,2,128,1152]{3,2,1,0:T(8,128)(2,1)} custom-call(f32[2,1,512]{2,1,0:T(1,128)} %compare_convert_fusion.ok_ref, f32[4,128,128]{2,1,0:T(8,128)} %concatenate.82.cos_ref, f32[4,128,128]{2,1,0:T(8,128)} %concatenate.83.up_ref, f32[4,128,128]{2,1,0:T(8,128)} %concatenate.84.down_ref, bf16[4,2,128,384]{3,2,1,0:T(8,128)(2,1)} %get-tuple-element.159.q_ref, ...), custom_call_target="tpu_custom_call" | custom-call | flops 4026531840 | bytes 3145728 | tf_op jit(solution)/shard_map/self_backward/pallas_call | solution.py:535
  581.4 7.0 convolution_convert_fusion
  592.4 5.7 convolution_convert_fusion.7
  610.0 4.8 collective-permute-done.74
  625.9 9.6 %collective-permute-done.70 = bf16[256,1536]{1,0:T(8,128)(2,1)} collective-permute-done((bf16[256,1536]{1,0:T(8,128)(2,1)}, bf16[256,1536]{1,0:T(8,128)(2,1)}, u32[]{:S(2)}, u32[]{:S(2)}) %collective-permute-start.70) | collective-permute-done | bytes 786464 | tf_op jit(solution)/shard_map/ppermute | solution.py:34
  635.5 11.1 %collective-permute-done.69 = bf16[4,192,1152]{2,1,0:T(8,128)(2,1)} collective-permute-done((bf16[4,192,1152]{2,1,0:T(8,128)(2,1)}, bf16[4,192,1152]{2,1,0:T(8,128)(2,1)}, u32[]{:S(2)}, u32[]{:S(2)}) %collective-permute-start.69) | collective-permute-done | bytes 1769504 | tf_op jit(solution)/shard_map/ppermute | solution.py:39
  646.6 3.8 collective-permute-done.68
  652.3 3.6 fusion.10
  690.4 4.7 all-to-all-done.6
  702.7 4.5 all-to-all-start.4
  709.7 19.7 %all-to-all-done.4 = bf16[4,48,4608]{2,1,0:T(8,128)(2,1)} async-done(((bf16[4,48,4608]{2,1,0:T(8,128)(2,1)}), bf16[4,48,4608]{2,1,0:T(8,128)(2,1)}, u32[]{:S(2)}, u32[]{:S(2)}) %all-to-all-start.4) | async-done | bytes 1769504 | tf_op jit(solution)/shard_map/all_to_all | solution.py:294
  729.4 3.7 reshape.798
  733.2 4.3 all-to-all-start.5
  (627 shorter events, 309.8 us)
Async XLA Ops:
  7.2 50.7 %all-gather.17.cloned.1.call-start = ((), (), s32[]{:S(2)}) async-start(), calls=%async_computation.20 | async-start | bytes 1474560 | tf_op jit(solution)/shard_map/all_gather | solution.py:155
  21.4 19.8 %collective-permute-start.11 = (bf16[48,3072]{1,0:T(8,128)(2,1)S(1)}, bf16[48,3072]{1,0:T(8,128)(2,1)S(1)}, u32[]{:S(2)}, u32[]{:S(2)}) collective-permute-start(bf16[48,3072]{1,0:T(8,128)(2,1)S(1)} %constant_dynamic-update-slice_fusion), channel_id=1, source_target_pairs={{0,1},{1,0},{2,3},{3,2},{4,5},{5,4},{6,7},{7,6},{8,9},{9,8},{10,11... | collective-permute-start | bytes 884744 | tf_op jit(solution)/shard_map/ppermute | solution.py:34
  34.1 50.8 %all-gather.9.cloned.1.call-start = ((), (), s32[]{:S(2)}) async-start(), calls=%async_computation.12 | async-start | bytes 1474560 | tf_op jit(solution)/shard_map/all_gather | solution.py:155
  41.1 108.5 %all-gather.19.cloned.1.call-start = ((), (), s32[]{:S(2)}) async-start(), calls=%async_computation.21 | async-start | bytes 3932160 | tf_op jit(solution)/shard_map/all_gather | solution.py:155
  59.0 38.2 %collective-permute-start.8 = (bf16[4,192,768]{2,1,0:T(8,128)(2,1)}, bf16[4,192,768]{2,1,0:T(8,128)(2,1)}, u32[]{:S(2)}, u32[]{:S(2)}) collective-permute-start(bf16[4,192,768]{2,1,0:T(8,128)(2,1)} %bitcast.442), channel_id=1, source_target_pairs={{0,4},{4,0},{8,12},{12,8},{16,20},{20,16},{24,28},{28,24},{1,5},{5... | collective-permute-start | bytes 3538952 | tf_op jit(solution)/shard_map/ppermute | solution.py:39
  67.6 29.1 %collective-permute-start.2 = (bf16[256,1536]{1,0:T(8,128)(2,1)S(1)}, bf16[256,1536]{1,0:T(8,128)(2,1)S(1)}, u32[]{:S(2)}, u32[]{:S(2)}) collective-permute-start(bf16[256,1536]{1,0:T(8,128)(2,1)S(1)} %bitcast.354), channel_id=1, source_target_pairs={{0,2},{1,3},{2,0},{3,1},{4,6},{5,7},{6,4},{7,5},{8,10},{9,11},{10,... | collective-permute-start | bytes 2359304 | tf_op jit(solution)/shard_map/ppermute | solution.py:34
  68.5 48.5 %collective-permute-start.1 = (bf16[256,1536]{1,0:T(8,128)(2,1)S(1)}, bf16[256,1536]{1,0:T(8,128)(2,1)}, u32[]{:S(2)}, u32[]{:S(2)}) collective-permute-start(bf16[256,1536]{1,0:T(8,128)(2,1)S(1)} %bitcast.355), channel_id=1, source_target_pairs={{0,1},{1,0},{2,3},{3,2},{4,5},{5,4},{6,7},{7,6},{8,9},{9,8},{10,11... | collective-permute-start | bytes 2359304 | tf_op jit(solution)/shard_map/ppermute | solution.py:34
  84.8 28.9 %collective-permute-start.9 = (bf16[4,192,768]{2,1,0:T(8,128)(2,1)}, bf16[4,192,768]{2,1,0:T(8,128)(2,1)}, u32[]{:S(2)}, u32[]{:S(2)}) collective-permute-start(bf16[4,192,768]{2,1,0:T(8,128)(2,1)} %all-gather.9.cloned.1.call-done), channel_id=1, source_target_pairs={{0,4},{4,0},{8,12},{12,8},{16,20},{20,16},{24,28},{28,24},{1,5},{5... | collective-permute-start | bytes 3538952 | tf_op jit(solution)/shard_map/ppermute | solution.py:39
  91.4 40.0 %all-to-all-start.2 = ((bf16[4,48,4608]{2,1,0:T(8,128)(2,1)}), bf16[4,48,4608]{2,1,0:T(8,128)(2,1)}, u32[]{:S(2)}, u32[]{:S(2)}) async-start(bf16[4,48,4608]{2,1,0:T(8,128)(2,1)} %reshape.759), calls=%async_computation.2 | async-start | bytes 3538944 | tf_op jit(solution)/shard_map/all_to_all | solution.py:288
  95.8 89.4 %all-gather.11.cloned.1.call-start = ((), (), s32[]{:S(2)}) async-start(), calls=%async_computation.13 | async-start | bytes 1474560 | tf_op jit(solution)/shard_map/all_gather | solution.py:155
  96.4 187.3 %all-gather.13.cloned.1.call-start = ((), (), s32[]{:S(2)}) async-start(), calls=%async_computation.14 | async-start | bytes 5898240 | tf_op jit(solution)/shard_map/all_gather | solution.py:243
  96.7 20.3 %collective-permute-start.3 = (bf16[256,1536]{1,0:T(8,128)(2,1)S(1)}, bf16[256,1536]{1,0:T(8,128)(2,1)S(1)}, u32[]{:S(2)}, u32[]{:S(2)}) collective-permute-start(bf16[256,1536]{1,0:T(8,128)(2,1)S(1)} %collective-permute-done.2), channel_id=1, source_target_pairs={{0,1},{1,0},{2,3},{3,2},{4,5},{5,4},{6,7},{7,6},{8,9},{9,8},{10,11... | collective-permute-start | bytes 2359304 | tf_op jit(solution)/shard_map/ppermute | solution.py:34
  161.7 22.1 %collective-permute-start.10 = (bf16[192,2304]{1,0:T(8,128)(2,1)S(1)}, bf16[192,2304]{1,0:T(8,128)(2,1)S(1)}, u32[]{:S(2)}, u32[]{:S(2)}) collective-permute-start(bf16[192,2304]{1,0:T(8,128)(2,1)S(1)} %bitcast.446), channel_id=1, source_target_pairs={{0,4},{4,0},{8,12},{12,8},{16,20},{20,16},{24,28},{28,24},{1,5},{5... | collective-permute-start | bytes 2654216 | tf_op jit(solution)/shard_map/ppermute | solution.py:39
  163.7 22.4 %collective-permute-start.15 = (bf16[256,1536]{1,0:T(8,128)(2,1)S(1)}, bf16[256,1536]{1,0:T(8,128)(2,1)S(1)}, u32[]{:S(2)}, u32[]{:S(2)}) collective-permute-start(bf16[256,1536]{1,0:T(8,128)(2,1)S(1)} %get-tuple-element.232), channel_id=1, source_target_pairs={{0,1},{1,0},{2,3},{3,2},{4,5},{5,4},{6,7},{7,6},{8,9},{9,8},{10,11... | collective-permute-start | bytes 2359304 | tf_op jit(solution)/shard_map/ppermute | solution.py:34
  165.1 20.1 %collective-permute-start.17 = (bf16[256,1536]{1,0:T(8,128)(2,1)}, bf16[256,1536]{1,0:T(8,128)(2,1)S(1)}, u32[]{:S(2)}, u32[]{:S(2)}) collective-permute-start(bf16[256,1536]{1,0:T(8,128)(2,1)} %add_convert_fusion.5), channel_id=1, source_target_pairs={{0,2},{1,3},{2,0},{3,1},{4,6},{5,7},{6,4},{7,5},{8,10},{9,11},{10,... | collective-permute-start | bytes 2359304 | tf_op jit(solution)/shard_map/ppermute | solution.py:34
  189.1 27.8 %collective-permute-start.20 = (bf16[4,192,768]{2,1,0:T(8,128)(2,1)}, bf16[4,192,768]{2,1,0:T(8,128)(2,1)S(1)}, u32[]{:S(2)}, u32[]{:S(2)}) collective-permute-start(bf16[4,192,768]{2,1,0:T(8,128)(2,1)} %all-gather.11.cloned.1.call-done), channel_id=1, source_target_pairs={{0,4},{4,0},{8,12},{12,8},{16,20},{20,16},{24,28},{28,24},{1,5},{5... | collective-permute-start | bytes 3538952 | tf_op jit(solution)/shard_map/ppermute | solution.py:39
  192.2 23.7 %collective-permute-start.19 = (bf16[256,1536]{1,0:T(8,128)(2,1)}, bf16[256,1536]{1,0:T(8,128)(2,1)}, u32[]{:S(2)}, u32[]{:S(2)}) collective-permute-start(bf16[256,1536]{1,0:T(8,128)(2,1)} %multiply_convert_fusion.5), channel_id=1, source_target_pairs={{0,2},{1,3},{2,0},{3,1},{4,6},{5,7},{6,4},{7,5},{8,10},{9,11},{10,... | collective-permute-start | bytes 2359304 | tf_op jit(solution)/shard_map/ppermute | solution.py:34
  194.4 166.1 %all-gather.15.cloned.1.call-start = ((), (), s32[]{:S(2)}) async-start(), calls=%async_computation.15 | async-start | bytes 2949120 | tf_op jit(solution)/shard_map/all_gather | solution.py:243
  194.5 20.9 %collective-permute-start.23 = (bf16[64,1536]{1,0:T(8,128)(2,1)S(1)}, bf16[64,1536]{1,0:T(8,128)(2,1)S(1)}, u32[]{:S(2)}, u32[]{:S(2)}) collective-permute-start(bf16[64,1536]{1,0:T(8,128)(2,1)S(1)} %bitcast.465), channel_id=1, source_target_pairs={{0,2},{1,3},{2,0},{3,1},{4,6},{5,7},{6,4},{7,5},{8,10},{9,11},{10,... | collective-permute-start | bytes 589832 | tf_op jit(solution)/shard_map/ppermute | solution.py:34
  195.6 22.1 %collective-permute-start.22 = (bf16[64,1536]{1,0:T(8,128)(2,1)S(1)}, bf16[64,1536]{1,0:T(8,128)(2,1)S(1)}, u32[]{:S(2)}, u32[]{:S(2)}) collective-permute-start(bf16[64,1536]{1,0:T(8,128)(2,1)S(1)} %bitcast.466), channel_id=1, source_target_pairs={{0,1},{1,0},{2,3},{3,2},{4,5},{5,4},{6,7},{7,6},{8,9},{9,8},{10,11... | collective-permute-start | bytes 589832 | tf_op jit(solution)/shard_map/ppermute | solution.py:34
  287.1 20.6 %collective-permute-start.33 = (bf16[256,1536]{1,0:T(8,128)(2,1)}, bf16[256,1536]{1,0:T(8,128)(2,1)}, u32[]{:S(2)}, u32[]{:S(2)}) collective-permute-start(bf16[256,1536]{1,0:T(8,128)(2,1)} %get-tuple-element.206), channel_id=1, source_target_pairs={{0,4},{4,0},{8,12},{12,8},{16,20},{20,16},{24,28},{28,24},{1,5},{5... | collective-permute-start | bytes 2359304 | tf_op jit(solution)/shard_map/ppermute | solution.py:39
  288.6 22.2 %collective-permute-start.30 = (bf16[256,1536]{1,0:T(8,128)(2,1)}, bf16[256,1536]{1,0:T(8,128)(2,1)}, u32[]{:S(2)}, u32[]{:S(2)}) collective-permute-start(bf16[256,1536]{1,0:T(8,128)(2,1)} %get-tuple-element.206), channel_id=1, source_target_pairs={{0,1},{1,0},{2,3},{3,2},{4,5},{5,4},{6,7},{7,6},{8,9},{9,8},{10,11... | collective-permute-start | bytes 2359304 | tf_op jit(solution)/shard_map/ppermute | solution.py:34
  289.5 147.6 %reduce-scatter.8.cloned.1.call-start = ((), (), s32[]{:S(2)}) async-start(), calls=%async_computation.16 | async-start | bytes 2949120 | tf_op jit(solution)/shard_map/reduce_scatter | solution.py:249
  390.6 159.8 %reduce-scatter.10.cloned.1.call-start = ((), (), s32[]{:S(2)}) async-start(), calls=%async_computation.17 | async-start | bytes 5898240 | tf_op jit(solution)/shard_map/reduce_scatter | solution.py:249
  401.4 32.4 %collective-permute-start.45 = (bf16[256,1536]{1,0:T(8,128)(2,1)}, bf16[256,1536]{1,0:T(8,128)(2,1)}, u32[]{:S(2)}, u32[]{:S(2)}) collective-permute-start(bf16[256,1536]{1,0:T(8,128)(2,1)} %get-tuple-element.219), channel_id=1, source_target_pairs={{0,1},{1,0},{2,3},{3,2},{4,5},{5,4},{6,7},{7,6},{8,9},{9,8},{10,11... | collective-permute-start | bytes 2359304 | tf_op jit(solution)/shard_map/ppermute | solution.py:34
  412.8 20.2 %collective-permute-start.50 = (bf16[256,1536]{1,0:T(8,128)(2,1)}, bf16[256,1536]{1,0:T(8,128)(2,1)}, u32[]{:S(2)}, u32[]{:S(2)}) collective-permute-start(bf16[256,1536]{1,0:T(8,128)(2,1)} %pad_maximum_fusion.18), channel_id=1, source_target_pairs={{0,2},{1,3},{2,0},{3,1},{4,6},{5,7},{6,4},{7,5},{8,10},{9,11},{10,... | collective-permute-start | bytes 2359304 | tf_op jit(solution)/shard_map/ppermute | solution.py:34
  413.8 19.9 %collective-permute-start.51 = (bf16[256,1536]{1,0:T(8,128)(2,1)}, bf16[256,1536]{1,0:T(8,128)(2,1)}, u32[]{:S(2)}, u32[]{:S(2)}) collective-permute-start(bf16[256,1536]{1,0:T(8,128)(2,1)} %pad_maximum_fusion.19), channel_id=1, source_target_pairs={{0,4},{4,0},{8,12},{12,8},{16,20},{20,16},{24,28},{28,24},{1,5},{5... | collective-permute-start | bytes 2359304 | tf_op jit(solution)/shard_map/ppermute | solution.py:39
  442.6 181.1 %reduce-scatter.16.cloned.1.call-start = ((), (), s32[]{:S(2)}) async-start(), calls=%async_computation.22 | async-start | bytes 4423680
  442.7 22.4 %collective-permute-start.52 = (bf16[256,1536]{1,0:T(8,128)(2,1)}, bf16[256,1536]{1,0:T(8,128)(2,1)S(1)}, u32[]{:S(2)}, u32[]{:S(2)}) collective-permute-start(bf16[256,1536]{1,0:T(8,128)(2,1)} %get-tuple-element.203), channel_id=1, source_target_pairs={{0,1},{1,0},{2,3},{3,2},{4,5},{5,4},{6,7},{7,6},{8,9},{9,8},{10,11... | collective-permute-start | bytes 2359304 | tf_op jit(solution)/shard_map/ppermute | solution.py:34
  464.1 20.2 %collective-permute-start.60 = (bf16[256,1536]{1,0:T(8,128)(2,1)}, bf16[256,1536]{1,0:T(8,128)(2,1)}, u32[]{:S(2)}, u32[]{:S(2)}) collective-permute-start(bf16[256,1536]{1,0:T(8,128)(2,1)} %get-tuple-element.215), channel_id=1, source_target_pairs={{0,1},{1,0},{2,3},{3,2},{4,5},{5,4},{6,7},{7,6},{8,9},{9,8},{10,11... | collective-permute-start | bytes 2359304 | tf_op jit(solution)/shard_map/ppermute | solution.py:34
  464.6 19.7 %collective-permute-start.61 = (bf16[256,1536]{1,0:T(8,128)(2,1)}, bf16[256,1536]{1,0:T(8,128)(2,1)}, u32[]{:S(2)}, u32[]{:S(2)}) collective-permute-start(bf16[256,1536]{1,0:T(8,128)(2,1)} %get-tuple-element.214), channel_id=1, source_target_pairs={{0,1},{1,0},{2,3},{3,2},{4,5},{5,4},{6,7},{7,6},{8,9},{9,8},{10,11... | collective-permute-start | bytes 2359304 | tf_op jit(solution)/shard_map/ppermute | solution.py:34
  464.6 53.8 %collective-permute-start.59 = (bf16[256,1536]{1,0:T(8,128)(2,1)}, bf16[256,1536]{1,0:T(8,128)(2,1)}, u32[]{:S(2)}, u32[]{:S(2)}) collective-permute-start(bf16[256,1536]{1,0:T(8,128)(2,1)} %get-tuple-element.216), channel_id=1, source_target_pairs={{0,1},{1,0},{2,3},{3,2},{4,5},{5,4},{6,7},{7,6},{8,9},{9,8},{10,11... | collective-permute-start | bytes 2359304 | tf_op jit(solution)/shard_map/ppermute | solution.py:34
  465.1 53.3 %collective-permute-start.63 = (bf16[256,1536]{1,0:T(8,128)(2,1)}, bf16[256,1536]{1,0:T(8,128)(2,1)}, u32[]{:S(2)}, u32[]{:S(2)}) collective-permute-start(bf16[256,1536]{1,0:T(8,128)(2,1)} %get-tuple-element.213), channel_id=1, source_target_pairs={{0,1},{1,0},{2,3},{3,2},{4,5},{5,4},{6,7},{7,6},{8,9},{9,8},{10,11... | collective-permute-start | bytes 2359304 | tf_op jit(solution)/shard_map/ppermute | solution.py:34
  487.9 36.7 %collective-permute-start.62 = (bf16[2,256,1536]{2,1,0:T(8,128)(2,1)}, bf16[2,256,1536]{2,1,0:T(8,128)(2,1)}, u32[]{:S(2)}, u32[]{:S(2)}) collective-permute-start(bf16[2,256,1536]{2,1,0:T(8,128)(2,1)} %pad_maximum_fusion.13), channel_id=1, source_target_pairs={{0,4},{4,0},{8,12},{12,8},{16,20},{20,16},{24,28},{28,24},{1,5},{5... | collective-permute-start | bytes 4718600 | tf_op jit(solution)/shard_map/ppermute | solution.py:39
  489.2 21.7 %collective-permute-start.55 = (bf16[256,1536]{1,0:T(8,128)(2,1)S(1)}, bf16[256,1536]{1,0:T(8,128)(2,1)S(1)}, u32[]{:S(2)}, u32[]{:S(2)}) collective-permute-start(bf16[256,1536]{1,0:T(8,128)(2,1)S(1)} %get-tuple-element.228), channel_id=1, source_target_pairs={{0,1},{1,0},{2,3},{3,2},{4,5},{5,4},{6,7},{7,6},{8,9},{9,8},{10,11... | collective-permute-start | bytes 2359304 | tf_op jit(solution)/shard_map/ppermute | solution.py:34
  490.9 20.0 %collective-permute-start.57 = (bf16[256,1536]{1,0:T(8,128)(2,1)S(1)}, bf16[256,1536]{1,0:T(8,128)(2,1)S(1)}, u32[]{:S(2)}, u32[]{:S(2)}) collective-permute-start(bf16[256,1536]{1,0:T(8,128)(2,1)S(1)} %add_convert_fusion.2), channel_id=1, source_target_pairs={{0,2},{1,3},{2,0},{3,1},{4,6},{5,7},{6,4},{7,5},{8,10},{9,11},{10,... | collective-permute-start | bytes 2359304 | tf_op jit(solution)/shard_map/ppermute | solution.py:34
  546.9 103.9 %reduce-scatter.12.cloned.1.call-start = ((), (), s32[]{:S(2)}) async-start(), calls=%async_computation.18 | async-start | bytes 1966080 | tf_op jit(solution)/shard_map/reduce_scatter | solution.py:207
  561.7 37.0 %collective-permute-start.66 = (bf16[4,64,3072]{2,1,0:T(8,128)(2,1)}, bf16[4,64,3072]{2,1,0:T(8,128)(2,1)}, u32[]{:S(2)}, u32[]{:S(2)}) collective-permute-start(bf16[4,64,3072]{2,1,0:T(8,128)(2,1)} %get-tuple-element.171), channel_id=1, source_target_pairs={{0,4},{4,0},{8,12},{12,8},{16,20},{20,16},{24,28},{28,24},{1,5},{5... | collective-permute-start | bytes 4718600 | tf_op jit(solution)/shard_map/ppermute | solution.py:39
  602.0 127.4 %reduce-scatter.14.cloned.1.call-start = ((), (), s32[]{:S(2)}) async-start(), calls=%async_computation.19 | async-start | bytes 2211840 | tf_op jit(solution)/shard_map/reduce_scatter | solution.py:207
  605.7 40.9 %collective-permute-start.69 = (bf16[4,192,1152]{2,1,0:T(8,128)(2,1)}, bf16[4,192,1152]{2,1,0:T(8,128)(2,1)}, u32[]{:S(2)}, u32[]{:S(2)}) collective-permute-start(bf16[4,192,1152]{2,1,0:T(8,128)(2,1)} %dynamic-slice_bitcast_fusion), channel_id=1, source_target_pairs={{0,4},{4,0},{8,12},{12,8},{16,20},{20,16},{24,28},{28,24},{1,5},{5... | collective-permute-start | bytes 5308424 | tf_op jit(solution)/shard_map/ppermute | solution.py:39
  614.8 20.7 %collective-permute-start.70 = (bf16[256,1536]{1,0:T(8,128)(2,1)}, bf16[256,1536]{1,0:T(8,128)(2,1)}, u32[]{:S(2)}, u32[]{:S(2)}) collective-permute-start(bf16[256,1536]{1,0:T(8,128)(2,1)} %get-tuple-element.177), channel_id=1, source_target_pairs={{0,2},{1,3},{2,0},{3,1},{4,6},{5,7},{6,4},{7,5},{8,10},{9,11},{10,... | collective-permute-start | bytes 2359304 | tf_op jit(solution)/shard_map/ppermute | solution.py:34
  618.6 31.8 %collective-permute-start.68 = (bf16[256,1536]{1,0:T(8,128)(2,1)}, bf16[256,1536]{1,0:T(8,128)(2,1)S(1)}, u32[]{:S(2)}, u32[]{:S(2)}) collective-permute-start(bf16[256,1536]{1,0:T(8,128)(2,1)} %fusion.28), channel_id=1, source_target_pairs={{0,2},{1,3},{2,0},{3,1},{4,6},{5,7},{6,4},{7,5},{8,10},{9,11},{10,... | collective-permute-start | bytes 2359304 | tf_op jit(solution)/shard_map/ppermute | solution.py:34
  623.7 38.3 %collective-permute-start.71 = (bf16[256,1536]{1,0:T(8,128)(2,1)}, bf16[256,1536]{1,0:T(8,128)(2,1)}, u32[]{:S(2)}, u32[]{:S(2)}) collective-permute-start(bf16[256,1536]{1,0:T(8,128)(2,1)} %get-tuple-element.224), channel_id=1, source_target_pairs={{0,1},{1,0},{2,3},{3,2},{4,5},{5,4},{6,7},{7,6},{8,9},{9,8},{10,11... | collective-permute-start | bytes 2359304 | tf_op jit(solution)/shard_map/ppermute | solution.py:34
  650.8 39.6 %collective-permute-start.82 = (bf16[64,3072]{1,0:T(8,128)(2,1)}, bf16[64,3072]{1,0:T(8,128)(2,1)}, u32[]{:S(2)}, u32[]{:S(2)}) collective-permute-start(bf16[64,3072]{1,0:T(8,128)(2,1)} %reduce-scatter.12.cloned.1.call-done), channel_id=1, source_target_pairs={{0,2},{1,3},{2,0},{3,1},{4,6},{5,7},{6,4},{7,5},{8,10},{9,11},{10,... | collective-permute-start | bytes 1179656 | tf_op jit(solution)/shard_map/ppermute | solution.py:34
  652.3 54.9 %collective-permute-start.81 = (bf16[64,3072]{1,0:T(8,128)(2,1)}, bf16[64,3072]{1,0:T(8,128)(2,1)}, u32[]{:S(2)}, u32[]{:S(2)}) collective-permute-start(bf16[64,3072]{1,0:T(8,128)(2,1)} %reduce-scatter.12.cloned.1.call-done), channel_id=1, source_target_pairs={{0,1},{1,0},{2,3},{3,2},{4,5},{5,4},{6,7},{7,6},{8,9},{9,8},{10,11... | collective-permute-start | bytes 1179656 | tf_op jit(solution)/shard_map/ppermute | solution.py:34
  657.7 25.1 %collective-permute-start.84 = (bf16[192,1152]{1,0:T(8,128)(2,1)S(1)}, bf16[192,1152]{1,0:T(8,128)(2,1)S(1)}, u32[]{:S(2)}, u32[]{:S(2)}) collective-permute-start(bf16[192,1152]{1,0:T(8,128)(2,1)S(1)} %dynamic-slice_bitcast_fusion.4), channel_id=1, source_target_pairs={{0,4},{4,0},{8,12},{12,8},{16,20},{20,16},{24,28},{28,24},{1,5},{5... | collective-permute-start | bytes 1327112 | tf_op jit(solution)/shard_map/ppermute | solution.py:39
  661.6 38.4 %collective-permute-start.80 = (bf16[192,2304]{1,0:T(8,128)(2,1)}, bf16[192,2304]{1,0:T(8,128)(2,1)}, u32[]{:S(2)}, u32[]{:S(2)}) collective-permute-start(bf16[192,2304]{1,0:T(8,128)(2,1)} %dynamic-slice_bitcast_fusion.3), channel_id=1, source_target_pairs={{0,4},{4,0},{8,12},{12,8},{16,20},{20,16},{24,28},{28,24},{1,5},{5... | collective-permute-start | bytes 2654216 | tf_op jit(solution)/shard_map/ppermute | solution.py:39
  702.7 26.7 %all-to-all-start.4 = ((bf16[4,48,4608]{2,1,0:T(8,128)(2,1)}), bf16[4,48,4608]{2,1,0:T(8,128)(2,1)}, u32[]{:S(2)}, u32[]{:S(2)}) async-start(bf16[4,48,4608]{2,1,0:T(8,128)(2,1)} %bitcast.154), calls=%async_computation.7 | async-start | bytes 3538944 | tf_op jit(solution)/shard_map/all_to_all | solution.py:294
  (150 other events, 1480.4 us)
Sparse Core Ops, SparseCore 0:
  21.0 30.9 all-gather.16
  54.1 30.6 all-gather.8
  87.0 62.5 all-gather.18
  151.0 28.8 all-gather.10
  194.5 89.0 all-gather.12
  289.6 46.7 all-gather.14
  390.8 46.0 reduce-scatter.7
  442.7 83.7 reduce-scatter.9
  547.1 65.3 reduce-scatter.15
  615.2 35.6 reduce-scatter.11
  656.1 37.6 reduce-scatter.13

commit v4 on v3

--- a/solution.py
+++ b/solution.py
@@ -753,7 +753,11 @@
     else:
         ds_low = gather_seq(d_after_self.astype(BF))
     ds_low = ds_low.reshape(total, width)
-    ds_low, own_gu = together(ds_low, own_gu)
+    ds_low, own_gu, own_down = together(ds_low, own_gu, own_down)
+    own_ffn = jnp.concatenate([own_gu, own_down], axis=1)
+    if ringed():
+        ffn_kept, ffn_away = split_rows(own_ffn)
+        ffn_arrived = x_swap(ffn_away)
     ds_low, grad_c_out = together(ds_low, grad_c_out)
     d_att = mm_t(ds_low, w_out).astype(BF).reshape(n, batch, tokens_dev, mine)
     grad_out = t_mm(attended, ds_low).astype(BF)
@@ -761,6 +765,10 @@
     d_att, out_kept, out_away = together(d_att, out_kept, out_away)
     out_arrived = x_swap(out_away) if ringed() else out_away
     d_qkv = self_backward(key_ok, tables, q_rot, k_rot, v_low, d_att).reshape(total, 3 * mine)
+    if ringed():
+        d_qkv, ffn_arrived = together(d_qkv, ffn_arrived)
+        own_ffn = join_hidden(ffn_kept, ffn_arrived)
+    own_ffn = collect(own_ffn)
     grad_qkv = t_mm(normed_one, d_qkv).astype(BF)
     d_qkv, grad_qkv = together(d_qkv, grad_qkv)
     qkv_kept, qkv_away = split_x(grad_qkv.reshape(dp, width // dp, grad_qkv.shape[1]))
@@ -771,26 +779,21 @@
     own_out = reduce_out_z(join_x(out_kept, out_arrived))
     qkv_arrived = dp_swap(qkv_away, 1) if ringed() else None
     if ringed():
-        d_norm1, qkv_arrived, cross_both, own_out, block_arrived = scatter_seq(
-            partial, (qkv_arrived, cross_both, own_out, seq_swap(block_far, 2))
+        d_norm1, qkv_arrived, cross_both, own_out, block_arrived, own_ffn = scatter_seq(
+            partial, (qkv_arrived, cross_both, own_out, seq_swap(block_far, 2), own_ffn)
         )
         block_sum = block_near + block_arrived.astype(F32)
     else:
         d_norm1 = scatter_seq(partial)
     qkv_both = join_x(qkv_kept, qkv_arrived)
     own_qkv = reduce_dp_z(qkv_both)
-    own_ffn = jnp.concatenate([own_gu, own_down], axis=1)
-    if ringed():
-        qkv_both, own_ffn, cross_both = together(qkv_both, own_ffn, cross_both)
-        ffn_kept, ffn_away = split_rows(own_ffn)
-        own_ffn = join_hidden(ffn_kept, x_swap(ffn_away))
+    if ringed():
+        qkv_both, cross_both = together(qkv_both, cross_both)
         cross_kept, cross_away = split_rows(cross_both)
         own_cross = join_x(cross_kept, x_swap(cross_away))
     else:
         block_sum, own_cross = scatter_seq(block_part), cross_both
     block = (after_cross + block_sum).astype(BF)
-    own_ffn = collect(own_ffn)
-    own_ffn, own_qkv = together(own_ffn, own_qkv)
     normal_one, inv_one, _ = norm_forward(tokens.astype(F32), gain_one)
     back, gain_grad_one = norm_backward(d_norm1, normal_one, inv_one, gain_one)
     grad_in = d_after_self + back

time: 772 us -> 755 us (0.978)
  local copies, waits for them, and re-layouts: 112 us -> 103 us
    all_to_all x3, waiting for transfers between devices: 24.4 us -> 13.8 us  [collect(): lax.all_to_all(x.reshape(n, -1, x.shape[-1]), 'seq', split_axis=0, concat...]
    ppermute x63, waiting for transfers between devices: 144 us -> 153 us  [seq_swap(): return lax.ppermute(x, 'seq', [(i, i ^ mask) for i in range(n)])]
    unnamed x226 -> x238, local copies, waits for them, and re-layouts: 35.5 us -> 33.3 us
  transfers between devices with their start and end apart: 102 -> 102, of which waited for: 37 -> 33; matrix products, arithmetic and copies ran while one was open for 36% -> 36% of each run, Pallas kernels for 7% -> 7%
where the time goes in v4:
time: 755 us; the launch traced here: 745 us
  waiting for transfers between devices  254 us (34%)
  matrix products  120 us (16%)
  local copies, waits for them, and re-layouts  103 us (14%)
  other arithmetic  102 us (14%)
  starting transfers between devices  85.1 us (11%)
  Pallas kernels  53.7 us (7%)
  between operations  16.3 us (2%)
  blocking collectives  10.5 us (1%)
    ppermute x63, waiting for transfers between devices, seq_swap(): return lax.ppermute(x, 'seq', [(i, i ^ mask) for i in range(n)])  153 us
    ppermute x22, waiting for transfers between devices, dp_swap(): return lax.ppermute(x, 'dp', [(i, i ^ mask) for i in range(n)])  63.2 us
    dot_general x9, matrix products, mm(): return jnp.dot(left, right, preferred_element_type=F32)  51.7 us
    dot_general x7, matrix products, mm_t(): lax.dot_general(left, right, (((1,), (1,)), ((), ())), preferred_element_...  37.3 us
    unnamed x238, local copies, waits for them, and re-layouts  33.3 us
    dot_general x7, matrix products, t_mm(): lax.dot_general(left, right, (((0,), (0,)), ((), ())), preferred_element_...  31.3 us
    ppermute x22, starting transfers between devices, dp_swap(): return lax.ppermute(x, 'dp', [(i, i ^ mask) for i in range(n)])  30.4 us
    ppermute x63, starting transfers between devices, seq_swap(): return lax.ppermute(x, 'seq', [(i, i ^ mask) for i in range(n)])  30.4 us
  transfers between devices with their start and end apart: 102, of which 33 were waited for; matrix products, arithmetic and copies ran while one was open for 36% of the time, Pallas kernels for 7%

profile of v4, /device:TPU:0, one launch (start us, length us, event | category | flops | bytes accessed | tf_op | source)
XLA Modules:
  0.0 745.3 jit_solution(1772919183609876280)
XLA Ops:
  10.3 10.5 %all_to_all.35 = bf16[4,48,768]{2,1,0:T(8,128)(2,1)} all-to-all(bf16[4,48,768]{2,1,0:T(8,128)(2,1)S(1)} %pad_maximum_fusion.19), channel_id=1, replica_groups=mesh['dp'=8,'seq'=4] {'seq'}, dimensions={0} | all-to-all | bytes 589824 | tf_op jit(solution)/shard_map/all_to_all | solution.py:288
  22.5 7.3 collective-permute-done.12
  34.1 6.2 all-to-all-done.1
  43.5 8.9 %collective-permute-done.14 = bf16[64,3072]{1,0:T(8,128)(2,1)S(1)} collective-permute-done((bf16[64,3072]{1,0:T(8,128)(2,1)S(1)}, bf16[64,3072]{1,0:T(8,128)(2,1)S(1)}, u32[]{:S(2)}, u32[]{:S(2)}) %collective-permute-start.14) | collective-permute-done | bytes 393248 | tf_op jit(solution)/shard_map/ppermute | solution.py:39
  77.8 4.1 all-to-all-start.3
  91.4 4.5 all-to-all-start.2
  100.8 12.9 %collective-permute-done.9 = bf16[4,192,768]{2,1,0:T(8,128)(2,1)} collective-permute-done((bf16[4,192,768]{2,1,0:T(8,128)(2,1)}, bf16[4,192,768]{2,1,0:T(8,128)(2,1)}, u32[]{:S(2)}, u32[]{:S(2)}) %collective-permute-start.9) | collective-permute-done | bytes 1179680 | tf_op jit(solution)/shard_map/ppermute | solution.py:39
  122.2 4.6 fusion.33.v_ref
  126.8 5.6 fusion.62.q_ref.k_ref
  134.9 15.8 %self_forward.1 = (bf16[4,2,128,384]{3,2,1,0:T(8,128)(2,1)}, bf16[4,2,128,384]{3,2,1,0:T(8,128)(2,1)}, bf16[4,2,128,384]{3,2,1,0:T(8,128)(2,1)}, bf16[4,2,128,384]{3,2,1,0:T(8,128)(2,1)}) custom-call(f32[2,1,512]{2,1,0:T(1,128)} %compare_convert_fusion.ok_ref, f32[4,128,128]{2,1,0:T(8,128)} %concatenate.82.cos_ref, f32[4,128,128]{2,1,0:T(8,128)} %concatenate.83.up_ref, ...), custom_call_target="tpu_custom_call" | custom-call | flops 1610612736 | bytes 3145728 | tf_op jit(solution)/shard_map/self_forward/pallas_call | solution.py:519
  159.1 3.6 constant_dynamic-slice_fusion.4
  167.0 18.0 %collective-permute-done.10 = bf16[192,2304]{1,0:T(8,128)(2,1)S(1)} collective-permute-done((bf16[192,2304]{1,0:T(8,128)(2,1)S(1)}, bf16[192,2304]{1,0:T(8,128)(2,1)S(1)}, u32[]{:S(2)}, u32[]{:S(2)}) %collective-permute-start.10) | collective-permute-done | bytes 884768 | tf_op jit(solution)/shard_map/ppermute | solution.py:39
  196.8 19.8 %collective-permute-done.23 = bf16[64,1536]{1,0:T(8,128)(2,1)S(1)} collective-permute-done((bf16[64,1536]{1,0:T(8,128)(2,1)S(1)}, bf16[64,1536]{1,0:T(8,128)(2,1)S(1)}, u32[]{:S(2)}, u32[]{:S(2)}) %collective-permute-start.23) | collective-permute-done | bytes 196640 | tf_op jit(solution)/shard_map/ppermute | solution.py:34
  231.2 7.8 %cross_forward.1 = bf16[4,2,128,384]{3,2,1,0:T(8,128)(2,1)} custom-call(f32[2,1,128]{2,1,0:T(1,128)} %compare_convert_fusion.1.ok_ref, bf16[4,2,128,384]{3,2,1,0:T(8,128)(2,1)} %bitcast.470, bf16[4,2,32,768]{3,2,1,0:T(8,128)(2,1)} %bitcast.454, bf16[4,2,32,768]{3,2,1,0:T(8,128)(2,1)} %bitcast.455), custom_call_target="tpu_custom_call" | custom-call | flops 402653184 | bytes 3145728 | tf_op jit(solution)/shard_map/cross_forward/pallas_call | solution.py:549
  239.0 6.2 collective-permute-done.25
  245.5 3.6 convolution_convert_fusion.5
  253.1 18.3 %collective-permute-done.29 = bf16[256,1536]{1,0:T(8,128)(2,1)S(1)} collective-permute-done((bf16[256,1536]{1,0:T(8,128)(2,1)S(1)}, bf16[256,1536]{1,0:T(8,128)(2,1)S(1)}, u32[]{:S(2)}, u32[]{:S(2)}) %collective-permute-start.29) | collective-permute-done | bytes 786464 | tf_op jit(solution)/shard_map/ppermute | solution.py:34
  271.8 13.0 %all-gather.13.cloned.1.call-done = bf16[1536,1536]{1,0:T(8,128)(2,1)} async-done(((bf16[384,1536]{1,0:T(8,128)(2,1)}), bf16[1536,1536]{1,0:T(8,128)(2,1)}) %all-gather.13.cloned.1.call-update) | async-done | bytes 4718608 | tf_op jit(solution)/shard_map/all_gather | solution.py:243
  290.7 15.5 %collective-permute-done.31 = bf16[256,1536]{1,0:T(8,128)(2,1)S(1)} collective-permute-done((bf16[256,1536]{1,0:T(8,128)(2,1)}, bf16[256,1536]{1,0:T(8,128)(2,1)S(1)}, u32[]{:S(2)}, u32[]{:S(2)}) %collective-permute-start.31) | collective-permute-done | bytes 786464 | tf_op jit(solution)/shard_map/ppermute | solution.py:34
  312.9 3.5 collective-permute-done.35
  326.7 9.7 %fusion.12 = f32[2048,768]{1,0:T(8,128)} fusion(bf16[2048,1536]{1,0:T(8,128)(2,1)} %bitcast.490, bf16[1536,1536]{1,0:T(8,128)(2,1)} %all-gather.13.cloned.1.call-done), kind=kOutput, calls=%fused_computation.48 | convolution fusion | flops 4831838208 | bytes 14942208 | tf_op jit(solution)/shard_map/dot_general | solution.py:21
  340.3 10.3 %multiply_convert_fusion.2 = (bf16[2048,768]{1,0:T(8,128)(2,1)S(1)}, f32[2048,768]{1,0:T(8,128)}) fusion(f32[2048,768]{1,0:T(8,128)} %fusion.12, bf16[2048,1536]{1,0:T(8,128)(2,1)S(1)} %bitcast.493, bf16[1536,1536]{1,0:T(8,128)(2,1)S(1)} %bitcast.506), kind=kOutput, calls=%fused_computation.11 | convolution fusion | flops 4841275392 | bytes 24379392 | tf_op jit(solution)/shard_map/dot_general | solution.py:21
  352.3 6.5 convolution_convert_fusion.9
  358.8 11.8 %multiply_convert_fusion.1 = (bf16[2048,768]{1,0:T(8,128)(2,1)S(1)}, bf16[2048,768]{1,0:T(8,128)(2,1)S(1)}) fusion(f32[2048,768]{1,0:T(8,128)} %fusion.12, f32[2048,768]{1,0:T(8,128)} %get-tuple-element.282, bf16[2048,1536]{1,0:T(8,128)(2,1)} %bitcast.489, bf16[1536,768]{1,0:T(8,128)(2,1)} %all-gather.15.cloned.1.call-done), kind=kOutput, calls=%fused_computation.10 | convolution fusion | flops 4852285440 | bytes 27525120 | tf_op jit(solution)/shard_map/dot_general | solution.py:21
  370.6 14.5 %convolution_convert_fusion.2 = bf16[2048,1536]{1,0:T(8,128)(2,1)S(1)} fusion(bf16[1536,1536]{1,0:T(8,128)(2,1)} %all-gather.13.cloned.1.call-done, bf16[2048,768]{1,0:T(8,128)(2,1)S(1)} %get-tuple-element.212, bf16[2048,768]{1,0:T(8,128)(2,1)S(1)} %get-tuple-element.211), kind=kOutput, calls=%fused_computation.2 | convolution fusion | flops 9679405056 | bytes 17301504 | tf_op jit(solution)/shard_map/dot_general | solution.py:25
  397.8 7.3 convolution_convert_fusion.1
  411.3 11.6 %convolution_convert_fusion.3 = bf16[1536,1536]{1,0:T(8,128)(2,1)} fusion(bf16[2048,1536]{1,0:T(8,128)(2,1)S(1)} %bitcast.496, bf16[2048,1536]{1,0:T(8,128)(2,1)S(1)} %pad_maximum_fusion), kind=kOutput, calls=%fused_computation.3 | convolution fusion | flops 9666035712 | bytes 17301504 | tf_op jit(solution)/shard_map/dot_general | solution.py:29
  422.9 6.5 collective-permute-done.50
  444.9 11.8 %collective-permute-done.53 = bf16[256,1536]{1,0:T(8,128)(2,1)} collective-permute-done((bf16[256,1536]{1,0:T(8,128)(2,1)}, bf16[256,1536]{1,0:T(8,128)(2,1)}, u32[]{:S(2)}, u32[]{:S(2)}) %collective-permute-start.53) | collective-permute-done | bytes 786464 | tf_op jit(solution)/shard_map/ppermute | solution.py:34
  466.9 10.3 %cross_backward.1 = (bf16[4,2,128,384]{3,2,1,0:T(8,128)(2,1)}, bf16[4,2,32,768]{3,2,1,0:T(8,128)(2,1)}) custom-call(f32[2,1,128]{2,1,0:T(1,128)} %compare_convert_fusion.1.ok_ref, bf16[4,2,128,384]{3,2,1,0:T(8,128)(2,1)} %bitcast.471, bf16[4,2,32,768]{3,2,1,0:T(8,128)(2,1)} %bitcast.456, bf16[4,2,32,768]{3,2,1,0:T(8,128)(2,1)} %bitcast.457, ...), custom_call_target="tpu_custom_call" | custom-call | flops 1006632960 | bytes 3145728 | tf_op jit(solution)/shard_map/cross_backward/pallas_call | solution.py:563
  491.4 15.4 %collective-permute-done.57 = bf16[256,1536]{1,0:T(8,128)(2,1)S(1)} collective-permute-done((bf16[256,1536]{1,0:T(8,128)(2,1)S(1)}, bf16[256,1536]{1,0:T(8,128)(2,1)S(1)}, u32[]{:S(2)}, u32[]{:S(2)}) %collective-permute-start.57) | collective-permute-done | bytes 786464 | tf_op jit(solution)/shard_map/ppermute | solution.py:34
  511.1 8.8 %collective-permute-done.62 = bf16[2,256,1536]{2,1,0:T(8,128)(2,1)S(1)} collective-permute-done((bf16[2,256,1536]{2,1,0:T(8,128)(2,1)S(1)}, bf16[2,256,1536]{2,1,0:T(8,128)(2,1)S(1)}, u32[]{:S(2)}, u32[]{:S(2)}) %collective-permute-start.62) | collective-permute-done | bytes 1572896 | tf_op jit(solution)/shard_map/ppermute | solution.py:39
  520.0 3.8 fusion.27
  524.7 4.0 collective-permute-done.58
  532.4 5.8 copy.116
  539.8 3.5 pad_maximum_fusion.4
  555.8 19.7 %self_backward.1 = bf16[4,2,128,1152]{3,2,1,0:T(8,128)(2,1)} custom-call(f32[2,1,512]{2,1,0:T(1,128)} %compare_convert_fusion.ok_ref, f32[4,128,128]{2,1,0:T(8,128)} %concatenate.82.cos_ref, f32[4,128,128]{2,1,0:T(8,128)} %concatenate.83.up_ref, f32[4,128,128]{2,1,0:T(8,128)} %concatenate.84.down_ref, bf16[4,2,128,384]{3,2,1,0:T(8,128)(2,1)} %get-tuple-element.160.q_ref, ...), custom_call_target="tpu_custom_call" | custom-call | flops 4026531840 | bytes 3145728 | tf_op jit(solution)/shard_map/self_backward/pallas_call | solution.py:535
  575.5 7.1 convolution_convert_fusion
  586.5 5.9 convolution_convert_fusion.7
  592.4 8.8 %collective-permute-done.67 = bf16[4,64,3072]{2,1,0:T(8,128)(2,1)} collective-permute-done((bf16[4,64,3072]{2,1,0:T(8,128)(2,1)}, bf16[4,64,3072]{2,1,0:T(8,128)(2,1)}, u32[]{:S(2)}, u32[]{:S(2)}) %collective-permute-start.67) | collective-permute-done | bytes 1572896 | tf_op jit(solution)/shard_map/ppermute | solution.py:39
  610.6 4.4 all-to-all-start.4
  620.7 37.5 %collective-permute-done.75 = bf16[64,1536]{1,0:T(8,128)(2,1)S(1)} collective-permute-done((bf16[64,1536]{1,0:T(8,128)(2,1)S(1)}, bf16[64,1536]{1,0:T(8,128)(2,1)S(1)}, u32[]{:S(2)}, u32[]{:S(2)}) %collective-permute-start.75) | collective-permute-done | bytes 196640 | tf_op jit(solution)/shard_map/ppermute | solution.py:34
  663.0 3.7 fusion.8
  685.0 3.7 reshape.736
  704.0 3.7 all-to-all-start.6
  708.7 6.8 all-to-all-done.6
  722.2 3.5 all-to-all-start.5
  726.5 7.1 all-to-all-done.5
  (641 shorter events, 285.6 us)
Async XLA Ops:
  7.2 50.7 %all-gather.17.cloned.1.call-start = ((), (), s32[]{:S(2)}) async-start(), calls=%async_computation.20 | async-start | bytes 1474560 | tf_op jit(solution)/shard_map/all_gather | solution.py:155
  21.4 19.8 %collective-permute-start.11 = (bf16[48,3072]{1,0:T(8,128)(2,1)S(1)}, bf16[48,3072]{1,0:T(8,128)(2,1)S(1)}, u32[]{:S(2)}, u32[]{:S(2)}) collective-permute-start(bf16[48,3072]{1,0:T(8,128)(2,1)S(1)} %constant_dynamic-update-slice_fusion), channel_id=1, source_target_pairs={{0,1},{1,0},{2,3},{3,2},{4,5},{5,4},{6,7},{7,6},{8,9},{9,8},{10,11... | collective-permute-start | bytes 884744 | tf_op jit(solution)/shard_map/ppermute | solution.py:34
  34.1 50.7 %all-gather.9.cloned.1.call-start = ((), (), s32[]{:S(2)}) async-start(), calls=%async_computation.12 | async-start | bytes 1474560 | tf_op jit(solution)/shard_map/all_gather | solution.py:155
  41.1 109.6 %all-gather.19.cloned.1.call-start = ((), (), s32[]{:S(2)}) async-start(), calls=%async_computation.21 | async-start | bytes 3932160 | tf_op jit(solution)/shard_map/all_gather | solution.py:155
  59.0 38.2 %collective-permute-start.8 = (bf16[4,192,768]{2,1,0:T(8,128)(2,1)}, bf16[4,192,768]{2,1,0:T(8,128)(2,1)}, u32[]{:S(2)}, u32[]{:S(2)}) collective-permute-start(bf16[4,192,768]{2,1,0:T(8,128)(2,1)} %bitcast.458), channel_id=1, source_target_pairs={{0,4},{4,0},{8,12},{12,8},{16,20},{20,16},{24,28},{28,24},{1,5},{5... | collective-permute-start | bytes 3538952 | tf_op jit(solution)/shard_map/ppermute | solution.py:39
  67.6 29.1 %collective-permute-start.2 = (bf16[256,1536]{1,0:T(8,128)(2,1)S(1)}, bf16[256,1536]{1,0:T(8,128)(2,1)S(1)}, u32[]{:S(2)}, u32[]{:S(2)}) collective-permute-start(bf16[256,1536]{1,0:T(8,128)(2,1)S(1)} %bitcast.367), channel_id=1, source_target_pairs={{0,2},{1,3},{2,0},{3,1},{4,6},{5,7},{6,4},{7,5},{8,10},{9,11},{10,... | collective-permute-start | bytes 2359304 | tf_op jit(solution)/shard_map/ppermute | solution.py:34
  68.5 48.5 %collective-permute-start.1 = (bf16[256,1536]{1,0:T(8,128)(2,1)S(1)}, bf16[256,1536]{1,0:T(8,128)(2,1)}, u32[]{:S(2)}, u32[]{:S(2)}) collective-permute-start(bf16[256,1536]{1,0:T(8,128)(2,1)S(1)} %bitcast.368), channel_id=1, source_target_pairs={{0,1},{1,0},{2,3},{3,2},{4,5},{5,4},{6,7},{7,6},{8,9},{9,8},{10,11... | collective-permute-start | bytes 2359304 | tf_op jit(solution)/shard_map/ppermute | solution.py:34
  84.8 28.9 %collective-permute-start.9 = (bf16[4,192,768]{2,1,0:T(8,128)(2,1)}, bf16[4,192,768]{2,1,0:T(8,128)(2,1)}, u32[]{:S(2)}, u32[]{:S(2)}) collective-permute-start(bf16[4,192,768]{2,1,0:T(8,128)(2,1)} %all-gather.9.cloned.1.call-done), channel_id=1, source_target_pairs={{0,4},{4,0},{8,12},{12,8},{16,20},{20,16},{24,28},{28,24},{1,5},{5... | collective-permute-start | bytes 3538952 | tf_op jit(solution)/shard_map/ppermute | solution.py:39
  91.4 41.1 %all-to-all-start.2 = ((bf16[4,48,4608]{2,1,0:T(8,128)(2,1)}), bf16[4,48,4608]{2,1,0:T(8,128)(2,1)}, u32[]{:S(2)}, u32[]{:S(2)}) async-start(bf16[4,48,4608]{2,1,0:T(8,128)(2,1)} %reshape.697), calls=%async_computation.2 | async-start | bytes 3538944 | tf_op jit(solution)/shard_map/all_to_all | solution.py:288
  95.8 90.5 %all-gather.11.cloned.1.call-start = ((), (), s32[]{:S(2)}) async-start(), calls=%async_computation.13 | async-start | bytes 1474560 | tf_op jit(solution)/shard_map/all_gather | solution.py:155
  96.4 188.4 %all-gather.13.cloned.1.call-start = ((), (), s32[]{:S(2)}) async-start(), calls=%async_computation.14 | async-start | bytes 5898240 | tf_op jit(solution)/shard_map/all_gather | solution.py:243
  96.7 20.3 %collective-permute-start.3 = (bf16[256,1536]{1,0:T(8,128)(2,1)S(1)}, bf16[256,1536]{1,0:T(8,128)(2,1)S(1)}, u32[]{:S(2)}, u32[]{:S(2)}) collective-permute-start(bf16[256,1536]{1,0:T(8,128)(2,1)S(1)} %collective-permute-done.2), channel_id=1, source_target_pairs={{0,1},{1,0},{2,3},{3,2},{4,5},{5,4},{6,7},{7,6},{8,9},{9,8},{10,11... | collective-permute-start | bytes 2359304 | tf_op jit(solution)/shard_map/ppermute | solution.py:34
  162.8 22.1 %collective-permute-start.10 = (bf16[192,2304]{1,0:T(8,128)(2,1)S(1)}, bf16[192,2304]{1,0:T(8,128)(2,1)S(1)}, u32[]{:S(2)}, u32[]{:S(2)}) collective-permute-start(bf16[192,2304]{1,0:T(8,128)(2,1)S(1)} %bitcast.462), channel_id=1, source_target_pairs={{0,4},{4,0},{8,12},{12,8},{16,20},{20,16},{24,28},{28,24},{1,5},{5... | collective-permute-start | bytes 2654216 | tf_op jit(solution)/shard_map/ppermute | solution.py:39
  164.9 22.4 %collective-permute-start.15 = (bf16[256,1536]{1,0:T(8,128)(2,1)S(1)}, bf16[256,1536]{1,0:T(8,128)(2,1)S(1)}, u32[]{:S(2)}, u32[]{:S(2)}) collective-permute-start(bf16[256,1536]{1,0:T(8,128)(2,1)S(1)} %get-tuple-element.234), channel_id=1, source_target_pairs={{0,1},{1,0},{2,3},{3,2},{4,5},{5,4},{6,7},{7,6},{8,9},{9,8},{10,11... | collective-permute-start | bytes 2359304 | tf_op jit(solution)/shard_map/ppermute | solution.py:34
  166.2 20.1 %collective-permute-start.17 = (bf16[256,1536]{1,0:T(8,128)(2,1)}, bf16[256,1536]{1,0:T(8,128)(2,1)S(1)}, u32[]{:S(2)}, u32[]{:S(2)}) collective-permute-start(bf16[256,1536]{1,0:T(8,128)(2,1)} %add_convert_fusion.5), channel_id=1, source_target_pairs={{0,2},{1,3},{2,0},{3,1},{4,6},{5,7},{6,4},{7,5},{8,10},{9,11},{10,... | collective-permute-start | bytes 2359304 | tf_op jit(solution)/shard_map/ppermute | solution.py:34
  190.3 27.8 %collective-permute-start.20 = (bf16[4,192,768]{2,1,0:T(8,128)(2,1)}, bf16[4,192,768]{2,1,0:T(8,128)(2,1)S(1)}, u32[]{:S(2)}, u32[]{:S(2)}) collective-permute-start(bf16[4,192,768]{2,1,0:T(8,128)(2,1)} %all-gather.11.cloned.1.call-done), channel_id=1, source_target_pairs={{0,4},{4,0},{8,12},{12,8},{16,20},{20,16},{24,28},{28,24},{1,5},{5... | collective-permute-start | bytes 3538952 | tf_op jit(solution)/shard_map/ppermute | solution.py:39
  193.4 23.7 %collective-permute-start.19 = (bf16[256,1536]{1,0:T(8,128)(2,1)}, bf16[256,1536]{1,0:T(8,128)(2,1)}, u32[]{:S(2)}, u32[]{:S(2)}) collective-permute-start(bf16[256,1536]{1,0:T(8,128)(2,1)} %multiply_convert_fusion.5), channel_id=1, source_target_pairs={{0,2},{1,3},{2,0},{3,1},{4,6},{5,7},{6,4},{7,5},{8,10},{9,11},{10,... | collective-permute-start | bytes 2359304 | tf_op jit(solution)/shard_map/ppermute | solution.py:34
  195.3 163.5 %all-gather.15.cloned.1.call-start = ((), (), s32[]{:S(2)}) async-start(), calls=%async_computation.15 | async-start | bytes 2949120 | tf_op jit(solution)/shard_map/all_gather | solution.py:243
  195.3 21.3 %collective-permute-start.23 = (bf16[64,1536]{1,0:T(8,128)(2,1)S(1)}, bf16[64,1536]{1,0:T(8,128)(2,1)S(1)}, u32[]{:S(2)}, u32[]{:S(2)}) collective-permute-start(bf16[64,1536]{1,0:T(8,128)(2,1)S(1)} %bitcast.482), channel_id=1, source_target_pairs={{0,2},{1,3},{2,0},{3,1},{4,6},{5,7},{6,4},{7,5},{8,10},{9,11},{10,... | collective-permute-start | bytes 589832 | tf_op jit(solution)/shard_map/ppermute | solution.py:34
  196.8 22.1 %collective-permute-start.22 = (bf16[64,1536]{1,0:T(8,128)(2,1)S(1)}, bf16[64,1536]{1,0:T(8,128)(2,1)S(1)}, u32[]{:S(2)}, u32[]{:S(2)}) collective-permute-start(bf16[64,1536]{1,0:T(8,128)(2,1)S(1)} %bitcast.483), channel_id=1, source_target_pairs={{0,1},{1,0},{2,3},{3,2},{4,5},{5,4},{6,7},{7,6},{8,9},{9,8},{10,11... | collective-permute-start | bytes 589832 | tf_op jit(solution)/shard_map/ppermute | solution.py:34
  225.5 19.7 %collective-permute-start.25 = (bf16[256,1536]{1,0:T(8,128)(2,1)S(1)}, bf16[256,1536]{1,0:T(8,128)(2,1)}, u32[]{:S(2)}, u32[]{:S(2)}) collective-permute-start(bf16[256,1536]{1,0:T(8,128)(2,1)S(1)} %bitcast.432), channel_id=1, source_target_pairs={{0,2},{1,3},{2,0},{3,1},{4,6},{5,7},{6,4},{7,5},{8,10},{9,11},{10,... | collective-permute-start | bytes 2359304 | tf_op jit(solution)/shard_map/ppermute | solution.py:34
  289.8 20.1 %collective-permute-start.30 = (bf16[256,1536]{1,0:T(8,128)(2,1)}, bf16[256,1536]{1,0:T(8,128)(2,1)}, u32[]{:S(2)}, u32[]{:S(2)}) collective-permute-start(bf16[256,1536]{1,0:T(8,128)(2,1)} %get-tuple-element.208), channel_id=1, source_target_pairs={{0,1},{1,0},{2,3},{3,2},{4,5},{5,4},{6,7},{7,6},{8,9},{9,8},{10,11... | collective-permute-start | bytes 2359304 | tf_op jit(solution)/shard_map/ppermute | solution.py:34
  290.7 143.6 %reduce-scatter.8.cloned.1.call-start = ((), (), s32[]{:S(2)}) async-start(), calls=%async_computation.16 | async-start | bytes 2949120 | tf_op jit(solution)/shard_map/reduce_scatter | solution.py:249
  388.3 155.1 %reduce-scatter.10.cloned.1.call-start = ((), (), s32[]{:S(2)}) async-start(), calls=%async_computation.17 | async-start | bytes 5898240 | tf_op jit(solution)/shard_map/reduce_scatter | solution.py:249
  397.8 32.5 %collective-permute-start.45 = (bf16[256,1536]{1,0:T(8,128)(2,1)S(1)}, bf16[256,1536]{1,0:T(8,128)(2,1)}, u32[]{:S(2)}, u32[]{:S(2)}) collective-permute-start(bf16[256,1536]{1,0:T(8,128)(2,1)S(1)} %get-tuple-element.221), channel_id=1, source_target_pairs={{0,1},{1,0},{2,3},{3,2},{4,5},{5,4},{6,7},{7,6},{8,9},{9,8},{10,11... | collective-permute-start | bytes 2359304 | tf_op jit(solution)/shard_map/ppermute | solution.py:34
  409.7 19.7 %collective-permute-start.50 = (bf16[256,1536]{1,0:T(8,128)(2,1)}, bf16[256,1536]{1,0:T(8,128)(2,1)S(1)}, u32[]{:S(2)}, u32[]{:S(2)}) collective-permute-start(bf16[256,1536]{1,0:T(8,128)(2,1)} %pad_maximum_fusion.17), channel_id=1, source_target_pairs={{0,2},{1,3},{2,0},{3,1},{4,6},{5,7},{6,4},{7,5},{8,10},{9,11},{10,... | collective-permute-start | bytes 2359304 | tf_op jit(solution)/shard_map/ppermute | solution.py:34
  441.4 218.7 %reduce-scatter.16.cloned.1.call-start = ((), (), s32[]{:S(2)}) async-start(), calls=%async_computation.22 | async-start | bytes 4423680
  461.0 20.4 %collective-permute-start.60 = (bf16[256,1536]{1,0:T(8,128)(2,1)}, bf16[256,1536]{1,0:T(8,128)(2,1)S(1)}, u32[]{:S(2)}, u32[]{:S(2)}) collective-permute-start(bf16[256,1536]{1,0:T(8,128)(2,1)} %get-tuple-element.217), channel_id=1, source_target_pairs={{0,1},{1,0},{2,3},{3,2},{4,5},{5,4},{6,7},{7,6},{8,9},{9,8},{10,11... | collective-permute-start | bytes 2359304 | tf_op jit(solution)/shard_map/ppermute | solution.py:34
  461.5 19.9 %collective-permute-start.61 = (bf16[256,1536]{1,0:T(8,128)(2,1)}, bf16[256,1536]{1,0:T(8,128)(2,1)}, u32[]{:S(2)}, u32[]{:S(2)}) collective-permute-start(bf16[256,1536]{1,0:T(8,128)(2,1)} %get-tuple-element.216), channel_id=1, source_target_pairs={{0,1},{1,0},{2,3},{3,2},{4,5},{5,4},{6,7},{7,6},{8,9},{9,8},{10,11... | collective-permute-start | bytes 2359304 | tf_op jit(solution)/shard_map/ppermute | solution.py:34
  461.5 49.6 %collective-permute-start.59 = (bf16[256,1536]{1,0:T(8,128)(2,1)}, bf16[256,1536]{1,0:T(8,128)(2,1)}, u32[]{:S(2)}, u32[]{:S(2)}) collective-permute-start(bf16[256,1536]{1,0:T(8,128)(2,1)} %get-tuple-element.218), channel_id=1, source_target_pairs={{0,1},{1,0},{2,3},{3,2},{4,5},{5,4},{6,7},{7,6},{8,9},{9,8},{10,11... | collective-permute-start | bytes 2359304 | tf_op jit(solution)/shard_map/ppermute | solution.py:34
  462.0 49.1 %collective-permute-start.63 = (bf16[256,1536]{1,0:T(8,128)(2,1)}, bf16[256,1536]{1,0:T(8,128)(2,1)}, u32[]{:S(2)}, u32[]{:S(2)}) collective-permute-start(bf16[256,1536]{1,0:T(8,128)(2,1)} %get-tuple-element.215), channel_id=1, source_target_pairs={{0,1},{1,0},{2,3},{3,2},{4,5},{5,4},{6,7},{7,6},{8,9},{9,8},{10,11... | collective-permute-start | bytes 2359304 | tf_op jit(solution)/shard_map/ppermute | solution.py:34
  483.6 36.4 %collective-permute-start.62 = (bf16[2,256,1536]{2,1,0:T(8,128)(2,1)S(1)}, bf16[2,256,1536]{2,1,0:T(8,128)(2,1)S(1)}, u32[]{:S(2)}, u32[]{:S(2)}) collective-permute-start(bf16[2,256,1536]{2,1,0:T(8,128)(2,1)S(1)} %pad_maximum_fusion.12), channel_id=1, source_target_pairs={{0,4},{4,0},{8,12},{12,8},{16,20},{20,16},{24,28},{28,24},{1,5},{5... | collective-permute-start | bytes 4718600 | tf_op jit(solution)/shard_map/ppermute | solution.py:39
  485.1 21.7 %collective-permute-start.55 = (bf16[256,1536]{1,0:T(8,128)(2,1)S(1)}, bf16[256,1536]{1,0:T(8,128)(2,1)S(1)}, u32[]{:S(2)}, u32[]{:S(2)}) collective-permute-start(bf16[256,1536]{1,0:T(8,128)(2,1)S(1)} %get-tuple-element.230), channel_id=1, source_target_pairs={{0,1},{1,0},{2,3},{3,2},{4,5},{5,4},{6,7},{7,6},{8,9},{9,8},{10,11... | collective-permute-start | bytes 2359304 | tf_op jit(solution)/shard_map/ppermute | solution.py:34
  487.0 19.8 %collective-permute-start.57 = (bf16[256,1536]{1,0:T(8,128)(2,1)S(1)}, bf16[256,1536]{1,0:T(8,128)(2,1)S(1)}, u32[]{:S(2)}, u32[]{:S(2)}) collective-permute-start(bf16[256,1536]{1,0:T(8,128)(2,1)S(1)} %add_convert_fusion.2), channel_id=1, source_target_pairs={{0,2},{1,3},{2,0},{3,1},{4,6},{5,7},{6,4},{7,5},{8,10},{9,11},{10,... | collective-permute-start | bytes 2359304 | tf_op jit(solution)/shard_map/ppermute | solution.py:34
  529.4 90.0 %collective-permute-start.74 = (bf16[64,1536]{1,0:T(8,128)(2,1)}, bf16[64,1536]{1,0:T(8,128)(2,1)}, u32[]{:S(2)}, u32[]{:S(2)}) collective-permute-start(bf16[64,1536]{1,0:T(8,128)(2,1)} %get-tuple-element.255), channel_id=1, source_target_pairs={{0,1},{1,0},{2,3},{3,2},{4,5},{5,4},{6,7},{7,6},{8,9},{9,8},{10,11... | collective-permute-start | bytes 589832 | tf_op jit(solution)/shard_map/ppermute | solution.py:34
  530.0 128.3 %collective-permute-start.73 = (bf16[64,1536]{1,0:T(8,128)(2,1)S(1)}, bf16[64,1536]{1,0:T(8,128)(2,1)}, u32[]{:S(2)}, u32[]{:S(2)}) collective-permute-start(bf16[64,1536]{1,0:T(8,128)(2,1)S(1)} %get-tuple-element.254), channel_id=1, source_target_pairs={{0,1},{1,0},{2,3},{3,2},{4,5},{5,4},{6,7},{7,6},{8,9},{9,8},{10,11... | collective-permute-start | bytes 589832 | tf_op jit(solution)/shard_map/ppermute | solution.py:34
  538.2 124.2 %reduce-scatter.12.cloned.1.call-start = ((), (), s32[]{:S(2)}) async-start(), calls=%async_computation.18 | async-start | bytes 1966080 | tf_op jit(solution)/shard_map/reduce_scatter | solution.py:207
  538.3 124.1 %collective-permute-start.71 = (bf16[256,1536]{1,0:T(8,128)(2,1)}, bf16[256,1536]{1,0:T(8,128)(2,1)}, u32[]{:S(2)}, u32[]{:S(2)}) collective-permute-start(bf16[256,1536]{1,0:T(8,128)(2,1)} %get-tuple-element.182), channel_id=1, source_target_pairs={{0,2},{1,3},{2,0},{3,1},{4,6},{5,7},{6,4},{7,5},{8,10},{9,11},{10,... | collective-permute-start | bytes 2359304 | tf_op jit(solution)/shard_map/ppermute | solution.py:34
  545.5 30.0 %collective-permute-start.66 = (bf16[192,2304]{1,0:T(8,128)(2,1)S(1)}, bf16[192,2304]{1,0:T(8,128)(2,1)}, u32[]{:S(2)}, u32[]{:S(2)}) collective-permute-start(bf16[192,2304]{1,0:T(8,128)(2,1)S(1)} %dynamic-slice_bitcast_fusion.3), channel_id=1, source_target_pairs={{0,4},{4,0},{8,12},{12,8},{16,20},{20,16},{24,28},{28,24},{1,5},{5... | collective-permute-start | bytes 2654216 | tf_op jit(solution)/shard_map/ppermute | solution.py:39
  554.1 47.0 %collective-permute-start.67 = (bf16[4,64,3072]{2,1,0:T(8,128)(2,1)}, bf16[4,64,3072]{2,1,0:T(8,128)(2,1)}, u32[]{:S(2)}, u32[]{:S(2)}) collective-permute-start(bf16[4,64,3072]{2,1,0:T(8,128)(2,1)} %get-tuple-element.176), channel_id=1, source_target_pairs={{0,4},{4,0},{8,12},{12,8},{16,20},{20,16},{24,28},{28,24},{1,5},{5... | collective-permute-start | bytes 4718600 | tf_op jit(solution)/shard_map/ppermute | solution.py:39
  608.1 54.2 %collective-permute-start.70 = (bf16[4,192,1152]{2,1,0:T(8,128)(2,1)}, bf16[4,192,1152]{2,1,0:T(8,128)(2,1)}, u32[]{:S(2)}, u32[]{:S(2)}) collective-permute-start(bf16[4,192,1152]{2,1,0:T(8,128)(2,1)} %dynamic-slice_bitcast_fusion), channel_id=1, source_target_pairs={{0,4},{4,0},{8,12},{12,8},{16,20},{20,16},{24,28},{28,24},{1,5},{5... | collective-permute-start | bytes 5308424 | tf_op jit(solution)/shard_map/ppermute | solution.py:39
  610.6 51.7 %all-to-all-start.4 = ((bf16[4,48,4608]{2,1,0:T(8,128)(2,1)}), bf16[4,48,4608]{2,1,0:T(8,128)(2,1)}, u32[]{:S(2)}, u32[]{:S(2)}) async-start(bf16[4,48,4608]{2,1,0:T(8,128)(2,1)} %bitcast.379), calls=%async_computation.7 | async-start | bytes 3538944 | tf_op jit(solution)/shard_map/all_to_all | solution.py:294
  615.1 107.1 %reduce-scatter.14.cloned.1.call-start = ((), (), s32[]{:S(2)}) async-start(), calls=%async_computation.19 | async-start | bytes 2211840 | tf_op jit(solution)/shard_map/reduce_scatter | solution.py:207
  617.6 44.8 %collective-permute-start.69 = (bf16[256,1536]{1,0:T(8,128)(2,1)}, bf16[256,1536]{1,0:T(8,128)(2,1)S(1)}, u32[]{:S(2)}, u32[]{:S(2)}) collective-permute-start(bf16[256,1536]{1,0:T(8,128)(2,1)} %fusion.26), channel_id=1, source_target_pairs={{0,2},{1,3},{2,0},{3,1},{4,6},{5,7},{6,4},{7,5},{8,10},{9,11},{10,... | collective-permute-start | bytes 2359304 | tf_op jit(solution)/shard_map/ppermute | solution.py:34
  620.6 37.7 %collective-permute-start.75 = (bf16[64,1536]{1,0:T(8,128)(2,1)S(1)}, bf16[64,1536]{1,0:T(8,128)(2,1)S(1)}, u32[]{:S(2)}, u32[]{:S(2)}) collective-permute-start(bf16[64,1536]{1,0:T(8,128)(2,1)S(1)} %add_convert_fusion.6), channel_id=1, source_target_pairs={{0,2},{1,3},{2,0},{3,1},{4,6},{5,7},{6,4},{7,5},{8,10},{9,11},{10,... | collective-permute-start | bytes 589832 | tf_op jit(solution)/shard_map/ppermute | solution.py:34
  662.4 45.3 %collective-permute-start.82 = (bf16[64,3072]{1,0:T(8,128)(2,1)}, bf16[64,3072]{1,0:T(8,128)(2,1)}, u32[]{:S(2)}, u32[]{:S(2)}) collective-permute-start(bf16[64,3072]{1,0:T(8,128)(2,1)} %reduce-scatter.12.cloned.1.call-done), channel_id=1, source_target_pairs={{0,2},{1,3},{2,0},{3,1},{4,6},{5,7},{6,4},{7,5},{8,10},{9,11},{10,... | collective-permute-start | bytes 1179656 | tf_op jit(solution)/shard_map/ppermute | solution.py:34
  662.8 57.7 %collective-permute-start.81 = (bf16[64,3072]{1,0:T(8,128)(2,1)}, bf16[64,3072]{1,0:T(8,128)(2,1)}, u32[]{:S(2)}, u32[]{:S(2)}) collective-permute-start(bf16[64,3072]{1,0:T(8,128)(2,1)} %reduce-scatter.12.cloned.1.call-done), channel_id=1, source_target_pairs={{0,1},{1,0},{2,3},{3,2},{4,5},{5,4},{6,7},{7,6},{8,9},{9,8},{10,11... | collective-permute-start | bytes 1179656 | tf_op jit(solution)/shard_map/ppermute | solution.py:34
  669.2 32.9 %collective-permute-start.84 = (bf16[192,1152]{1,0:T(8,128)(2,1)}, bf16[192,1152]{1,0:T(8,128)(2,1)}, u32[]{:S(2)}, u32[]{:S(2)}) collective-permute-start(bf16[192,1152]{1,0:T(8,128)(2,1)} %dynamic-slice_bitcast_fusion.4), channel_id=1, source_target_pairs={{0,4},{4,0},{8,12},{12,8},{16,20},{20,16},{24,28},{28,24},{1,5},{5... | collective-permute-start | bytes 1327112 | tf_op jit(solution)/shard_map/ppermute | solution.py:39
  (155 other events, 1557.6 us)
Sparse Core Ops, SparseCore 0:
  21.0 30.9 all-gather.16
  54.1 30.6 all-gather.8
  87.0 62.5 all-gather.18
  151.0 28.8 all-gather.10
  195.4 89.4 all-gather.12
  290.8 46.7 all-gather.14
  388.4 45.8 reduce-scatter.7
  441.5 83.7 reduce-scatter.9
  538.3 65.9 reduce-scatter.15
  606.4 35.6 reduce-scatter.11
  666.9 39.0 reduce-scatter.13

commit v5 on v4

--- a/solution.py
+++ b/solution.py
@@ -5,6 +5,7 @@
 import jax.numpy as jnp
 from jax import lax
 from jax.experimental import pallas as pl
+from jax.experimental.layout import Layout, with_layout_constraint
 from jax.experimental.pallas import tpu as pltpu
 from jax.sharding import PartitionSpec as P
 
@@ -739,6 +740,7 @@
     d_ckv = d_ckv.reshape(n * batch * cond_dev, 2 * mine)
     partial = mm_t(d_cq, cq_w).astype(BF).reshape(n, rows, width)
     grad_cross = jnp.concatenate([t_mm(normed_two, d_cq), t_mm(cond_all, d_ckv)], axis=1).astype(BF)
+    grad_cross = with_layout_constraint(grad_cross, Layout(major_to_minor=(0, 1)))
     d_norm2, grad_cross = scatter_seq(partial, (grad_cross,))
     cross_both = reduce_hidden(grad_cross)
     partial = mm_t(d_ckv, ckv_w).astype(BF).reshape(n, batch * cond_dev, width)

time: 755 us -> 755 us (level)
    unnamed x238 -> x239, local copies, waits for them, and re-layouts: 33.3 us -> 26.8 us
where the time goes in v5:
time: 755 us; the launch traced here: 745 us
  waiting for transfers between devices  255 us (34%)
  matrix products  121 us (16%)
  other arithmetic  109 us (14%)
  local copies, waits for them, and re-layouts  96.1 us (13%)
  starting transfers between devices  83.9 us (11%)
  Pallas kernels  53.7 us (7%)
  between operations  16.3 us (2%)
  blocking collectives  10.5 us (1%)
    ppermute x63, waiting for transfers between devices, seq_swap(): return lax.ppermute(x, 'seq', [(i, i ^ mask) for i in range(n)])  158 us
    ppermute x22, waiting for transfers between devices, dp_swap(): return lax.ppermute(x, 'dp', [(i, i ^ mask) for i in range(n)])  59 us
    dot_general x9, matrix products, mm(): return jnp.dot(left, right, preferred_element_type=F32)  51.8 us
    dot_general x7, matrix products, mm_t(): lax.dot_general(left, right, (((1,), (1,)), ((), ())), preferred_element_...  37.1 us
    dot_general x7, matrix products, t_mm(): lax.dot_general(left, right, (((0,), (0,)), ((), ())), preferred_element_...  31.8 us
    ppermute x63, starting transfers between devices, seq_swap(): return lax.ppermute(x, 'seq', [(i, i ^ mask) for i in range(n)])  30.4 us
    ppermute x22, starting transfers between devices, dp_swap(): return lax.ppermute(x, 'dp', [(i, i ^ mask) for i in range(n)])  29.2 us
    unnamed x239, local copies, waits for them, and re-layouts  26.8 us
  transfers between devices with their start and end apart: 102, of which 33 were waited for; matrix products, arithmetic and copies ran while one was open for 36% of the time, Pallas kernels for 7%

profile of v5, /device:TPU:0, one launch (start us, length us, event | category | flops | bytes accessed | tf_op | source)
XLA Modules:
  0.0 744.6 jit_solution(16974903543594892081)
XLA Ops:
  10.3 10.5 %all_to_all.35 = bf16[4,48,768]{2,1,0:T(8,128)(2,1)} all-to-all(bf16[4,48,768]{2,1,0:T(8,128)(2,1)S(1)} %pad_maximum_fusion.19), channel_id=1, replica_groups=mesh['dp'=8,'seq'=4] {'seq'}, dimensions={0} | all-to-all | bytes 589824 | tf_op jit(solution)/shard_map/all_to_all | solution.py:289
  22.5 7.3 collective-permute-done.12
  30.6 3.5 all-to-all-start.1
  34.1 6.2 all-to-all-done.1
  43.5 8.9 %collective-permute-done.14 = bf16[64,3072]{1,0:T(8,128)(2,1)S(1)} collective-permute-done((bf16[64,3072]{1,0:T(8,128)(2,1)S(1)}, bf16[64,3072]{1,0:T(8,128)(2,1)S(1)}, u32[]{:S(2)}, u32[]{:S(2)}) %collective-permute-start.14) | collective-permute-done | bytes 393248 | tf_op jit(solution)/shard_map/ppermute | solution.py:40
  77.8 4.1 all-to-all-start.3
  91.4 4.5 all-to-all-start.2
  100.8 12.9 %collective-permute-done.9 = bf16[4,192,768]{2,1,0:T(8,128)(2,1)} collective-permute-done((bf16[4,192,768]{2,1,0:T(8,128)(2,1)}, bf16[4,192,768]{2,1,0:T(8,128)(2,1)}, u32[]{:S(2)}, u32[]{:S(2)}) %collective-permute-start.9) | collective-permute-done | bytes 1179680 | tf_op jit(solution)/shard_map/ppermute | solution.py:40
  122.1 4.6 fusion.33.v_ref
  126.8 5.6 fusion.62.q_ref.k_ref
  134.9 15.8 %self_forward.1 = (bf16[4,2,128,384]{3,2,1,0:T(8,128)(2,1)}, bf16[4,2,128,384]{3,2,1,0:T(8,128)(2,1)}, bf16[4,2,128,384]{3,2,1,0:T(8,128)(2,1)}, bf16[4,2,128,384]{3,2,1,0:T(8,128)(2,1)}) custom-call(f32[2,1,512]{2,1,0:T(1,128)} %compare_convert_fusion.ok_ref, f32[4,128,128]{2,1,0:T(8,128)} %concatenate.82.cos_ref, f32[4,128,128]{2,1,0:T(8,128)} %concatenate.83.up_ref, ...), custom_call_target="tpu_custom_call" | custom-call | flops 1610612736 | bytes 3145728 | tf_op jit(solution)/shard_map/self_forward/pallas_call | solution.py:520
  159.1 3.6 constant_dynamic-slice_fusion.4
  167.0 17.9 %collective-permute-done.10 = bf16[192,2304]{1,0:T(8,128)(2,1)S(1)} collective-permute-done((bf16[192,2304]{1,0:T(8,128)(2,1)S(1)}, bf16[192,2304]{1,0:T(8,128)(2,1)S(1)}, u32[]{:S(2)}, u32[]{:S(2)}) %collective-permute-start.10) | collective-permute-done | bytes 884768 | tf_op jit(solution)/shard_map/ppermute | solution.py:40
  196.6 19.8 %collective-permute-done.23 = bf16[64,1536]{1,0:T(8,128)(2,1)S(1)} collective-permute-done((bf16[64,1536]{1,0:T(8,128)(2,1)S(1)}, bf16[64,1536]{1,0:T(8,128)(2,1)S(1)}, u32[]{:S(2)}, u32[]{:S(2)}) %collective-permute-start.23) | collective-permute-done | bytes 196640 | tf_op jit(solution)/shard_map/ppermute | solution.py:35
  231.3 7.8 %cross_forward.1 = bf16[4,2,128,384]{3,2,1,0:T(8,128)(2,1)} custom-call(f32[2,1,128]{2,1,0:T(1,128)} %compare_convert_fusion.1.ok_ref, bf16[4,2,128,384]{3,2,1,0:T(8,128)(2,1)} %bitcast.469, bf16[4,2,32,768]{3,2,1,0:T(8,128)(2,1)} %bitcast.449, bf16[4,2,32,768]{3,2,1,0:T(8,128)(2,1)} %bitcast.450), custom_call_target="tpu_custom_call" | custom-call | flops 402653184 | bytes 3145728 | tf_op jit(solution)/shard_map/cross_forward/pallas_call | solution.py:550
  239.1 5.9 collective-permute-done.25
  245.5 3.6 convolution_convert_fusion.5
  253.0 18.4 %collective-permute-done.29 = bf16[256,1536]{1,0:T(8,128)(2,1)S(1)} collective-permute-done((bf16[256,1536]{1,0:T(8,128)(2,1)S(1)}, bf16[256,1536]{1,0:T(8,128)(2,1)S(1)}, u32[]{:S(2)}, u32[]{:S(2)}) %collective-permute-start.29) | collective-permute-done | bytes 786464 | tf_op jit(solution)/shard_map/ppermute | solution.py:35
  271.8 13.0 %all-gather.13.cloned.1.call-done = bf16[1536,1536]{1,0:T(8,128)(2,1)} async-done(((bf16[384,1536]{1,0:T(8,128)(2,1)}), bf16[1536,1536]{1,0:T(8,128)(2,1)}) %all-gather.13.cloned.1.call-update) | async-done | bytes 4718608 | tf_op jit(solution)/shard_map/all_gather | solution.py:244
  290.6 15.5 %collective-permute-done.31 = bf16[256,1536]{1,0:T(8,128)(2,1)S(1)} collective-permute-done((bf16[256,1536]{1,0:T(8,128)(2,1)}, bf16[256,1536]{1,0:T(8,128)(2,1)S(1)}, u32[]{:S(2)}, u32[]{:S(2)}) %collective-permute-start.31) | collective-permute-done | bytes 786464 | tf_op jit(solution)/shard_map/ppermute | solution.py:35
  312.9 3.5 collective-permute-done.35
  326.6 9.7 %fusion.12 = f32[2048,768]{1,0:T(8,128)} fusion(bf16[2048,1536]{1,0:T(8,128)(2,1)} %bitcast.489, bf16[1536,1536]{1,0:T(8,128)(2,1)} %all-gather.13.cloned.1.call-done), kind=kOutput, calls=%fused_computation.48 | convolution fusion | flops 4831838208 | bytes 14942208 | tf_op jit(solution)/shard_map/dot_general | solution.py:22
  340.3 10.4 %multiply_convert_fusion.2 = (bf16[2048,768]{1,0:T(8,128)(2,1)S(1)}, f32[2048,768]{1,0:T(8,128)}) fusion(f32[2048,768]{1,0:T(8,128)} %fusion.12, bf16[2048,1536]{1,0:T(8,128)(2,1)S(1)} %bitcast.492, bf16[1536,1536]{1,0:T(8,128)(2,1)S(1)} %bitcast.505), kind=kOutput, calls=%fused_computation.11 | convolution fusion | flops 4841275392 | bytes 24379392 | tf_op jit(solution)/shard_map/dot_general | solution.py:22
  352.2 6.4 convolution_convert_fusion.9
  358.7 11.8 %multiply_convert_fusion.1 = (bf16[2048,768]{1,0:T(8,128)(2,1)S(1)}, bf16[2048,768]{1,0:T(8,128)(2,1)S(1)}) fusion(f32[2048,768]{1,0:T(8,128)} %fusion.12, f32[2048,768]{1,0:T(8,128)} %get-tuple-element.282, bf16[2048,1536]{1,0:T(8,128)(2,1)} %bitcast.488, bf16[1536,768]{1,0:T(8,128)(2,1)} %all-gather.15.cloned.1.call-done), kind=kOutput, calls=%fused_computation.10 | convolution fusion | flops 4852285440 | bytes 27525120 | tf_op jit(solution)/shard_map/dot_general | solution.py:22
  370.5 14.5 %convolution_convert_fusion.2 = bf16[2048,1536]{1,0:T(8,128)(2,1)S(1)} fusion(bf16[1536,1536]{1,0:T(8,128)(2,1)} %all-gather.13.cloned.1.call-done, bf16[2048,768]{1,0:T(8,128)(2,1)S(1)} %get-tuple-element.212, bf16[2048,768]{1,0:T(8,128)(2,1)S(1)} %get-tuple-element.211), kind=kOutput, calls=%fused_computation.2 | convolution fusion | flops 9679405056 | bytes 17301504 | tf_op jit(solution)/shard_map/dot_general | solution.py:26
  397.7 7.2 convolution_convert_fusion.1
  411.2 11.7 %convolution_convert_fusion.3 = bf16[1536,1536]{1,0:T(8,128)(2,1)} fusion(bf16[2048,1536]{1,0:T(8,128)(2,1)S(1)} %bitcast.495, bf16[2048,1536]{1,0:T(8,128)(2,1)S(1)} %pad_maximum_fusion), kind=kOutput, calls=%fused_computation.3 | convolution fusion | flops 9666035712 | bytes 17301504 | tf_op jit(solution)/shard_map/dot_general | solution.py:30
  422.9 6.4 collective-permute-done.50
  444.8 11.8 %collective-permute-done.53 = bf16[256,1536]{1,0:T(8,128)(2,1)} collective-permute-done((bf16[256,1536]{1,0:T(8,128)(2,1)}, bf16[256,1536]{1,0:T(8,128)(2,1)}, u32[]{:S(2)}, u32[]{:S(2)}) %collective-permute-start.53) | collective-permute-done | bytes 786464 | tf_op jit(solution)/shard_map/ppermute | solution.py:35
  466.7 10.3 %cross_backward.1 = (bf16[4,2,128,384]{3,2,1,0:T(8,128)(2,1)}, bf16[4,2,32,768]{3,2,1,0:T(8,128)(2,1)}) custom-call(f32[2,1,128]{2,1,0:T(1,128)} %compare_convert_fusion.1.ok_ref, bf16[4,2,128,384]{3,2,1,0:T(8,128)(2,1)} %bitcast.470, bf16[4,2,32,768]{3,2,1,0:T(8,128)(2,1)} %bitcast.451, bf16[4,2,32,768]{3,2,1,0:T(8,128)(2,1)} %bitcast.452, ...), custom_call_target="tpu_custom_call" | custom-call | flops 1006632960 | bytes 3145728 | tf_op jit(solution)/shard_map/cross_backward/pallas_call | solution.py:564
  494.2 15.8 %collective-permute-done.57 = bf16[256,1536]{1,0:T(8,128)(2,1)} collective-permute-done((bf16[256,1536]{1,0:T(8,128)(2,1)}, bf16[256,1536]{1,0:T(8,128)(2,1)}, u32[]{:S(2)}, u32[]{:S(2)}) %collective-permute-start.57) | collective-permute-done | bytes 786464 | tf_op jit(solution)/shard_map/ppermute | solution.py:35
  513.1 3.8 fusion.64
  518.3 3.7 collective-permute-done.62
  522.0 4.3 fusion.27
  527.3 8.8 %collective-permute-done.58 = bf16[256,1536]{1,0:T(8,128)(2,1)S(1)} collective-permute-done((bf16[256,1536]{1,0:T(8,128)(2,1)}, bf16[256,1536]{1,0:T(8,128)(2,1)S(1)}, u32[]{:S(2)}, u32[]{:S(2)}) %collective-permute-start.58) | collective-permute-done | bytes 786464 | tf_op jit(solution)/shard_map/ppermute | solution.py:35
  557.2 19.8 %self_backward.1 = bf16[4,2,128,1152]{3,2,1,0:T(8,128)(2,1)} custom-call(f32[2,1,512]{2,1,0:T(1,128)} %compare_convert_fusion.ok_ref, f32[4,128,128]{2,1,0:T(8,128)} %concatenate.82.cos_ref, f32[4,128,128]{2,1,0:T(8,128)} %concatenate.83.up_ref, f32[4,128,128]{2,1,0:T(8,128)} %concatenate.84.down_ref, bf16[4,2,128,384]{3,2,1,0:T(8,128)(2,1)} %get-tuple-element.160.q_ref, ...), custom_call_target="tpu_custom_call" | custom-call | flops 4026531840 | bytes 3145728 | tf_op jit(solution)/shard_map/self_backward/pallas_call | solution.py:536
  577.0 7.1 convolution_convert_fusion
  588.1 5.8 convolution_convert_fusion.7
  593.9 9.7 %collective-permute-done.67 = bf16[4,64,3072]{2,1,0:T(8,128)(2,1)} collective-permute-done((bf16[4,64,3072]{2,1,0:T(8,128)(2,1)}, bf16[4,64,3072]{2,1,0:T(8,128)(2,1)}, u32[]{:S(2)}, u32[]{:S(2)}) %collective-permute-start.67) | collective-permute-done | bytes 1572896 | tf_op jit(solution)/shard_map/ppermute | solution.py:40
  612.5 4.5 all-to-all-start.4
  623.3 37.0 %collective-permute-done.75 = bf16[64,1536]{1,0:T(8,128)(2,1)S(1)} collective-permute-done((bf16[64,1536]{1,0:T(8,128)(2,1)S(1)}, bf16[64,1536]{1,0:T(8,128)(2,1)S(1)}, u32[]{:S(2)}, u32[]{:S(2)}) %collective-permute-start.75) | collective-permute-done | bytes 196640 | tf_op jit(solution)/shard_map/ppermute | solution.py:35
  662.8 3.7 fusion.8
  684.7 3.7 reshape.736
  703.3 3.5 all-to-all-start.6
  707.8 6.8 all-to-all-done.6
  721.3 3.7 all-to-all-start.5
  725.9 7.0 all-to-all-done.5
  (640 shorter events, 286.1 us)
Async XLA Ops:
  7.2 50.7 %all-gather.17.cloned.1.call-start = ((), (), s32[]{:S(2)}) async-start(), calls=%async_computation.21 | async-start | bytes 1474560 | tf_op jit(solution)/shard_map/all_gather | solution.py:156
  21.4 19.8 %collective-permute-start.11 = (bf16[48,3072]{1,0:T(8,128)(2,1)S(1)}, bf16[48,3072]{1,0:T(8,128)(2,1)S(1)}, u32[]{:S(2)}, u32[]{:S(2)}) collective-permute-start(bf16[48,3072]{1,0:T(8,128)(2,1)S(1)} %constant_dynamic-update-slice_fusion), channel_id=1, source_target_pairs={{0,1},{1,0},{2,3},{3,2},{4,5},{5,4},{6,7},{7,6},{8,9},{9,8},{10,11... | collective-permute-start | bytes 884744 | tf_op jit(solution)/shard_map/ppermute | solution.py:35
  34.1 50.7 %all-gather.9.cloned.1.call-start = ((), (), s32[]{:S(2)}) async-start(), calls=%async_computation.12 | async-start | bytes 1474560 | tf_op jit(solution)/shard_map/all_gather | solution.py:156
  41.1 109.6 %all-gather.19.cloned.1.call-start = ((), (), s32[]{:S(2)}) async-start(), calls=%async_computation.22 | async-start | bytes 3932160 | tf_op jit(solution)/shard_map/all_gather | solution.py:156
  59.0 38.2 %collective-permute-start.8 = (bf16[4,192,768]{2,1,0:T(8,128)(2,1)}, bf16[4,192,768]{2,1,0:T(8,128)(2,1)}, u32[]{:S(2)}, u32[]{:S(2)}) collective-permute-start(bf16[4,192,768]{2,1,0:T(8,128)(2,1)} %bitcast.453), channel_id=1, source_target_pairs={{0,4},{4,0},{8,12},{12,8},{16,20},{20,16},{24,28},{28,24},{1,5},{5... | collective-permute-start | bytes 3538952 | tf_op jit(solution)/shard_map/ppermute | solution.py:40
  67.6 29.1 %collective-permute-start.2 = (bf16[256,1536]{1,0:T(8,128)(2,1)S(1)}, bf16[256,1536]{1,0:T(8,128)(2,1)S(1)}, u32[]{:S(2)}, u32[]{:S(2)}) collective-permute-start(bf16[256,1536]{1,0:T(8,128)(2,1)S(1)} %bitcast.366), channel_id=1, source_target_pairs={{0,2},{1,3},{2,0},{3,1},{4,6},{5,7},{6,4},{7,5},{8,10},{9,11},{10,... | collective-permute-start | bytes 2359304 | tf_op jit(solution)/shard_map/ppermute | solution.py:35
  68.5 48.5 %collective-permute-start.1 = (bf16[256,1536]{1,0:T(8,128)(2,1)S(1)}, bf16[256,1536]{1,0:T(8,128)(2,1)}, u32[]{:S(2)}, u32[]{:S(2)}) collective-permute-start(bf16[256,1536]{1,0:T(8,128)(2,1)S(1)} %bitcast.367), channel_id=1, source_target_pairs={{0,1},{1,0},{2,3},{3,2},{4,5},{5,4},{6,7},{7,6},{8,9},{9,8},{10,11... | collective-permute-start | bytes 2359304 | tf_op jit(solution)/shard_map/ppermute | solution.py:35
  84.8 28.9 %collective-permute-start.9 = (bf16[4,192,768]{2,1,0:T(8,128)(2,1)}, bf16[4,192,768]{2,1,0:T(8,128)(2,1)}, u32[]{:S(2)}, u32[]{:S(2)}) collective-permute-start(bf16[4,192,768]{2,1,0:T(8,128)(2,1)} %all-gather.9.cloned.1.call-done), channel_id=1, source_target_pairs={{0,4},{4,0},{8,12},{12,8},{16,20},{20,16},{24,28},{28,24},{1,5},{5... | collective-permute-start | bytes 3538952 | tf_op jit(solution)/shard_map/ppermute | solution.py:40
  91.4 41.1 %all-to-all-start.2 = ((bf16[4,48,4608]{2,1,0:T(8,128)(2,1)}), bf16[4,48,4608]{2,1,0:T(8,128)(2,1)}, u32[]{:S(2)}, u32[]{:S(2)}) async-start(bf16[4,48,4608]{2,1,0:T(8,128)(2,1)} %reshape.697), calls=%async_computation.2 | async-start | bytes 3538944 | tf_op jit(solution)/shard_map/all_to_all | solution.py:289
  95.8 90.5 %all-gather.11.cloned.1.call-start = ((), (), s32[]{:S(2)}) async-start(), calls=%async_computation.13 | async-start | bytes 1474560 | tf_op jit(solution)/shard_map/all_gather | solution.py:156
  96.4 188.3 %all-gather.13.cloned.1.call-start = ((), (), s32[]{:S(2)}) async-start(), calls=%async_computation.14 | async-start | bytes 5898240 | tf_op jit(solution)/shard_map/all_gather | solution.py:244
  96.7 20.3 %collective-permute-start.3 = (bf16[256,1536]{1,0:T(8,128)(2,1)S(1)}, bf16[256,1536]{1,0:T(8,128)(2,1)S(1)}, u32[]{:S(2)}, u32[]{:S(2)}) collective-permute-start(bf16[256,1536]{1,0:T(8,128)(2,1)S(1)} %collective-permute-done.2), channel_id=1, source_target_pairs={{0,1},{1,0},{2,3},{3,2},{4,5},{5,4},{6,7},{7,6},{8,9},{9,8},{10,11... | collective-permute-start | bytes 2359304 | tf_op jit(solution)/shard_map/ppermute | solution.py:35
  162.8 22.1 %collective-permute-start.10 = (bf16[192,2304]{1,0:T(8,128)(2,1)S(1)}, bf16[192,2304]{1,0:T(8,128)(2,1)S(1)}, u32[]{:S(2)}, u32[]{:S(2)}) collective-permute-start(bf16[192,2304]{1,0:T(8,128)(2,1)S(1)} %bitcast.459), channel_id=1, source_target_pairs={{0,4},{4,0},{8,12},{12,8},{16,20},{20,16},{24,28},{28,24},{1,5},{5... | collective-permute-start | bytes 2654216 | tf_op jit(solution)/shard_map/ppermute | solution.py:40
  164.8 22.4 %collective-permute-start.15 = (bf16[256,1536]{1,0:T(8,128)(2,1)S(1)}, bf16[256,1536]{1,0:T(8,128)(2,1)S(1)}, u32[]{:S(2)}, u32[]{:S(2)}) collective-permute-start(bf16[256,1536]{1,0:T(8,128)(2,1)S(1)} %get-tuple-element.234), channel_id=1, source_target_pairs={{0,1},{1,0},{2,3},{3,2},{4,5},{5,4},{6,7},{7,6},{8,9},{9,8},{10,11... | collective-permute-start | bytes 2359304 | tf_op jit(solution)/shard_map/ppermute | solution.py:35
  166.2 20.1 %collective-permute-start.17 = (bf16[256,1536]{1,0:T(8,128)(2,1)}, bf16[256,1536]{1,0:T(8,128)(2,1)S(1)}, u32[]{:S(2)}, u32[]{:S(2)}) collective-permute-start(bf16[256,1536]{1,0:T(8,128)(2,1)} %add_convert_fusion.5), channel_id=1, source_target_pairs={{0,2},{1,3},{2,0},{3,1},{4,6},{5,7},{6,4},{7,5},{8,10},{9,11},{10,... | collective-permute-start | bytes 2359304 | tf_op jit(solution)/shard_map/ppermute | solution.py:35
  190.2 27.8 %collective-permute-start.20 = (bf16[4,192,768]{2,1,0:T(8,128)(2,1)}, bf16[4,192,768]{2,1,0:T(8,128)(2,1)S(1)}, u32[]{:S(2)}, u32[]{:S(2)}) collective-permute-start(bf16[4,192,768]{2,1,0:T(8,128)(2,1)} %all-gather.11.cloned.1.call-done), channel_id=1, source_target_pairs={{0,4},{4,0},{8,12},{12,8},{16,20},{20,16},{24,28},{28,24},{1,5},{5... | collective-permute-start | bytes 3538952 | tf_op jit(solution)/shard_map/ppermute | solution.py:40
  193.2 23.7 %collective-permute-start.19 = (bf16[256,1536]{1,0:T(8,128)(2,1)}, bf16[256,1536]{1,0:T(8,128)(2,1)}, u32[]{:S(2)}, u32[]{:S(2)}) collective-permute-start(bf16[256,1536]{1,0:T(8,128)(2,1)} %multiply_convert_fusion.5), channel_id=1, source_target_pairs={{0,2},{1,3},{2,0},{3,1},{4,6},{5,7},{6,4},{7,5},{8,10},{9,11},{10,... | collective-permute-start | bytes 2359304 | tf_op jit(solution)/shard_map/ppermute | solution.py:35
  195.1 163.5 %all-gather.15.cloned.1.call-start = ((), (), s32[]{:S(2)}) async-start(), calls=%async_computation.15 | async-start | bytes 2949120 | tf_op jit(solution)/shard_map/all_gather | solution.py:244
  195.2 21.2 %collective-permute-start.23 = (bf16[64,1536]{1,0:T(8,128)(2,1)S(1)}, bf16[64,1536]{1,0:T(8,128)(2,1)S(1)}, u32[]{:S(2)}, u32[]{:S(2)}) collective-permute-start(bf16[64,1536]{1,0:T(8,128)(2,1)S(1)} %bitcast.481), channel_id=1, source_target_pairs={{0,2},{1,3},{2,0},{3,1},{4,6},{5,7},{6,4},{7,5},{8,10},{9,11},{10,... | collective-permute-start | bytes 589832 | tf_op jit(solution)/shard_map/ppermute | solution.py:35
  196.6 22.1 %collective-permute-start.22 = (bf16[64,1536]{1,0:T(8,128)(2,1)S(1)}, bf16[64,1536]{1,0:T(8,128)(2,1)S(1)}, u32[]{:S(2)}, u32[]{:S(2)}) collective-permute-start(bf16[64,1536]{1,0:T(8,128)(2,1)S(1)} %bitcast.482), channel_id=1, source_target_pairs={{0,1},{1,0},{2,3},{3,2},{4,5},{5,4},{6,7},{7,6},{8,9},{9,8},{10,11... | collective-permute-start | bytes 589832 | tf_op jit(solution)/shard_map/ppermute | solution.py:35
  225.4 19.7 %collective-permute-start.25 = (bf16[256,1536]{1,0:T(8,128)(2,1)S(1)}, bf16[256,1536]{1,0:T(8,128)(2,1)}, u32[]{:S(2)}, u32[]{:S(2)}) collective-permute-start(bf16[256,1536]{1,0:T(8,128)(2,1)S(1)} %bitcast.427), channel_id=1, source_target_pairs={{0,2},{1,3},{2,0},{3,1},{4,6},{5,7},{6,4},{7,5},{8,10},{9,11},{10,... | collective-permute-start | bytes 2359304 | tf_op jit(solution)/shard_map/ppermute | solution.py:35
  289.7 20.1 %collective-permute-start.30 = (bf16[256,1536]{1,0:T(8,128)(2,1)}, bf16[256,1536]{1,0:T(8,128)(2,1)}, u32[]{:S(2)}, u32[]{:S(2)}) collective-permute-start(bf16[256,1536]{1,0:T(8,128)(2,1)} %get-tuple-element.208), channel_id=1, source_target_pairs={{0,1},{1,0},{2,3},{3,2},{4,5},{5,4},{6,7},{7,6},{8,9},{9,8},{10,11... | collective-permute-start | bytes 2359304 | tf_op jit(solution)/shard_map/ppermute | solution.py:35
  290.6 143.6 %reduce-scatter.6.cloned.1.call-start = ((), (), s32[]{:S(2)}) async-start(), calls=%async_computation.16 | async-start | bytes 2949120 | tf_op jit(solution)/shard_map/reduce_scatter | solution.py:250
  388.2 156.7 %reduce-scatter.8.cloned.1.call-start = ((), (), s32[]{:S(2)}) async-start(), calls=%async_computation.17 | async-start | bytes 5898240 | tf_op jit(solution)/shard_map/reduce_scatter | solution.py:250
  397.7 32.4 %collective-permute-start.45 = (bf16[256,1536]{1,0:T(8,128)(2,1)S(1)}, bf16[256,1536]{1,0:T(8,128)(2,1)}, u32[]{:S(2)}, u32[]{:S(2)}) collective-permute-start(bf16[256,1536]{1,0:T(8,128)(2,1)S(1)} %get-tuple-element.221), channel_id=1, source_target_pairs={{0,1},{1,0},{2,3},{3,2},{4,5},{5,4},{6,7},{7,6},{8,9},{9,8},{10,11... | collective-permute-start | bytes 2359304 | tf_op jit(solution)/shard_map/ppermute | solution.py:35
  409.6 19.7 %collective-permute-start.50 = (bf16[256,1536]{1,0:T(8,128)(2,1)}, bf16[256,1536]{1,0:T(8,128)(2,1)S(1)}, u32[]{:S(2)}, u32[]{:S(2)}) collective-permute-start(bf16[256,1536]{1,0:T(8,128)(2,1)} %pad_maximum_fusion.17), channel_id=1, source_target_pairs={{0,2},{1,3},{2,0},{3,1},{4,6},{5,7},{6,4},{7,5},{8,10},{9,11},{10,... | collective-permute-start | bytes 2359304 | tf_op jit(solution)/shard_map/ppermute | solution.py:35
  441.4 220.7 %reduce-scatter.10.cloned.1.call-start = ((), (), s32[]{:S(2)}) async-start(), calls=%async_computation.18 | async-start | bytes 4423680 | tf_op jit(solution)/shard_map/reduce_scatter | solution.py:250
  460.7 21.3 %collective-permute-start.60 = (bf16[256,1536]{1,0:T(8,128)(2,1)}, bf16[256,1536]{1,0:T(8,128)(2,1)S(1)}, u32[]{:S(2)}, u32[]{:S(2)}) collective-permute-start(bf16[256,1536]{1,0:T(8,128)(2,1)} %get-tuple-element.217), channel_id=1, source_target_pairs={{0,1},{1,0},{2,3},{3,2},{4,5},{5,4},{6,7},{7,6},{8,9},{9,8},{10,11... | collective-permute-start | bytes 2359304 | tf_op jit(solution)/shard_map/ppermute | solution.py:35
  461.2 20.7 %collective-permute-start.61 = (bf16[256,1536]{1,0:T(8,128)(2,1)S(1)}, bf16[256,1536]{1,0:T(8,128)(2,1)}, u32[]{:S(2)}, u32[]{:S(2)}) collective-permute-start(bf16[256,1536]{1,0:T(8,128)(2,1)S(1)} %get-tuple-element.216), channel_id=1, source_target_pairs={{0,1},{1,0},{2,3},{3,2},{4,5},{5,4},{6,7},{7,6},{8,9},{9,8},{10,11... | collective-permute-start | bytes 2359304 | tf_op jit(solution)/shard_map/ppermute | solution.py:35
  461.2 57.1 %collective-permute-start.59 = (bf16[256,1536]{1,0:T(8,128)(2,1)}, bf16[256,1536]{1,0:T(8,128)(2,1)}, u32[]{:S(2)}, u32[]{:S(2)}) collective-permute-start(bf16[256,1536]{1,0:T(8,128)(2,1)} %get-tuple-element.218), channel_id=1, source_target_pairs={{0,1},{1,0},{2,3},{3,2},{4,5},{5,4},{6,7},{7,6},{8,9},{9,8},{10,11... | collective-permute-start | bytes 2359304 | tf_op jit(solution)/shard_map/ppermute | solution.py:35
  461.7 56.6 %collective-permute-start.63 = (bf16[256,1536]{1,0:T(8,128)(2,1)}, bf16[256,1536]{1,0:T(8,128)(2,1)}, u32[]{:S(2)}, u32[]{:S(2)}) collective-permute-start(bf16[256,1536]{1,0:T(8,128)(2,1)} %get-tuple-element.215), channel_id=1, source_target_pairs={{0,1},{1,0},{2,3},{3,2},{4,5},{5,4},{6,7},{7,6},{8,9},{9,8},{10,11... | collective-permute-start | bytes 2359304 | tf_op jit(solution)/shard_map/ppermute | solution.py:35
  485.3 36.7 %collective-permute-start.62 = (bf16[2,256,1536]{2,1,0:T(8,128)(2,1)}, bf16[2,256,1536]{2,1,0:T(8,128)(2,1)}, u32[]{:S(2)}, u32[]{:S(2)}) collective-permute-start(bf16[2,256,1536]{2,1,0:T(8,128)(2,1)} %pad_maximum_fusion.12), channel_id=1, source_target_pairs={{0,4},{4,0},{8,12},{12,8},{16,20},{20,16},{24,28},{28,24},{1,5},{5... | collective-permute-start | bytes 4718600 | tf_op jit(solution)/shard_map/ppermute | solution.py:40
  486.8 23.3 %collective-permute-start.55 = (bf16[256,1536]{1,0:T(8,128)(2,1)}, bf16[256,1536]{1,0:T(8,128)(2,1)}, u32[]{:S(2)}, u32[]{:S(2)}) collective-permute-start(bf16[256,1536]{1,0:T(8,128)(2,1)} %get-tuple-element.230), channel_id=1, source_target_pairs={{0,1},{1,0},{2,3},{3,2},{4,5},{5,4},{6,7},{7,6},{8,9},{9,8},{10,11... | collective-permute-start | bytes 2359304 | tf_op jit(solution)/shard_map/ppermute | solution.py:35
  489.8 20.3 %collective-permute-start.57 = (bf16[256,1536]{1,0:T(8,128)(2,1)}, bf16[256,1536]{1,0:T(8,128)(2,1)}, u32[]{:S(2)}, u32[]{:S(2)}) collective-permute-start(bf16[256,1536]{1,0:T(8,128)(2,1)} %add_convert_fusion.2), channel_id=1, source_target_pairs={{0,2},{1,3},{2,0},{3,1},{4,6},{5,7},{6,4},{7,5},{8,10},{9,11},{10,... | collective-permute-start | bytes 2359304 | tf_op jit(solution)/shard_map/ppermute | solution.py:35
  536.9 84.6 %collective-permute-start.74 = (bf16[64,1536]{1,0:T(8,128)(2,1)}, bf16[64,1536]{1,0:T(8,128)(2,1)}, u32[]{:S(2)}, u32[]{:S(2)}) collective-permute-start(bf16[64,1536]{1,0:T(8,128)(2,1)} %get-tuple-element.255), channel_id=1, source_target_pairs={{0,1},{1,0},{2,3},{3,2},{4,5},{5,4},{6,7},{7,6},{8,9},{9,8},{10,11... | collective-permute-start | bytes 589832 | tf_op jit(solution)/shard_map/ppermute | solution.py:35
  537.4 122.9 %collective-permute-start.73 = (bf16[64,1536]{1,0:T(8,128)(2,1)S(1)}, bf16[64,1536]{1,0:T(8,128)(2,1)}, u32[]{:S(2)}, u32[]{:S(2)}) collective-permute-start(bf16[64,1536]{1,0:T(8,128)(2,1)S(1)} %get-tuple-element.254), channel_id=1, source_target_pairs={{0,1},{1,0},{2,3},{3,2},{4,5},{5,4},{6,7},{7,6},{8,9},{9,8},{10,11... | collective-permute-start | bytes 589832 | tf_op jit(solution)/shard_map/ppermute | solution.py:35
  539.9 122.3 %reduce-scatter.12.cloned.1.call-start = ((), (), s32[]{:S(2)}) async-start(), calls=%async_computation.19 | async-start | bytes 1966080 | tf_op jit(solution)/shard_map/reduce_scatter | solution.py:208
  539.9 122.2 %collective-permute-start.71 = (bf16[256,1536]{1,0:T(8,128)(2,1)}, bf16[256,1536]{1,0:T(8,128)(2,1)}, u32[]{:S(2)}, u32[]{:S(2)}) collective-permute-start(bf16[256,1536]{1,0:T(8,128)(2,1)} %get-tuple-element.182), channel_id=1, source_target_pairs={{0,2},{1,3},{2,0},{3,1},{4,6},{5,7},{6,4},{7,5},{8,10},{9,11},{10,... | collective-permute-start | bytes 2359304 | tf_op jit(solution)/shard_map/ppermute | solution.py:35
  547.7 29.3 %collective-permute-start.66 = (bf16[192,2304]{1,0:T(8,128)(2,1)}, bf16[192,2304]{1,0:T(8,128)(2,1)}, u32[]{:S(2)}, u32[]{:S(2)}) collective-permute-start(bf16[192,2304]{1,0:T(8,128)(2,1)} %dynamic-slice_bitcast_fusion.3), channel_id=1, source_target_pairs={{0,4},{4,0},{8,12},{12,8},{16,20},{20,16},{24,28},{28,24},{1,5},{5... | collective-permute-start | bytes 2654216 | tf_op jit(solution)/shard_map/ppermute | solution.py:40
  555.7 47.9 %collective-permute-start.67 = (bf16[4,64,3072]{2,1,0:T(8,128)(2,1)}, bf16[4,64,3072]{2,1,0:T(8,128)(2,1)}, u32[]{:S(2)}, u32[]{:S(2)}) collective-permute-start(bf16[4,64,3072]{2,1,0:T(8,128)(2,1)} %get-tuple-element.176), channel_id=1, source_target_pairs={{0,4},{4,0},{8,12},{12,8},{16,20},{20,16},{24,28},{28,24},{1,5},{5... | collective-permute-start | bytes 4718600 | tf_op jit(solution)/shard_map/ppermute | solution.py:40
  610.6 51.5 %collective-permute-start.70 = (bf16[4,192,1152]{2,1,0:T(8,128)(2,1)}, bf16[4,192,1152]{2,1,0:T(8,128)(2,1)}, u32[]{:S(2)}, u32[]{:S(2)}) collective-permute-start(bf16[4,192,1152]{2,1,0:T(8,128)(2,1)} %dynamic-slice_bitcast_fusion), channel_id=1, source_target_pairs={{0,4},{4,0},{8,12},{12,8},{16,20},{20,16},{24,28},{28,24},{1,5},{5... | collective-permute-start | bytes 5308424 | tf_op jit(solution)/shard_map/ppermute | solution.py:40
  612.5 49.6 %all-to-all-start.4 = ((bf16[4,48,4608]{2,1,0:T(8,128)(2,1)}), bf16[4,48,4608]{2,1,0:T(8,128)(2,1)}, u32[]{:S(2)}, u32[]{:S(2)}) async-start(bf16[4,48,4608]{2,1,0:T(8,128)(2,1)} %bitcast.144), calls=%async_computation.8 | async-start | bytes 3538944 | tf_op jit(solution)/shard_map/all_to_all | solution.py:295
  617.1 104.2 %reduce-scatter.14.cloned.1.call-start = ((), (), s32[]{:S(2)}) async-start(), calls=%async_computation.20 | async-start | bytes 2211840 | tf_op jit(solution)/shard_map/reduce_scatter | solution.py:208
  619.6 42.5 %collective-permute-start.69 = (bf16[256,1536]{1,0:T(8,128)(2,1)}, bf16[256,1536]{1,0:T(8,128)(2,1)S(1)}, u32[]{:S(2)}, u32[]{:S(2)}) collective-permute-start(bf16[256,1536]{1,0:T(8,128)(2,1)} %fusion.26), channel_id=1, source_target_pairs={{0,2},{1,3},{2,0},{3,1},{4,6},{5,7},{6,4},{7,5},{8,10},{9,11},{10,... | collective-permute-start | bytes 2359304 | tf_op jit(solution)/shard_map/ppermute | solution.py:35
  622.5 37.7 %collective-permute-start.75 = (bf16[64,1536]{1,0:T(8,128)(2,1)S(1)}, bf16[64,1536]{1,0:T(8,128)(2,1)S(1)}, u32[]{:S(2)}, u32[]{:S(2)}) collective-permute-start(bf16[64,1536]{1,0:T(8,128)(2,1)S(1)} %add_convert_fusion.6), channel_id=1, source_target_pairs={{0,2},{1,3},{2,0},{3,1},{4,6},{5,7},{6,4},{7,5},{8,10},{9,11},{10,... | collective-permute-start | bytes 589832 | tf_op jit(solution)/shard_map/ppermute | solution.py:35
  662.2 44.7 %collective-permute-start.82 = (bf16[64,3072]{1,0:T(8,128)(2,1)}, bf16[64,3072]{1,0:T(8,128)(2,1)}, u32[]{:S(2)}, u32[]{:S(2)}) collective-permute-start(bf16[64,3072]{1,0:T(8,128)(2,1)} %reduce-scatter.12.cloned.1.call-done), channel_id=1, source_target_pairs={{0,2},{1,3},{2,0},{3,1},{4,6},{5,7},{6,4},{7,5},{8,10},{9,11},{10,... | collective-permute-start | bytes 1179656 | tf_op jit(solution)/shard_map/ppermute | solution.py:35
  662.6 57.0 %collective-permute-start.81 = (bf16[64,3072]{1,0:T(8,128)(2,1)}, bf16[64,3072]{1,0:T(8,128)(2,1)}, u32[]{:S(2)}, u32[]{:S(2)}) collective-permute-start(bf16[64,3072]{1,0:T(8,128)(2,1)} %reduce-scatter.12.cloned.1.call-done), channel_id=1, source_target_pairs={{0,1},{1,0},{2,3},{3,2},{4,5},{5,4},{6,7},{7,6},{8,9},{9,8},{10,11... | collective-permute-start | bytes 1179656 | tf_op jit(solution)/shard_map/ppermute | solution.py:35
  668.5 32.8 %collective-permute-start.84 = (bf16[192,1152]{1,0:T(8,128)(2,1)}, bf16[192,1152]{1,0:T(8,128)(2,1)}, u32[]{:S(2)}, u32[]{:S(2)}) collective-permute-start(bf16[192,1152]{1,0:T(8,128)(2,1)} %dynamic-slice_bitcast_fusion.4), channel_id=1, source_target_pairs={{0,4},{4,0},{8,12},{12,8},{16,20},{20,16},{24,28},{28,24},{1,5},{5... | collective-permute-start | bytes 1327112 | tf_op jit(solution)/shard_map/ppermute | solution.py:40
  (156 other events, 1617.4 us)
Sparse Core Ops, SparseCore 0:
  21.0 30.9 all-gather.16
  54.1 30.6 all-gather.8
  86.9 62.5 all-gather.18
  151.0 28.8 all-gather.10
  195.3 89.4 all-gather.12
  290.7 46.7 all-gather.14
  388.3 45.8 reduce-scatter.5
  441.5 83.7 reduce-scatter.7
  540.0 65.4 reduce-scatter.9
  608.2 35.5 reduce-scatter.11
  666.7 39.6 reduce-scatter.13
